TPU v7x, 32 devices: a whole 2x2x4 slice. The times are simulated.
32 devices in a mesh: section: 2 (over y), dp: 16 (over z, x, core).
Axes of the slice: x: 2, y: 2, z: 4, core: 2. Of those that a mesh axis runs over, the one named last changes fastest.
Arguments:
- tokens: bfloat16 [2, 4096, 768], P(None, 'dp'), may hold values from -6 to 6
- lengths: int32 [2, 16], replicated, may hold values from 200 to 256
- w_qkv: float32 [2, 768, 2304], P('section', 'dp'), may hold values from -0.21875 to 0.21875
- w_out: float32 [2, 768, 768], P('section', 'dp'), may hold values from -0.625 to 0.625
- w_gate_up: float32 [2, 768, 6144], P('section', 'dp'), may hold values from -0.21875 to 0.21875
- w_down: float32 [2, 3072, 768], P('section', 'dp'), may hold values from -0.109375 to 0.109375
- norm_gain: float32 [2, 2, 768], P('section', None, 'dp'), may hold values from 0.25 to 1.75
- norm_bias: float32 [2, 2, 768], P('section', None, 'dp'), may hold values from -3 to 3
- cotangent: bfloat16 [2, 4096, 768], P(None, 'dp'), may hold values from -6 to 6
Outputs:
- layer_outputs: bfloat16 [2, 2, 4096, 768], P('section', None, 'dp')
- input_grads: float32 [2, 2, 4096, 768], P('section', None, 'dp')
- grad_w_qkv: float32 [2, 768, 2304], P('section', 'dp')
- grad_w_out: float32 [2, 768, 768], P('section', 'dp')
- grad_w_gate_up: float32 [2, 768, 6144], P('section', 'dp')
- grad_w_down: float32 [2, 3072, 768], P('section', 'dp')
- grad_norm_gain: float32 [2, 2, 768], P('section', None, 'dp')
- grad_norm_bias: float32 [2, 2, 768], P('section', None, 'dp')
Inputs may be any that keep to these rules, and one draw needn't show every extreme that they name: `lengths`: positions of a window from its length on are padding.
All inputs are finite; a program needn't handle non-finite values.
Results may differ from a plain program's by a relative error of at most 0.024.
The roundings to bfloat16 on the way count: a program that leaves them out, or rounds other values in their place, can miss the bound.
Values may be sent and summed in bfloat16 or wider, within the bound.
No kernel may reach another device: no remote copies, remote signals or barrier semaphores. Data moves between devices by JAX's collectives and lax.ppermute only.
A program may use at most 256 MiB of HBM per device.

v0:
```python
import jax
import jax.numpy as jnp
from jax import lax
from jax.sharding import PartitionSpec as P

D = 768
HEADS = 12
HEAD = 64
FF = 3072


EPSILON = 1e-05
NEGATIVE = -1e30


def shifted(shard, axis, by):
    devices = lax.axis_size(axis)
    pairs = [(i, i + by) for i in range(devices) if 0 <= i + by < devices]
    return lax.ppermute(shard, axis, pairs)


def norm_forward(row_values, gain_row, bias_row):
    center = row_values - jnp.mean(row_values, axis=-1, keepdims=True)
    scale_inv = lax.rsqrt(jnp.mean(center * center, axis=-1, keepdims=True) + EPSILON)
    normed = center * scale_inv
    return (normed * gain_row + bias_row, normed, scale_inv)


def norm_backward(upstream, normed, scale_inv, gain_row):
    scaled = upstream * gain_row
    inner_sum = (
        scaled
        - jnp.mean(scaled, axis=-1, keepdims=True)
        - normed * jnp.mean(scaled * normed, axis=-1, keepdims=True)
    )
    return (scale_inv * inner_sum, jnp.sum(upstream * normed, axis=0), jnp.sum(upstream, axis=0))


def score_block(queries, keys_all, length):
    seq_rows = queries.shape[0]
    slopes = jnp.exp2(-8.0 * (jnp.arange(HEADS).astype(jnp.float32) + 1.0) / HEADS)
    raw_scores = jnp.einsum(
        "qhd,khd->hqk", queries, keys_all, preferred_element_type=jnp.float32
    ) * HEAD ** (-0.5)
    places = jnp.arange(seq_rows, dtype=jnp.int32)
    distance = jnp.abs(places[:, None] - places[None, :]).astype(jnp.float32)
    raw_scores = raw_scores - slopes[:, None, None] * distance[None]
    key_valid = places < length
    return jnp.where(key_valid[None, None, :], raw_scores, NEGATIVE)


def layer_forward(inputs, length, weights):
    qkv_matrix, out_matrix, gate_matrix, down_matrix, gain_rows, bias_rows = weights
    seq_rows = inputs.shape[0]
    projected = jnp.dot(inputs, qkv_matrix, preferred_element_type=jnp.float32).astype(jnp.bfloat16)
    queries = projected[:, :D]
    key_values = projected[:, D:]
    scores = score_block(
        queries.reshape(seq_rows, HEADS, HEAD),
        key_values[:, :D].reshape(seq_rows, HEADS, HEAD),
        length,
    )
    row_peak = jnp.max(scores, axis=-1, keepdims=True)
    row_exp = jnp.exp(scores - row_peak)
    totals = jnp.sum(row_exp, axis=-1, keepdims=True)
    attn_probs = row_exp / totals
    log_sum = row_peak + jnp.log(totals)
    context = jnp.einsum(
        "hqk,khd->qhd",
        attn_probs.astype(jnp.bfloat16),
        key_values[:, D:].reshape(seq_rows, HEADS, HEAD),
        preferred_element_type=jnp.float32,
    )
    context = context.reshape(seq_rows, D).astype(jnp.bfloat16)
    attended = jnp.dot(context, out_matrix, preferred_element_type=jnp.float32)
    gain_float = gain_rows.astype(jnp.float32)
    bias_float = bias_rows.astype(jnp.float32)
    first_norm, normed_one, inv_one = norm_forward(
        inputs.astype(jnp.float32) + attended, gain_float[0], bias_float[0]
    )
    first_low = first_norm.astype(jnp.bfloat16)
    gate_up = jnp.dot(first_low, gate_matrix, preferred_element_type=jnp.float32)
    gated_rows = (jax.nn.gelu(gate_up[:, :FF], approximate=False) * gate_up[:, FF:]).astype(
        jnp.bfloat16
    )
    down_rows = jnp.dot(gated_rows, down_matrix, preferred_element_type=jnp.float32)
    layer_out, normed_two, inv_two = norm_forward(
        first_norm + down_rows, gain_float[1], bias_float[1]
    )
    stored = (
        inputs,
        queries,
        key_values,
        log_sum,
        context,
        normed_one,
        inv_one,
        first_low,
        gate_up,
        normed_two,
        inv_two,
    )
    return (layer_out, stored)


def layer_backward(upstream, stored, length, weights):
    qkv_matrix, out_matrix, gate_matrix, down_matrix, gain_rows, bias_rows = weights
    (
        inputs,
        queries,
        key_values,
        log_sum,
        context,
        normed_one,
        inv_one,
        first_low,
        gate_up,
        normed_two,
        inv_two,
    ) = stored
    seq_rows = inputs.shape[0]
    gain_float = gain_rows.astype(jnp.float32)
    grad_two, gain_two, bias_two = norm_backward(upstream, normed_two, inv_two, gain_float[1])
    down_grad = grad_two.astype(jnp.bfloat16)
    gate_vals = gate_up[:, :FF]
    up_vals = gate_up[:, FF:]
    gelu_vals = jax.nn.gelu(gate_vals, approximate=False)
    gated_rows = (gelu_vals * up_vals).astype(jnp.bfloat16)
    grad_down_w = jnp.einsum("tf,td->fd", gated_rows, down_grad, preferred_element_type=jnp.float32)
    grad_gated = jnp.einsum("td,fd->tf", down_grad, down_matrix, preferred_element_type=jnp.float32)
    gauss_cdf = 0.5 * (1.0 + lax.erf(gate_vals * 2.0 ** (-0.5)))
    density = jnp.exp(-0.5 * gate_vals * gate_vals) * (2.0 * jnp.pi) ** (-0.5)
    grad_gate = grad_gated * up_vals * (gauss_cdf + gate_vals * density)
    grad_up = grad_gated * gelu_vals
    gate_up_grad = jnp.concatenate([grad_gate, grad_up], axis=1).astype(jnp.bfloat16)
    grad_gu_w = jnp.einsum("td,tf->df", first_low, gate_up_grad, preferred_element_type=jnp.float32)
    grad_first = grad_two + jnp.einsum(
        "tf,df->td", gate_up_grad, gate_matrix, preferred_element_type=jnp.float32
    )
    grad_one, gain_one, bias_one = norm_backward(grad_first, normed_one, inv_one, gain_float[0])
    attn_grad = grad_one.astype(jnp.bfloat16)
    grad_out_w = jnp.einsum("td,te->de", context, attn_grad, preferred_element_type=jnp.float32)
    context_grad = jnp.einsum(
        "te,de->td", attn_grad, out_matrix, preferred_element_type=jnp.float32
    )
    context_grad = context_grad.astype(jnp.bfloat16).reshape(seq_rows, HEADS, HEAD)
    query_heads = queries.reshape(seq_rows, HEADS, HEAD)
    keys_all = key_values[:, :D].reshape(seq_rows, HEADS, HEAD)
    values_all = key_values[:, D:].reshape(seq_rows, HEADS, HEAD)
    scores = score_block(query_heads, keys_all, length)
    attn_probs = jnp.exp(scores - log_sum)
    prob_grad = jnp.einsum(
        "qhd,khd->hqk", context_grad, values_all, preferred_element_type=jnp.float32
    )
    inner_sum = jnp.sum(attn_probs * prob_grad, axis=-1, keepdims=True)
    score_grad = (attn_probs * (prob_grad - inner_sum)).astype(jnp.bfloat16)
    query_grad = jnp.einsum(
        "hqk,khd->qhd", score_grad, keys_all, preferred_element_type=jnp.float32
    ) * HEAD ** (-0.5)
    key_grad = jnp.einsum(
        "hqk,qhd->khd", score_grad, query_heads, preferred_element_type=jnp.float32
    ) * HEAD ** (-0.5)
    value_grad = jnp.einsum(
        "hqk,qhd->khd",
        attn_probs.astype(jnp.bfloat16),
        context_grad,
        preferred_element_type=jnp.float32,
    )
    qkv_grad = jnp.concatenate(
        [
            query_grad.reshape(seq_rows, D),
            key_grad.reshape(seq_rows, D),
            value_grad.reshape(seq_rows, D),
        ],
        axis=1,
    ).astype(jnp.bfloat16)
    grad_qkv_w = jnp.einsum("td,te->de", inputs, qkv_grad, preferred_element_type=jnp.float32)
    input_grad = grad_one + jnp.einsum(
        "te,de->td", qkv_grad, qkv_matrix, preferred_element_type=jnp.float32
    )
    grad_terms = (
        grad_qkv_w,
        grad_out_w,
        grad_gu_w,
        grad_down_w,
        jnp.stack([gain_one, gain_two]),
        jnp.stack([bias_one, bias_two]),
    )
    return (input_grad, grad_terms)


def store_slot(slot_index, active, buffer, new_value):
    previous = lax.dynamic_index_in_dim(buffer, slot_index, 0, keepdims=False)
    return lax.dynamic_update_index_in_dim(
        buffer, jnp.where(active, new_value, previous), slot_index, 0
    )


def shards(tokens, lengths, w_qkv, w_out, w_gate_up, w_down, norm_gain, norm_bias, cotangent):
    section_index = lax.axis_index("section")
    window = lax.axis_index("dp")
    micro_count = tokens.shape[0]
    seq_rows = tokens.shape[1]
    forward_weights = (
        lax.all_gather(w_qkv[0].astype(jnp.bfloat16), "dp", axis=0, tiled=True),
        lax.all_gather(w_out[0].astype(jnp.bfloat16), "dp", axis=0, tiled=True),
        lax.all_gather(w_gate_up[0].astype(jnp.bfloat16), "dp", axis=0, tiled=True),
        lax.all_gather(w_down[0].astype(jnp.bfloat16), "dp", axis=0, tiled=True),
        lax.all_gather(norm_gain[0].astype(jnp.bfloat16), "dp", axis=1, tiled=True),
        lax.all_gather(norm_bias[0].astype(jnp.bfloat16), "dp", axis=1, tiled=True),
    )

    def length_of(slot_index):
        length_row = lax.dynamic_index_in_dim(lengths, slot_index, 0, keepdims=False)
        return lax.dynamic_index_in_dim(length_row, window, 0, keepdims=False)

    def slot_zeros(shape, dtype):
        return jnp.zeros((micro_count,) + shape, dtype)

    stash_init = (
        slot_zeros((seq_rows, D), jnp.bfloat16),
        slot_zeros((seq_rows, D), jnp.bfloat16),
        slot_zeros((seq_rows, 2 * D), jnp.bfloat16),
        slot_zeros((HEADS, seq_rows, 1), jnp.float32),
        slot_zeros((seq_rows, D), jnp.bfloat16),
        slot_zeros((seq_rows, D), jnp.float32),
        slot_zeros((seq_rows, 1), jnp.float32),
        slot_zeros((seq_rows, D), jnp.bfloat16),
        slot_zeros((seq_rows, 2 * FF), jnp.float32),
        slot_zeros((seq_rows, D), jnp.float32),
        slot_zeros((seq_rows, 1), jnp.float32),
        slot_zeros((seq_rows, D), jnp.bfloat16),
    )

    def forward_tick(carry, tick_now):
        arrived, stash = carry
        offset = tick_now - section_index
        slot_index = jnp.clip(offset, 0, micro_count - 1)
        active = (offset >= 0) & (offset < micro_count)
        own_input = lax.dynamic_index_in_dim(tokens, slot_index, 0, keepdims=False)
        layer_input = jnp.where(section_index == 0, own_input, arrived)
        layer_out, stored = layer_forward(layer_input, length_of(slot_index), forward_weights)
        sent_rows = layer_out.astype(jnp.bfloat16)
        passed = shifted(sent_rows, "section", 1)
        stash = tuple(
            (
                store_slot(slot_index, active, buffer, new_value)
                for buffer, new_value in zip(stash, stored + (sent_rows,))
            )
        )
        return ((passed, stash), None)

    tick_list = jnp.arange(micro_count + 1, dtype=jnp.int32)
    start_rows = jnp.zeros((seq_rows, D), jnp.bfloat16)
    (unused, stash), unused_out = lax.scan(forward_tick, (start_rows, stash_init), tick_list)
    backward_weights = (
        lax.all_gather(w_qkv[0].astype(jnp.bfloat16), "dp", axis=0, tiled=True),
        lax.all_gather(w_out[0].astype(jnp.bfloat16), "dp", axis=0, tiled=True),
        lax.all_gather(w_gate_up[0].astype(jnp.bfloat16), "dp", axis=0, tiled=True),
        lax.all_gather(w_down[0].astype(jnp.bfloat16), "dp", axis=0, tiled=True),
        lax.all_gather(norm_gain[0].astype(jnp.bfloat16), "dp", axis=1, tiled=True),
        lax.all_gather(norm_bias[0].astype(jnp.bfloat16), "dp", axis=1, tiled=True),
    )

    def backward_tick(carry, tick_now):
        arrived, summed, grads_in = carry
        offset = tick_now - 1 + section_index
        slot_index = jnp.clip(offset, 0, micro_count - 1)
        active = (offset >= 0) & (offset < micro_count)
        cot_rows = lax.dynamic_index_in_dim(cotangent, slot_index, 0, keepdims=False).astype(
            jnp.float32
        )
        upstream = jnp.where(section_index == 1, cot_rows, arrived.astype(jnp.float32))
        stored = tuple(
            (
                lax.dynamic_index_in_dim(buffer, slot_index, 0, keepdims=False)
                for buffer in stash[:-1]
            )
        )
        input_grad, grad_terms = layer_backward(
            upstream, stored, length_of(slot_index), backward_weights
        )
        weight_flag = active.astype(jnp.float32)
        masked = tuple((term * weight_flag for term in grad_terms))
        summed = tuple((left + right for left, right in zip(summed, masked)))
        passed = shifted(input_grad.astype(jnp.bfloat16), "section", -1)
        grads_in = store_slot(slot_index, active, grads_in, input_grad)
        return ((passed, summed, grads_in), None)

    summed_init = (
        jnp.zeros((D, 3 * D), jnp.float32),
        jnp.zeros((D, D), jnp.float32),
        jnp.zeros((D, 2 * FF), jnp.float32),
        jnp.zeros((FF, D), jnp.float32),
        jnp.zeros((2, D), jnp.float32),
        jnp.zeros((2, D), jnp.float32),
    )
    grads_init = jnp.zeros((micro_count, seq_rows, D), jnp.float32)
    (unused_back, summed, grads_in), unused_list = lax.scan(
        backward_tick, (start_rows, summed_init, grads_init), tick_list
    )
    attn_share = (
        lax.psum_scatter(summed[0], "dp", scatter_dimension=0, tiled=True),
        lax.psum_scatter(summed[1], "dp", scatter_dimension=0, tiled=True),
        lax.psum_scatter(summed[4], "dp", scatter_dimension=1, tiled=True),
        lax.psum_scatter(summed[5], "dp", scatter_dimension=1, tiled=True),
    )
    gate_share = lax.psum_scatter(summed[2], "dp", scatter_dimension=0, tiled=True)
    down_share = lax.psum_scatter(summed[3], "dp", scatter_dimension=0, tiled=True)
    shares = (attn_share[0], attn_share[1], gate_share, down_share, attn_share[2], attn_share[3])
    return (
        stash[-1][None],
        grads_in[None],
        shares[0][None],
        shares[1][None],
        shares[2][None],
        shares[3][None],
        shares[4][None],
        shares[5][None],
    )


def solution(mesh):
    return jax.shard_map(
        shards,
        mesh=mesh,
        in_specs=(
            P(None, "dp", None),
            P(),
            P("section", "dp", None),
            P("section", "dp", None),
            P("section", "dp", None),
            P("section", "dp", None),
            P("section", None, "dp"),
            P("section", None, "dp"),
            P(None, "dp", None),
        ),
        out_specs=(
            P("section", None, "dp", None),
            P("section", None, "dp", None),
            P("section", "dp", None),
            P("section", "dp", None),
            P("section", "dp", None),
            P("section", "dp", None),
            P("section", None, "dp"),
            P("section", None, "dp"),
        ),
        check_vma=False,
    )
```

profile of v0, /device:TPU:0, one launch (start us, length us, event | category | flops | bytes accessed | tf_op | source)
XLA Modules:
  0.0 1286.7 jit_solution(15711562108209963430)
XLA Ops:
  13.9 24.4 %all-gather.2 = bf16[1,2,768]{1,0,2:T(2,128)(2,1)S(1)} all-gather(bf16[1,2,48]{1,0,2:T(2,128)(2,1)S(1)} %copy.83), channel_id=4, replica_groups=mesh['section'=2,'dp'=16] {'dp'}, dimensions={2}, use_global_device_ids=true | all-gather | bytes 3264 | tf_op jit(solution)/shard_map/all_gather | solution.py:209
  39.1 18.7 %all-gather.3 = bf16[1,2,768]{1,0,2:T(2,128)(2,1)S(1)} all-gather(bf16[1,2,48]{1,0,2:T(2,128)(2,1)S(1)} %copy.85), channel_id=5, replica_groups=mesh['section'=2,'dp'=16] {'dp'}, dimensions={2}, use_global_device_ids=true | all-gather | bytes 3264 | tf_op jit(solution)/shard_map/all_gather | solution.py:210
  58.7 42.9 %all-gather.11.cloned.1.call-done = bf16[1,768,2304]{2,1,0:T(8,128)(2,1)} async-done(((bf16[1,48,2304]{2,1,0:T(8,128)(2,1)}), bf16[1,768,2304]{2,1,0:T(8,128)(2,1)}) %all-gather.11.cloned.1.call-update) | async-done | bytes 3538960 | tf_op jit(solution)/shard_map/all_gather | solution.py:205
  101.6 55.1 %all-gather.17.cloned.1.call-done = bf16[1,3072,768]{2,1,0:T(8,128)(2,1)} async-done(((bf16[1,192,768]{2,1,0:T(8,128)(2,1)}), bf16[1,3072,768]{2,1,0:T(8,128)(2,1)}) %all-gather.17.cloned.1.call-update) | async-done | bytes 4718608 | tf_op jit(solution)/shard_map/all_gather | solution.py:208
  156.7 82.7 %all-gather.15.cloned.1.call-done = bf16[1,768,6144]{2,1,0:T(8,128)(2,1)} async-done(((bf16[1,48,6144]{2,1,0:T(8,128)(2,1)}), bf16[1,768,6144]{2,1,0:T(8,128)(2,1)}) %all-gather.15.cloned.1.call-update) | async-done | bytes 9437200 | tf_op jit(solution)/shard_map/all_gather | solution.py:207
  251.1 6.1 broadcast_in_dim.183
  257.3 182.2 %while.65 = (s32[]{:T(128)}, bf16[256,768]{1,0:T(8,128)(2,1)}, bf16[2,256,768]{2,1,0:T(8,128)(2,1)}, bf16[2,256,768]{2,1,0:T(8,128)(2,1)}, bf16[2,256,1536]{2,1,...) while((s32[]{:T(128)}, bf16[256,768]{1,0:T(8,128)(2,1)}, ...), condition=%wide.region_7.8_spmd, body=%wide.region_0.7_spmd.sunk | while | flops 5104144384 | bytes 246386960 | solution.py:255
  268.4 3.1 convolution_convert_fusion.4
  279.3 9.0 bitcast_dynamic-update-slice_fusion.15
  288.3 15.4 %fusion.202 = (f32[256]{0:T(256)S(1)}, f32[256,768]{1,0:T(8,128)S(1)}) fusion(bf16[3072,768]{1,0:T(8,128)(2,1)} %get-tuple-element.1968, f32[256,6144]{1,0:T(8,128)} %get-tuple-element.1817, f32[768]{0:T(1024)S(1)} %get-tuple-element.1814, f32[768]{0:T(1024)S(1)} %get-tuple-element.1815, f32[256]{0:T(256)S(1)} %add_rsqrt_fusion.4, ...), kind=kOutput, calls=%fused_computation.222.clone.1 | convolution fusion | flops 1261043456 | bytes 12592128 | tf_op jit(solution)/shard_map/while/body/eval_jaxpr/dot_general | solution.py:86
  305.1 4.4 collective-permute-start
  314.6 2.6 bitcast_dynamic-update-slice_fusion.18
  328.9 3.1 convolution_convert_fusion.4
  339.9 9.0 bitcast_dynamic-update-slice_fusion.15
  348.9 15.3 %fusion.202 = (f32[256]{0:T(256)S(1)}, f32[256,768]{1,0:T(8,128)S(1)}) fusion(bf16[3072,768]{1,0:T(8,128)(2,1)} %get-tuple-element.1968, f32[256,6144]{1,0:T(8,128)} %get-tuple-element.1817, f32[768]{0:T(1024)S(1)} %get-tuple-element.1814, f32[768]{0:T(1024)S(1)} %get-tuple-element.1815, f32[256]{0:T(256)S(1)} %add_rsqrt_fusion.4, ...), kind=kOutput, calls=%fused_computation.222.clone.1 | convolution fusion | flops 1261043456 | bytes 12592128 | tf_op jit(solution)/shard_map/while/body/eval_jaxpr/dot_general | solution.py:86
  365.7 5.4 collective-permute-start
  376.2 2.6 bitcast_dynamic-update-slice_fusion.18
  389.8 3.1 convolution_convert_fusion.4
  400.7 9.0 bitcast_dynamic-update-slice_fusion.15
  409.8 15.4 %fusion.202 = (f32[256]{0:T(256)S(1)}, f32[256,768]{1,0:T(8,128)S(1)}) fusion(bf16[3072,768]{1,0:T(8,128)(2,1)} %get-tuple-element.1968, f32[256,6144]{1,0:T(8,128)} %get-tuple-element.1817, f32[768]{0:T(1024)S(1)} %get-tuple-element.1814, f32[768]{0:T(1024)S(1)} %get-tuple-element.1815, f32[256]{0:T(256)S(1)} %add_rsqrt_fusion.4, ...), kind=kOutput, calls=%fused_computation.222.clone.1 | convolution fusion | flops 1261043456 | bytes 12592128 | tf_op jit(solution)/shard_map/while/body/eval_jaxpr/dot_general | solution.py:86
  426.6 5.2 collective-permute-start
  442.0 244.6 %while.66 = (s32[]{:T(128)}, bf16[256,768]{1,0:T(8,128)(2,1)}, f32[768,2304]{1,0:T(8,128)}, f32[768,768]{1,0:T(8,128)}, f32[768,6144]{1,0:T(8,128)}, /*index=5*/...) while((s32[]{:T(128)}, bf16[256,768]{1,0:T(8,128)(2,1)}, ...), condition=%wide.region_18.19_spmd.clone, body=%wide.region_8.18_spmd.clone.sunk | while | flops 10294599680 | bytes 342882656 | solution.py:299
  459.2 4.1 dynamic-slice_bitcast_fusion.4
  465.1 10.6 multiply_convert_fusion.8
  475.8 3.4 fusion.227
  493.2 7.3 select_add_fusion.11
  500.4 5.1 select_add_fusion.8
  505.6 8.4 select_add_fusion.10
  533.1 4.1 dynamic-slice_bitcast_fusion.4
  539.1 10.6 multiply_convert_fusion.8
  549.8 3.4 fusion.227
  568.3 10.0 select_add_fusion.11
  578.3 7.2 select_add_fusion.8
  585.6 12.1 select_add_fusion.10
  597.7 3.5 select_add_fusion.9
  618.5 4.1 dynamic-slice_bitcast_fusion.4
  624.4 10.6 multiply_convert_fusion.8
  635.1 3.4 fusion.227
  653.6 10.0 select_add_fusion.11
  663.6 7.2 select_add_fusion.8
  670.9 12.1 select_add_fusion.10
  683.1 3.5 select_add_fusion.9
  692.8 52.8 %reduce-scatter.21.cloned.1.call-done = f32[48,2]{1,0:T(8,128)} async-done(((f32[768,2]{1,0:T(8,128)}), f32[48,2]{1,0:T(8,128)}) %reduce-scatter.21.cloned.1.call-update) | async-done | bytes 400
  747.0 57.0 %reduce-scatter.19.cloned.1.call-done = f32[48,2]{1,0:T(8,128)} async-done(((f32[768,2]{1,0:T(8,128)}), f32[48,2]{1,0:T(8,128)}) %reduce-scatter.19.cloned.1.call-update) | async-done | bytes 400
  805.4 65.0 %reduce-scatter.13.cloned.1.call-done = f32[48,768]{1,0:T(8,128)} async-done(((f32[768,768]{1,0:T(8,128)}), f32[48,768]{1,0:T(8,128)}) %reduce-scatter.13.cloned.1.call-update) | async-done | bytes 147472 | tf_op jit(solution)/shard_map/reduce_scatter | solution.py:304
  870.4 94.1 %reduce-scatter.11.cloned.1.call-done = f32[48,2304]{1,0:T(8,128)} async-done(((f32[768,2304]{1,0:T(8,128)}), f32[48,2304]{1,0:T(8,128)}) %reduce-scatter.11.cloned.1.call-update) | async-done | bytes 442384 | tf_op jit(solution)/shard_map/reduce_scatter | solution.py:303
  964.5 115.6 %reduce-scatter.17.cloned.1.call-done = f32[192,768]{1,0:T(8,128)} async-done(((f32[3072,768]{1,0:T(8,128)}), f32[192,768]{1,0:T(8,128)}) %reduce-scatter.17.cloned.1.call-update) | async-done | bytes 589840 | tf_op jit(solution)/shard_map/reduce_scatter | solution.py:309
  1080.2 199.7 %reduce-scatter.15.cloned.1.call-done = f32[48,6144]{1,0:T(8,128)} async-done(((f32[768,6144]{1,0:T(8,128)}), f32[48,6144]{1,0:T(8,128)}) %reduce-scatter.15.cloned.1.call-update) | async-done | bytes 1179664 | tf_op jit(solution)/shard_map/reduce_scatter | solution.py:308
  (694 shorter events, 208.0 us)
Async XLA Ops:
  7.2 51.5 %all-gather.13.cloned.1.call-start = ((), (), s32[]{:S(2)}) async-start(), calls=%async_computation.11 | async-start | bytes 1253376 | tf_op jit(solution)/shard_map/all_gather | solution.py:206
  8.9 92.7 %all-gather.11.cloned.1.call-start = ((), (), s32[]{:S(2)}) async-start(), calls=%async_computation.10 | async-start | bytes 3760128 | tf_op jit(solution)/shard_map/all_gather | solution.py:205
  10.7 146.0 %all-gather.17.cloned.1.call-start = ((), (), s32[]{:S(2)}) async-start(), calls=%async_computation.13 | async-start | bytes 5013504 | tf_op jit(solution)/shard_map/all_gather | solution.py:208
  12.6 226.8 %all-gather.15.cloned.1.call-start = ((), (), s32[]{:S(2)}) async-start(), calls=%async_computation.12 | async-start | bytes 10027008 | tf_op jit(solution)/shard_map/all_gather | solution.py:207
  13.5 732.1 %reduce-scatter.21.cloned.1.call-start = ((), (), s32[]{:S(2)}) async-start(), calls=%async_computation.15 | async-start | bytes 417792
  288.3 15.4 %copy-start = (f32[2,256,6144]{2,1,0:T(8,128)}, f32[2,256,6144]{2,1,0:T(8,128)S(1)}, u32[]{:S(2)}) copy-start(f32[2,256,6144]{2,1,0:T(8,128)S(1)} %get-tuple-element.1953) | copy-start | bytes 37748740 | tf_op jit(solution)/shard_map/while
  288.3 15.7 %copy-start.38 = (f32[768]{0:T(1024)S(1)}, f32[768]{0:T(1024)}, u32[]{:S(2)}) copy-start(f32[768]{0:T(1024)} %get-tuple-element.1805) | copy-start | bytes 9220 | tf_op jit(solution)/shard_map/while
  288.3 15.7 %copy-start.39 = (f32[768]{0:T(1024)S(1)}, f32[768]{0:T(1024)}, u32[]{:S(2)}) copy-start(f32[768]{0:T(1024)} %get-tuple-element.1806) | copy-start | bytes 9220 | tf_op jit(solution)/shard_map/while
  288.3 21.2 %copy-start.26 = (bf16[2,256,768]{2,1,0:T(8,128)(2,1)S(1)}, bf16[2,256,768]{2,1,0:T(8,128)(2,1)}, u32[]{:S(2)}) copy-start(bf16[2,256,768]{2,1,0:T(8,128)(2,1)} %get-tuple-element.1917) | copy-start | bytes 2359300 | tf_op jit(solution)/shard_map/while
  288.3 21.3 %copy-start.20 = (bf16[2,256,768]{2,1,0:T(8,128)(2,1)S(1)}, bf16[2,256,768]{2,1,0:T(8,128)(2,1)}, u32[]{:S(2)}) copy-start(bf16[2,256,768]{2,1,0:T(8,128)(2,1)} %get-tuple-element.1923) | copy-start | bytes 2359300 | tf_op jit(solution)/shard_map/while
  305.1 12.7 collective-permute-start
  348.9 15.4 %copy-start = (f32[2,256,6144]{2,1,0:T(8,128)}, f32[2,256,6144]{2,1,0:T(8,128)S(1)}, u32[]{:S(2)}) copy-start(f32[2,256,6144]{2,1,0:T(8,128)S(1)} %get-tuple-element.1953) | copy-start | bytes 37748740 | tf_op jit(solution)/shard_map/while
  348.9 15.7 %copy-start.38 = (f32[768]{0:T(1024)S(1)}, f32[768]{0:T(1024)}, u32[]{:S(2)}) copy-start(f32[768]{0:T(1024)} %get-tuple-element.1805) | copy-start | bytes 9220 | tf_op jit(solution)/shard_map/while
  348.9 15.7 %copy-start.39 = (f32[768]{0:T(1024)S(1)}, f32[768]{0:T(1024)}, u32[]{:S(2)}) copy-start(f32[768]{0:T(1024)} %get-tuple-element.1806) | copy-start | bytes 9220 | tf_op jit(solution)/shard_map/while
  348.9 22.2 %copy-start.26 = (bf16[2,256,768]{2,1,0:T(8,128)(2,1)S(1)}, bf16[2,256,768]{2,1,0:T(8,128)(2,1)}, u32[]{:S(2)}) copy-start(bf16[2,256,768]{2,1,0:T(8,128)(2,1)} %get-tuple-element.1917) | copy-start | bytes 2359300 | tf_op jit(solution)/shard_map/while
  348.9 22.2 %copy-start.20 = (bf16[2,256,768]{2,1,0:T(8,128)(2,1)S(1)}, bf16[2,256,768]{2,1,0:T(8,128)(2,1)}, u32[]{:S(2)}) copy-start(bf16[2,256,768]{2,1,0:T(8,128)(2,1)} %get-tuple-element.1923) | copy-start | bytes 2359300 | tf_op jit(solution)/shard_map/while
  365.7 13.0 %collective-permute-start = (bf16[256,768]{1,0:T(8,128)(2,1)}, bf16[256,768]{1,0:T(8,128)(2,1)}, u32[]{:S(2)}, u32[]{:S(2)}) collective-permute-start(bf16[256,768]{1,0:T(8,128)(2,1)} %get-tuple-element.1820), channel_id=1, source_target_pairs={{0,16},{1,17},{2,18},{3,19},{4,20},{5,21},{6,22},{7,23},{8,24},{9,... | collective-permute-start | bytes 1179656 | tf_op jit(solution)/shard_map/while/body/eval_jaxpr/ppermute | solution.py:19
  409.7 15.4 %copy-start = (f32[2,256,6144]{2,1,0:T(8,128)}, f32[2,256,6144]{2,1,0:T(8,128)S(1)}, u32[]{:S(2)}) copy-start(f32[2,256,6144]{2,1,0:T(8,128)S(1)} %get-tuple-element.1953) | copy-start | bytes 37748740 | tf_op jit(solution)/shard_map/while
  409.7 15.7 %copy-start.38 = (f32[768]{0:T(1024)S(1)}, f32[768]{0:T(1024)}, u32[]{:S(2)}) copy-start(f32[768]{0:T(1024)} %get-tuple-element.1805) | copy-start | bytes 9220 | tf_op jit(solution)/shard_map/while
  409.7 15.7 %copy-start.39 = (f32[768]{0:T(1024)S(1)}, f32[768]{0:T(1024)}, u32[]{:S(2)}) copy-start(f32[768]{0:T(1024)} %get-tuple-element.1806) | copy-start | bytes 9220 | tf_op jit(solution)/shard_map/while
  409.8 22.1 %copy-start.26 = (bf16[2,256,768]{2,1,0:T(8,128)(2,1)S(1)}, bf16[2,256,768]{2,1,0:T(8,128)(2,1)}, u32[]{:S(2)}) copy-start(bf16[2,256,768]{2,1,0:T(8,128)(2,1)} %get-tuple-element.1917) | copy-start | bytes 2359300 | tf_op jit(solution)/shard_map/while
  409.8 22.1 %copy-start.20 = (bf16[2,256,768]{2,1,0:T(8,128)(2,1)S(1)}, bf16[2,256,768]{2,1,0:T(8,128)(2,1)}, u32[]{:S(2)}) copy-start(bf16[2,256,768]{2,1,0:T(8,128)(2,1)} %get-tuple-element.1923) | copy-start | bytes 2359300 | tf_op jit(solution)/shard_map/while
  426.6 12.9 %collective-permute-start = (bf16[256,768]{1,0:T(8,128)(2,1)}, bf16[256,768]{1,0:T(8,128)(2,1)}, u32[]{:S(2)}, u32[]{:S(2)}) collective-permute-start(bf16[256,768]{1,0:T(8,128)(2,1)} %get-tuple-element.1820), channel_id=1, source_target_pairs={{0,16},{1,17},{2,18},{3,19},{4,20},{5,21},{6,22},{7,23},{8,24},{9,... | collective-permute-start | bytes 1179656 | tf_op jit(solution)/shard_map/while/body/eval_jaxpr/ppermute | solution.py:19
  463.3 12.5 copy-start.1
  463.4 12.4 slice-start.3
  465.1 10.7 copy-start.7
  465.1 10.7 slice-start.4
  465.1 10.7 slice-start.5
  489.3 26.7 %collective-permute-start.1 = (bf16[256,768]{1,0:T(8,128)(2,1)}, bf16[256,768]{1,0:T(8,128)(2,1)}, u32[]{:S(2)}, u32[]{:S(2)}) collective-permute-start(bf16[256,768]{1,0:T(8,128)(2,1)} %get-tuple-element.1876), channel_id=1, source_target_pairs={{16,0},{17,1},{18,2},{19,3},{20,4},{21,5},{22,6},{23,7},{24,8},{25... | collective-permute-start | bytes 1179656 | tf_op jit(solution)/shard_map/while/body/eval_jaxpr/ppermute | solution.py:19
  537.3 12.5 copy-start.1
  537.3 12.4 slice-start.3
  539.0 10.7 copy-start.7
  563.3 38.0 %collective-permute-start.1 = (bf16[256,768]{1,0:T(8,128)(2,1)}, bf16[256,768]{1,0:T(8,128)(2,1)}, u32[]{:S(2)}, u32[]{:S(2)}) collective-permute-start(bf16[256,768]{1,0:T(8,128)(2,1)} %get-tuple-element.1876), channel_id=1, source_target_pairs={{16,0},{17,1},{18,2},{19,3},{20,4},{21,5},{22,6},{23,7},{24,8},{25... | collective-permute-start | bytes 1179656 | tf_op jit(solution)/shard_map/while/body/eval_jaxpr/ppermute | solution.py:19
  585.5 12.2 copy-start.42
  585.5 12.1 copy-start.44
  585.5 12.2 copy-start.25
  622.6 12.5 copy-start.1
  622.7 12.4 slice-start.3
  624.4 10.7 copy-start.7
  648.6 38.0 %collective-permute-start.1 = (bf16[256,768]{1,0:T(8,128)(2,1)}, bf16[256,768]{1,0:T(8,128)(2,1)}, u32[]{:S(2)}, u32[]{:S(2)}) collective-permute-start(bf16[256,768]{1,0:T(8,128)(2,1)} %get-tuple-element.1876), channel_id=1, source_target_pairs={{16,0},{17,1},{18,2},{19,3},{20,4},{21,5},{22,6},{23,7},{24,8},{25... | collective-permute-start | bytes 1179656 | tf_op jit(solution)/shard_map/while/body/eval_jaxpr/ppermute | solution.py:19
  670.8 12.2 copy-start.42
  670.9 12.1 copy-start.44
  670.9 12.2 copy-start.25
  688.3 115.7 %reduce-scatter.19.cloned.1.call-start = ((), (), s32[]{:S(2)}) async-start(), calls=%async_computation.14 | async-start | bytes 417792
  690.0 180.4 %reduce-scatter.13.cloned.1.call-start = ((), (), s32[]{:S(2)}) async-start(), calls=%async_computation.7 | async-start | bytes 2506752 | tf_op jit(solution)/shard_map/reduce_scatter | solution.py:304
  690.8 273.8 %reduce-scatter.11.cloned.1.call-start = ((), (), s32[]{:S(2)}) async-start(), calls=%async_computation.6 | async-start | bytes 7520256 | tf_op jit(solution)/shard_map/reduce_scatter | solution.py:303
  691.5 388.6 %reduce-scatter.17.cloned.1.call-start = ((), (), s32[]{:S(2)}) async-start(), calls=%async_computation.9 | async-start | bytes 10027008 | tf_op jit(solution)/shard_map/reduce_scatter | solution.py:309
  692.3 587.6 %reduce-scatter.15.cloned.1.call-start = ((), (), s32[]{:S(2)}) async-start(), calls=%async_computation.8 | async-start | bytes 20054016 | tf_op jit(solution)/shard_map/reduce_scatter | solution.py:308
  (164 other events, 703.4 us)
Sparse Core Ops, SparseCore 0:
  10.9 42.0 all-gather.12
  55.9 45.6 all-gather.10
  104.4 52.2 all-gather.16
  159.4 79.9 all-gather.14
  688.4 57.1 reduce-scatter.20
  749.4 54.5 reduce-scatter.18
  808.4 62.0 reduce-scatter.12
  875.5 88.9 reduce-scatter.10
  969.2 110.8 reduce-scatter.16
  1085.2 194.5 reduce-scatter.14
where the time goes:
time: 1290 us
  waiting for transfers between devices  768 us (60%)
  matrix products  244 us (19%)
  local copies, waits for them, and re-layouts  119 us (9%)
  other arithmetic  71.3 us (6%)
  blocking collectives  43 us (3%)
  starting transfers between devices  19.6 us (2%)
  between operations  14.3 us (1%)
    reduce_scatter x1, waiting for transfers between devices, shards(): lax.psum_scatter(summed[2], 'dp', scatter_dimension=0, tiled=True)  200 us
    reduce_scatter x1, waiting for transfers between devices, shards(): lax.psum_scatter(summed[3], 'dp', scatter_dimension=0, tiled=True)  116 us
    unnamed x12, waiting for transfers between devices  112 us
    reduce_scatter x1, waiting for transfers between devices, shards(): lax.psum_scatter(summed[0], 'dp', scatter_dimension=0, tiled=True)  94.1 us
    all_gather x1, waiting for transfers between devices, shards(): lax.all_gather(w_gate_up[0].astype(jnp.bfloat16), 'dp', axis=0, tiled=True)  82.7 us
    reduce_scatter x1, waiting for transfers between devices, shards(): lax.psum_scatter(summed[1], 'dp', scatter_dimension=0, tiled=True)  65 us
    all_gather x1, waiting for transfers between devices, shards(): lax.all_gather(w_down[0].astype(jnp.bfloat16), 'dp', axis=0, tiled=True)  55.1 us
    dot_general x3, matrix products, layer_forward(): jnp.dot(gated_rows, down_matrix, preferred_element_type=jnp.float32)  46.1 us
  transfers between devices with their start and end apart: 16, of which 10 were waited for; matrix products, arithmetic and copies ran while one was open for 9% of the time, Pallas kernels for 0%

commit v1 on v0

v1 whole, which is shorter than its diff:
```python
import functools

import jax
import jax.numpy as jnp
from jax import lax
from jax.experimental import pallas as pl
from jax.experimental.pallas import tpu as pltpu
from jax.sharding import PartitionSpec as P

D = 768
HEADS = 12
HEAD = 64
FF = 3072
SEQ = 256
MICRO = 2
EPSILON = 1e-05
FAR = 1e30
INV_SQRT_2PI = 0.3989422804014327
ROOT_HALF = 2.0 ** (-0.5)

COL_OUT = 3 * D
COL_GU = 4 * D
COL_DOWN = COL_GU + 2 * FF
COL_NORM = COL_DOWN + FF
WIDE = COL_NORM + 128

CHUNK = 1024
CHUNKS = FF // CHUNK
BF = jnp.bfloat16
F32 = jnp.float32
NN = (((1,), (0,)), ((), ()))
NT = (((1,), (1,)), ((), ()))
TN = (((0,), (0,)), ((), ()))
SLOPES = [2.0 ** (-8.0 * (h + 1) / HEADS) for h in range(HEADS)]

ANY = pl.BlockSpec(memory_space=pl.ANY)
SMEM = pl.BlockSpec(memory_space=pltpu.SMEM)


def matmul(left, right, dims=NN):
    return lax.dot_general(left, right, dims, preferred_element_type=F32)


def begin(source, target, semaphore):
    copy = pltpu.make_async_copy(source, target, semaphore)
    copy.start()
    return copy


def row_mean(values):
    return jnp.mean(values, axis=-1, keepdims=True)


def norm_forward(values, gain, bias):
    center = values - row_mean(values)
    inverse = lax.rsqrt(row_mean(center * center) + EPSILON)
    normed = center * inverse
    return normed * gain + bias, normed, inverse


def norm_backward(upstream, normed, inverse, gain):
    scaled = upstream * gain
    return inverse * (scaled - row_mean(scaled) - normed * row_mean(scaled * normed))


def forward_window(
    ids, lengths, given, wide, down, norms,
    x_out, qkv_out, probs_out, context_out, n1_out, h1_out, n2_out, inv_out, layer_out, hop_out,
    w_qkv, w_out, w_gu, w_down, x, qkv, probs, context, n1, h1, n2, inv, result, norm,
    w_sem, o_sem, i_sem, *, micro,
):
    window = ids[1]
    copies = {}
    copies["x"] = begin(given, x, i_sem.at[0])
    for k in range(3):
        cols = pl.ds(D * k, D)
        copies["qkv", k] = begin(wide.at[:, cols], w_qkv.at[:, cols], w_sem.at[k])
    copies["norm"] = begin(norms, norm, i_sem.at[1])

    def fetch_chunk(j):
        gate = wide.at[:, pl.ds(COL_GU + j * CHUNK, CHUNK)]
        rise = wide.at[:, pl.ds(COL_GU + FF + j * CHUNK, CHUNK)]
        copies["gate", j] = begin(gate, w_gu.at[j], w_sem.at[4 + j])
        copies["up", j] = begin(rise, w_gu.at[CHUNKS + j], w_sem.at[4 + CHUNKS + j])
        rows = down.at[pl.ds(j * CHUNK, CHUNK)]
        copies["down", j] = begin(rows, w_down.at[j], w_sem.at[4 + 2 * CHUNKS + j])

    flushed = []

    def flush(source, target):
        flushed.append(begin(source, target, o_sem.at[len(flushed)]))

    row_place = lax.broadcasted_iota(jnp.int32, (SEQ, SEQ), 0)
    key_place = lax.broadcasted_iota(jnp.int32, (SEQ, SEQ), 1)
    distance = jnp.abs(row_place - key_place).astype(F32)
    distance = jnp.where(key_place < lengths[micro, window], distance, FAR)
    lane = lax.broadcasted_iota(jnp.int32, (SEQ, 128), 1)
    first = lane < HEAD
    copies["x"].wait()
    rows_in = x[...]
    flush(x, x_out.at[micro])
    for k in range(3):
        copies["qkv", k].wait()
        if k == 1:
            copies["out"] = begin(wide.at[:, pl.ds(COL_OUT, D)], w_out, w_sem.at[3])
            fetch_chunk(0)
        if k == 2:
            for j in range(1, CHUNKS):
                fetch_chunk(j)
        cols = pl.ds(D * k, D)
        qkv[:, cols] = matmul(rows_in, w_qkv[:, cols]).astype(BF)
    flush(qkv, qkv_out.at[micro])
    for pair in range(HEADS // 2):
        query = qkv[:, pl.ds(128 * pair, 128)] * jnp.asarray(HEAD ** (-0.5), BF)
        key = qkv[:, pl.ds(D + 128 * pair, 128)]
        value = qkv[:, pl.ds(2 * D + 128 * pair, 128)]
        total = None
        for side in range(2):
            head = 2 * pair + side
            keep = first if side == 0 else ~first
            own_query = jnp.where(keep, query, jnp.zeros_like(query))
            own_value = jnp.where(keep, value, jnp.zeros_like(value))
            scores = matmul(own_query, key, NT) - distance * SLOPES[head]
            peak = jnp.max(scores, axis=-1, keepdims=True)
            grown = jnp.exp(scores - peak)
            share = 1.0 / jnp.sum(grown, axis=-1, keepdims=True)
            low_probs = (grown * share).astype(BF)
            probs[head] = low_probs
            mixed = matmul(low_probs, own_value)
            total = mixed if total is None else total + mixed
        context[:, pl.ds(128 * pair, 128)] = total.astype(BF)
    flush(probs, probs_out.at[micro])
    flush(context, context_out.at[micro])
    copies["out"].wait()
    copies["norm"].wait()
    summed = rows_in.astype(F32) + matmul(context[...], w_out[...])
    hidden, normed, inverse_one = norm_forward(summed, norm[0:1, :], norm[2:3, :])
    n1[...] = normed
    flush(n1, n1_out.at[micro])
    low_hidden = hidden.astype(BF)
    h1[...] = low_hidden
    flush(h1, h1_out.at[micro])
    for j in range(CHUNKS):
        copies["gate", j].wait()
        copies["up", j].wait()
        gate = matmul(low_hidden, w_gu[j])
        rise = matmul(low_hidden, w_gu[CHUNKS + j])
        gated = (gate * (0.5 * (1.0 + lax.erf(gate * ROOT_HALF))) * rise).astype(BF)
        copies["down", j].wait()
        hidden = hidden + matmul(gated, w_down[j])
    final, normed, inverse_two = norm_forward(hidden, norm[1:2, :], norm[3:4, :])
    result[...] = final.astype(BF)
    flush(result, hop_out)
    flush(result, layer_out.at[micro])
    n2[...] = normed
    flush(n2, n2_out.at[micro])
    inv[...] = jnp.where(first, inverse_one, inverse_two)
    flush(inv, inv_out.at[micro])
    for copy in flushed:
        copy.wait()


def backward_window(
    ids, given, wide, down, norms, qkv_in, probs_in, n1_in, h1_in, n2_in, inv_in,
    gated_out, down_out, gu_out, attn_out, qkv_out, grad_out, norm_out, hop_out,
    w_qkv, w_out, w_gu, w_down, upstream, qkv, probs, n1, h1, n2, inv, norm,
    gated, down_grad, gu_grad, attn_grad, context_grad, qkv_grad, grad, norm_grad, result,
    w_sem, o_sem, i_sem, *, micro,
):
    arriving = begin(given, upstream, i_sem.at[0])
    normed_two = begin(n2_in.at[micro], n2, i_sem.at[1])
    inverses = begin(inv_in.at[micro], inv, i_sem.at[2])
    gains = begin(norms, norm, i_sem.at[3])
    hidden = begin(h1_in.at[micro], h1, i_sem.at[4])
    copies = {}

    def fetch_chunk(j):
        gate = wide.at[:, pl.ds(COL_GU + j * CHUNK, CHUNK)]
        rise = wide.at[:, pl.ds(COL_GU + FF + j * CHUNK, CHUNK)]
        copies["gate", j] = begin(gate, w_gu.at[j], w_sem.at[j])
        copies["up", j] = begin(rise, w_gu.at[CHUNKS + j], w_sem.at[CHUNKS + j])
        rows = down.at[pl.ds(j * CHUNK, CHUNK)]
        copies["down", j] = begin(rows, w_down.at[j], w_sem.at[2 * CHUNKS + j])

    fetch_chunk(0)
    flushed = []

    def flush(source, target):
        flushed.append(begin(source, target, o_sem.at[len(flushed)]))

    arriving.wait()
    normed_two.wait()
    inverses.wait()
    gains.wait()
    up = upstream[...].astype(F32)
    normed = n2[...]
    grad_two = norm_backward(up, normed, inv[:, HEAD : HEAD + 1], norm[1:2, :])
    norm_grad[1:2, :] = jnp.sum(up * normed, axis=0, keepdims=True)
    norm_grad[3:4, :] = jnp.sum(up, axis=0, keepdims=True)
    low_grad = grad_two.astype(BF)
    down_grad[...] = low_grad
    flush(down_grad, down_out.at[micro])
    hidden.wait()
    low_hidden = h1[...]
    total = grad_two
    for j in range(CHUNKS):
        copies["gate", j].wait()
        copies["up", j].wait()
        if j + 1 < CHUNKS:
            fetch_chunk(j + 1)
        else:
            copies["probs"] = begin(probs_in.at[micro], probs, i_sem.at[5])
            copies["qkv"] = begin(qkv_in.at[micro], qkv, i_sem.at[6])
            copies["n1"] = begin(n1_in.at[micro], n1, i_sem.at[7])
            copies["out"] = begin(wide.at[:, pl.ds(COL_OUT, D)], w_out, w_sem.at[3 * CHUNKS])
            for k in range(3):
                cols = pl.ds(D * k, D)
                copies["w_qkv", k] = begin(
                    wide.at[:, cols], w_qkv.at[:, cols], w_sem.at[3 * CHUNKS + 1 + k]
                )
        gate = matmul(low_hidden, w_gu[j])
        rise = matmul(low_hidden, w_gu[CHUNKS + j])
        copies["down", j].wait()
        gated_grad = matmul(low_grad, w_down[j], NT)
        cdf = 0.5 * (1.0 + lax.erf(gate * ROOT_HALF))
        density = jnp.exp(-0.5 * gate * gate) * INV_SQRT_2PI
        bent = gate * cdf
        cols = pl.ds(j * CHUNK, CHUNK)
        late_cols = pl.ds(FF + j * CHUNK, CHUNK)
        gated[:, cols] = (bent * rise).astype(BF)
        flush(gated.at[:, cols], gated_out.at[micro, :, cols])
        gate_grad = (gated_grad * rise * (cdf + gate * density)).astype(BF)
        rise_grad = (gated_grad * bent).astype(BF)
        gu_grad[:, cols] = gate_grad
        gu_grad[:, late_cols] = rise_grad
        flush(gu_grad.at[:, cols], gu_out.at[micro, :, cols])
        flush(gu_grad.at[:, late_cols], gu_out.at[micro, :, late_cols])
        total = total + matmul(gate_grad, w_gu[j], NT) + matmul(rise_grad, w_gu[CHUNKS + j], NT)
    copies["n1"].wait()
    normed = n1[...]
    grad_one = norm_backward(total, normed, inv[:, 0:1], norm[0:1, :])
    norm_grad[0:1, :] = jnp.sum(total * normed, axis=0, keepdims=True)
    norm_grad[2:3, :] = jnp.sum(total, axis=0, keepdims=True)
    flush(norm_grad, norm_out.at[micro])
    low_attn = grad_one.astype(BF)
    attn_grad[...] = low_attn
    flush(attn_grad, attn_out.at[micro])
    copies["out"].wait()
    context_grad[...] = matmul(low_attn, w_out[...], NT).astype(BF)
    copies["probs"].wait()
    copies["qkv"].wait()
    first = lax.broadcasted_iota(jnp.int32, (SEQ, 128), 1) < HEAD
    root = jnp.asarray(HEAD ** (-0.5), BF)
    for pair in range(HEADS // 2):
        query = qkv[:, pl.ds(128 * pair, 128)] * root
        key = qkv[:, pl.ds(D + 128 * pair, 128)]
        value = qkv[:, pl.ds(2 * D + 128 * pair, 128)]
        upper = context_grad[:, pl.ds(128 * pair, 128)]
        query_across = query.T
        upper_across = upper.T
        query_sum, key_parts, value_parts = None, [], []
        for side in range(2):
            keep = first if side == 0 else ~first
            own_upper = jnp.where(keep, upper, jnp.zeros_like(upper))
            own_key = jnp.where(keep, key * root, jnp.zeros_like(key))
            low_probs = probs[2 * pair + side]
            wide_probs = low_probs.astype(F32)
            weighted = wide_probs * matmul(own_upper, value, NT)
            inner = jnp.sum(weighted, axis=-1, keepdims=True)
            score_grad = (weighted - wide_probs * inner).astype(BF)
            part = matmul(score_grad, own_key)
            query_sum = part if query_sum is None else query_sum + part
            rows = slice(HEAD * side, HEAD * (side + 1))
            key_parts.append(matmul(query_across[rows], score_grad))
            value_parts.append(matmul(upper_across[rows], low_probs))
        qkv_grad[:, pl.ds(128 * pair, 128)] = query_sum.astype(BF)
        key_grad = jnp.concatenate(key_parts, axis=0).T
        qkv_grad[:, pl.ds(D + 128 * pair, 128)] = key_grad.astype(BF)
        value_grad = jnp.concatenate(value_parts, axis=0).T
        qkv_grad[:, pl.ds(2 * D + 128 * pair, 128)] = value_grad.astype(BF)
    flush(qkv_grad, qkv_out.at[micro])
    input_grad = grad_one
    for k in range(3):
        copies["w_qkv", k].wait()
        cols = pl.ds(D * k, D)
        input_grad = input_grad + matmul(qkv_grad[:, cols], w_qkv[:, cols], NT)
    result[...] = input_grad.astype(BF)
    flush(result, hop_out)
    grad[...] = input_grad
    flush(grad, grad_out.at[micro])
    for copy in flushed:
        copy.wait()


FORWARD_KEPT = (
    (SEQ, D, BF),
    (SEQ, 3 * D, BF),
    (HEADS, SEQ, SEQ, BF),
    (SEQ, D, BF),
    (SEQ, D, F32),
    (SEQ, D, BF),
    (SEQ, D, F32),
    (SEQ, 128, F32),
    (SEQ, D, BF),
)
BACKWARD_KEPT = (
    (SEQ, FF, BF),
    (SEQ, D, BF),
    (SEQ, 2 * FF, BF),
    (SEQ, D, BF),
    (SEQ, 3 * D, BF),
    (SEQ, D, F32),
    (8, D, F32),
)
WEIGHT_SCRATCH = (
    pltpu.VMEM((D, 3 * D), BF),
    pltpu.VMEM((D, D), BF),
    pltpu.VMEM((2 * CHUNKS, D, CHUNK), BF),
    pltpu.VMEM((CHUNKS, CHUNK, D), BF),
)
DMA = pltpu.SemaphoreType.DMA


def guarded(body, inputs, kept, owner, carried):
    def kernel(*refs):
        @pl.when(refs[0][0] == owner)
        def _():
            skip = kept if carried else 0
            body(*refs[:inputs], *refs[inputs + skip :])

    return kernel


def call_window(body, name, owner, inputs, kept_shapes, before, scratch, flops, small):
    carried = before is not None
    count = len(kept_shapes)
    operands = tuple(inputs) + (tuple(before) if carried else ())
    shapes = [jax.ShapeDtypeStruct((MICRO,) + s[:-1], s[-1]) for s in kept_shapes]
    shapes.append(jax.ShapeDtypeStruct((SEQ, D), BF))
    specs = [SMEM] * small + [ANY] * (len(operands) - small)
    aliases = {len(inputs) + i: i for i in range(count)} if carried else {}
    return pl.pallas_call(
        guarded(body, len(inputs), count, owner, carried),
        out_shape=shapes,
        in_specs=specs,
        out_specs=[ANY] * (count + 1),
        input_output_aliases=aliases,
        scratch_shapes=list(WEIGHT_SCRATCH) + scratch,
        compiler_params=pltpu.CompilerParams(vmem_limit_bytes=58 << 20),
        cost_estimate=pl.CostEstimate(
            flops=flops, bytes_accessed=30_000_000, transcendentals=1_600_000
        ),
        name=name,
    )(*operands)


def forward_call(owner, micro, ids, lengths, given, wide, down, norms, before):
    scratch = [
        pltpu.VMEM((SEQ, D), BF),
        pltpu.VMEM((SEQ, 3 * D), BF),
        pltpu.VMEM((HEADS, SEQ, SEQ), BF),
        pltpu.VMEM((SEQ, D), BF),
        pltpu.VMEM((SEQ, D), F32),
        pltpu.VMEM((SEQ, D), BF),
        pltpu.VMEM((SEQ, D), F32),
        pltpu.VMEM((SEQ, 128), F32),
        pltpu.VMEM((SEQ, D), BF),
        pltpu.VMEM((8, D), F32),
        DMA((4 + 3 * CHUNKS,)),
        DMA((10,)),
        DMA((2,)),
    ]
    return call_window(
        functools.partial(forward_window, micro=micro),
        "layer_forward",
        owner,
        (ids, lengths, given, wide, down, norms),
        FORWARD_KEPT,
        before,
        scratch,
        5_000_000_000,
        2,
    )


def backward_call(owner, micro, ids, given, wide, down, norms, stash, before):
    scratch = [
        pltpu.VMEM((SEQ, D), BF),
        pltpu.VMEM((SEQ, 3 * D), BF),
        pltpu.VMEM((HEADS, SEQ, SEQ), BF),
        pltpu.VMEM((SEQ, D), F32),
        pltpu.VMEM((SEQ, D), BF),
        pltpu.VMEM((SEQ, D), F32),
        pltpu.VMEM((SEQ, 128), F32),
        pltpu.VMEM((8, D), F32),
        pltpu.VMEM((SEQ, FF), BF),
        pltpu.VMEM((SEQ, D), BF),
        pltpu.VMEM((SEQ, 2 * FF), BF),
        pltpu.VMEM((SEQ, D), BF),
        pltpu.VMEM((SEQ, D), BF),
        pltpu.VMEM((SEQ, 3 * D), BF),
        pltpu.VMEM((SEQ, D), F32),
        pltpu.VMEM((8, D), F32),
        pltpu.VMEM((SEQ, D), BF),
        DMA((4 + 3 * CHUNKS,)),
        DMA((6 + 3 * CHUNKS,)),
        DMA((8,)),
    ]
    return call_window(
        functools.partial(backward_window, micro=micro),
        "layer_backward",
        owner,
        (ids, given, wide, down, norms) + tuple(stash),
        BACKWARD_KEPT,
        before,
        scratch,
        8_000_000_000,
        1,
    )


def pack(w_qkv, w_out, w_gate_up, w_down, norm_gain, norm_bias):
    rows = w_qkv.shape[0]
    split_down = w_down.reshape(4, rows, D).transpose(1, 0, 2).reshape(rows, FF)
    norms = jnp.concatenate([norm_gain, norm_bias], axis=0).T
    norms = jnp.pad(norms, ((0, 0), (0, 128 - 4)))
    return jnp.concatenate([w_qkv, w_out, w_gate_up, split_down, norms], axis=1)


def shards(tokens, lengths, w_qkv, w_out, w_gate_up, w_down, norm_gain, norm_bias, cotangent):
    rows = w_qkv.shape[1]
    devices = D // rows
    section = lax.axis_index("section")
    ids = jnp.stack([section, lax.axis_index("dp")]).astype(jnp.int32)
    packed = pack(
        *(w[0].astype(BF) for w in (w_qkv, w_out, w_gate_up, w_down, norm_gain, norm_bias))
    )
    wide = lax.all_gather(packed, "dp", axis=0, tiled=True)
    down = wide[:, COL_DOWN:COL_NORM].reshape(devices, rows, 4, D)
    down = down.transpose(0, 2, 1, 3).reshape(FF, D)
    norms = wide[:, COL_NORM : COL_NORM + 8].astype(F32).T

    def hop(rows_sent, pair):
        return lax.ppermute(rows_sent, "section", [pair])

    common = (ids, lengths)
    weights = (wide, down, norms)
    *kept, sent = forward_call(0, 0, *common, tokens[0], *weights, None)
    arrived_first = hop(sent, (0, 1))
    *kept, sent = forward_call(0, 1, *common, tokens[1], *weights, kept)
    arrived_second = hop(sent, (0, 1))
    *kept, sent = forward_call(1, 0, *common, arrived_first, *weights, kept)
    *kept, sent = forward_call(1, 1, *common, arrived_second, *weights, kept)
    inputs, qkv, probs, context, n1, h1, n2, inv, layer_out = kept
    stash = (qkv, probs, n1, h1, n2, inv)

    *grads, sent = backward_call(1, 0, ids, cotangent[0], *weights, stash, None)
    arrived_first = hop(sent, (1, 0))
    *grads, sent = backward_call(1, 1, ids, cotangent[1], *weights, stash, grads)
    arrived_second = hop(sent, (1, 0))
    *grads, sent = backward_call(0, 0, ids, arrived_first, *weights, stash, grads)
    *grads, sent = backward_call(0, 1, ids, arrived_second, *weights, stash, grads)
    gated, down_grad, gu_grad, attn_grad, qkv_grad, input_grads, norm_grads = grads

    def flat(values):
        return values.reshape(MICRO * SEQ, values.shape[-1])

    def weight_grad(left, right):
        return matmul(flat(left), flat(right), TN)

    grad_qkv = weight_grad(inputs, qkv_grad).astype(BF)
    grad_out = weight_grad(context, attn_grad).astype(BF)
    grad_gu = weight_grad(h1, gu_grad).astype(BF)
    grad_down = weight_grad(gated, down_grad).astype(BF)
    grad_down = grad_down.reshape(devices, 4, rows, D).transpose(0, 2, 1, 3).reshape(D, FF)
    norm_sum = jnp.sum(norm_grads, axis=0)[:4].T.astype(BF)
    norm_sum = jnp.pad(norm_sum, ((0, 0), (0, 128 - 4)))
    summed = jnp.concatenate([grad_qkv, grad_out, grad_gu, grad_down, norm_sum], axis=1)
    share = lax.psum_scatter(summed, "dp", scatter_dimension=0, tiled=True).astype(F32)
    share_down = share[:, COL_DOWN:COL_NORM].reshape(rows, 4, D).transpose(1, 0, 2)
    share_norm = share[:, COL_NORM : COL_NORM + 4].T
    return (
        layer_out[None],
        input_grads[None],
        share[:, :COL_OUT][None],
        share[:, COL_OUT:COL_GU][None],
        share[:, COL_GU:COL_DOWN][None],
        share_down.reshape(4 * rows, D)[None],
        share_norm[:2][None],
        share_norm[2:][None],
    )


def solution(mesh):
    return jax.shard_map(
        shards,
        mesh=mesh,
        in_specs=(
            P(None, "dp", None),
            P(),
            P("section", "dp", None),
            P("section", "dp", None),
            P("section", "dp", None),
            P("section", "dp", None),
            P("section", None, "dp"),
            P("section", None, "dp"),
            P(None, "dp", None),
        ),
        out_specs=(
            P("section", None, "dp", None),
            P("section", None, "dp", None),
            P("section", "dp", None),
            P("section", "dp", None),
            P("section", "dp", None),
            P("section", "dp", None),
            P("section", None, "dp"),
            P("section", None, "dp"),
        ),
        check_vma=False,
    )
```

time: 1290 us -> 517 us (0.40)
  waiting for transfers between devices: 768 us -> 326 us
  matrix products: 244 us -> 18.9 us
  Pallas kernels: 0 us -> 92.2 us
  local copies, waits for them, and re-layouts: 119 us -> 44.7 us
  other arithmetic: 71.3 us -> 6.62 us
  blocking collectives: 43 us -> 0 us
  starting transfers between devices: 19.6 us -> 5.29 us
    reduce_scatter x4 -> x1, waiting for transfers between devices: 474 us -> 196 us  [shards(): lax.psum_scatter(summed, 'dp', scatter_dimension=0, tiled=True).astype(F32)]
    dot_general x57 -> x4, matrix products: 244 us -> 18.9 us  [matmul(): return lax.dot_general(left, right, dims, preferred_element_type=F32)]
    unnamed x12 -> x2, waiting for transfers between devices: 112 us -> 0.03 us
    pallas_call x0 -> x8, Pallas kernels: none -> 92.2 us  [call_window(): pl.pallas_call(guarded(body, len(inputs), count, owner, carried), out_sha...]
    all_gather x4 -> x1, waiting for transfers between devices: 181 us -> 100 us  [shards(): wide = lax.all_gather(packed, 'dp', axis=0, tiled=True)]
    dynamic_slice x57 -> x0, local copies, waits for them, and re-layouts: 45.6 us -> none  [the longest x27 15.5 us: store_slot(): previous = lax.dynamic_index_in_dim(buffer, slot_index, 0, keepdims=False)]
    all_gather x2 -> x0, blocking collectives: 43 us -> none  [the longest x1 24.4 us: shards(): lax.all_gather(norm_gain[0].astype(jnp.bfloat16), 'dp', axis=1, tiled=True)]
    ppermute x6 -> x4, waiting for transfers between devices: 0.61 us -> 29.7 us  [hop(): return lax.ppermute(rows_sent, 'section', [pair])]
  transfers between devices with their start and end apart: 16 -> 6, of which waited for: 10 -> 5; matrix products, arithmetic and copies ran while one was open for 9% -> 0% of each run, Pallas kernels for 0% -> 9%
where the time goes in v1:
time: 517 us; the launch traced here: 508 us
  waiting for transfers between devices  326 us (63%)
  Pallas kernels  92.2 us (18%)
  local copies, waits for them, and re-layouts  44.7 us (9%)
  matrix products  18.9 us (4%)
  between operations  14.6 us (3%)
  other arithmetic  6.62 us (1%)
  starting transfers between devices  5.29 us (1%)
    reduce_scatter x1, waiting for transfers between devices, shards(): lax.psum_scatter(summed, 'dp', scatter_dimension=0, tiled=True).astype(F32)  196 us
    all_gather x1, waiting for transfers between devices, shards(): wide = lax.all_gather(packed, 'dp', axis=0, tiled=True)  100 us
    pallas_call x8, Pallas kernels, call_window(): pl.pallas_call(guarded(body, len(inputs), count, owner, carried), out_sha...  92.2 us
    ppermute x4, waiting for transfers between devices, hop(): return lax.ppermute(rows_sent, 'section', [pair])  29.7 us
    dot_general x4, matrix products, matmul(): return lax.dot_general(left, right, dims, preferred_element_type=F32)  18.9 us
  transfers between devices with their start and end apart: 6, of which 5 were waited for; matrix products, arithmetic and copies ran while one was open for 0% of the time, Pallas kernels for 9%

profile of v1, /device:TPU:0, one launch (start us, length us, event | category | flops | bytes accessed | tf_op | source)
XLA Modules:
  0.0 507.9 jit_solution(9377556362244936314)
XLA Ops:
  7.2 0.8 convert_bitcast_fusion.1
  8.2 1.1 convert_element_type.67
  9.5 1.1 bitcast_dynamic-update-slice_fusion.1
  10.8 1.0 copy-done.5
  11.8 0.6 pad_add_fusion.refs_0_
  12.5 0.9 slice_bitcast_fusion.4
  13.4 0.9 slice_bitcast_fusion.2
  14.4 100.2 %all-gather.2.cloned.1.call-done.refs_3_.refs_2_ = bf16[768,12416]{1,0:T(8,128)(2,1)} async-done(((bf16[48,12416]{1,0:T(8,128)(2,1)}), bf16[768,12416]{1,0:T(8,128)(2,1)}) %all-gather.2.cloned.1.call-update) | async-done | bytes 19070992 | tf_op jit(solution)/shard_map/all_gather | solution.py:438
  114.5 0.9 slice.58
  116.2 4.8 slice.57
  121.0 9.7 %reshape.51 = bf16[16,48,4,768]{3,2,1,0:T(4,128)(2,1)} reshape(bf16[768,3072]{1,0:T(8,128)(2,1)} %slice.57) | data formatting | bytes 9437184 | tf_op jit(solution)/shard_map/reshape | solution.py:439
  130.8 5.5 %copy.112 = bf16[16,4,48,768]{3,2,1,0:T(8,128)(2,1)} copy(bf16[16,4,48,768]{3,1,2,0:T(4,128)(2,1)} %bitcast.81) | data formatting | bytes 9437184 | tf_op jit(solution)/shard_map/transpose | solution.py:440
  136.3 13.8 %layer_forward.4 = (bf16[2,256,768]{2,1,0:T(8,128)(2,1)}, bf16[2,256,2304]{2,1,0:T(8,128)(2,1)}, bf16[2,12,256,256]{3,2,1,0:T(8,128)(2,1)}, bf16[2,256,768]{2,1,...) custom-call(s32[2]{0:T(128)} %pad_add_fusion.refs_0_, ...), custom_call_target="tpu_custom_call" | custom-call | flops 5000000000 | bytes 30000000 | tf_op jit(solution)/shard_map/layer_forward/pallas_call | solution.py:342
  150.1 1.3 collective-permute-start.1
  151.4 14.0 %layer_forward.5 = (bf16[2,256,768]{2,1,0:T(8,128)(2,1)}, bf16[2,256,2304]{2,1,0:T(8,128)(2,1)}, bf16[2,12,256,256]{3,2,1,0:T(8,128)(2,1)}, bf16[2,256,768]{2,1,...) custom-call(s32[2]{0:T(128)} %pad_add_fusion.refs_0_, ...), custom_call_target="tpu_custom_call", output_to_operand_aliasing={{0}: (6, {}), {1}: (7, {}), {2}: (8, {}), {3}: (9, {}), {4}... | custom-call | flops 5000000000 | bytes 30000000 | tf_op jit(solution)/shard_map/layer_forward/pallas_call | solution.py:342
  165.4 1.3 collective-permute-start
  166.7 0.7 copy-done.10
  167.5 1.3 layer_forward.6
  168.8 7.3 %collective-permute-done.refs_2_ = bf16[256,768]{1,0:T(8,128)(2,1)S(1)} collective-permute-done((bf16[256,768]{1,0:T(8,128)(2,1)}, bf16[256,768]{1,0:T(8,128)(2,1)S(1)}, u32[]{:S(2)}, u32[]{:S(2)}) %collective-permute-start) | collective-permute-done | bytes 393248 | tf_op jit(solution)/shard_map/ppermute | solution.py:444
  176.1 0.7 copy-done.11
  176.8 5.8 %layer_forward.7 = (bf16[2,256,768]{2,1,0:T(8,128)(2,1)}, bf16[2,256,2304]{2,1,0:T(8,128)(2,1)}, bf16[2,12,256,256]{3,2,1,0:T(8,128)(2,1)}, bf16[2,256,768]{2,1,...) custom-call(s32[2]{0:T(128)} %pad_add_fusion.refs_0_, ...), custom_call_target="tpu_custom_call", output_to_operand_aliasing={{0}: (6, {}), {1}: (7, {}), {2}: (8, {}), {3}: (9, {}), {4}... | custom-call | flops 5000000000 | bytes 30000000 | tf_op jit(solution)/shard_map/layer_forward/pallas_call | solution.py:342
  182.6 9.1 %layer_backward.4 = (bf16[2,256,3072]{2,1,0:T(8,128)(2,1)}, bf16[2,256,768]{2,1,0:T(8,128)(2,1)}, bf16[2,256,6144]{2,1,0:T(8,128)(2,1)}, bf16[2,256,768]{2,1,0:T...) custom-call(s32[2]{0:T(128)} %pad_add_fusion.refs_0_, ...), custom_call_target="tpu_custom_call" | custom-call | flops 8000000000 | bytes 30000000 | tf_op jit(solution)/shard_map/layer_backward/pallas_call | solution.py:342
  191.7 1.3 collective-permute-start.3
  193.0 7.5 %layer_backward.5 = (bf16[2,256,3072]{2,1,0:T(8,128)(2,1)}, bf16[2,256,768]{2,1,0:T(8,128)(2,1)}, bf16[2,256,6144]{2,1,0:T(8,128)(2,1)}, bf16[2,256,768]{2,1,0:T...) custom-call(s32[2]{0:T(128)} %pad_add_fusion.refs_0_, ...), custom_call_target="tpu_custom_call", output_to_operand_aliasing={{0}: (11, {}), {1}: (12, {}), {2}: (13, {}), {3}: (14, {}),... | custom-call | flops 8000000000 | bytes 30000000 | tf_op jit(solution)/shard_map/layer_backward/pallas_call | solution.py:342
  200.5 1.3 collective-permute-start.2
  201.8 22.1 %collective-permute-done.3.refs_1_ = bf16[256,768]{1,0:T(8,128)(2,1)S(1)} collective-permute-done((bf16[256,768]{1,0:T(8,128)(2,1)}, bf16[256,768]{1,0:T(8,128)(2,1)S(1)}, u32[]{:S(2)}, u32[]{:S(2)}) %collective-permute-start.3) | collective-permute-done | bytes 393248 | tf_op jit(solution)/shard_map/ppermute | solution.py:444
  223.9 0.7 copy-done.12
  224.7 20.5 %layer_backward.6 = (bf16[2,256,3072]{2,1,0:T(8,128)(2,1)}, bf16[2,256,768]{2,1,0:T(8,128)(2,1)}, bf16[2,256,6144]{2,1,0:T(8,128)(2,1)}, bf16[2,256,768]{2,1,0:T...) custom-call(s32[2]{0:T(128)} %pad_add_fusion.refs_0_, ...), custom_call_target="tpu_custom_call", output_to_operand_aliasing={{0}: (11, {}), {1}: (12, {}), {2}: (13, {}), {3}: (14, {}),... | custom-call | flops 8000000000 | bytes 30000000 | tf_op jit(solution)/shard_map/layer_backward/pallas_call | solution.py:342
  245.5 0.7 copy-done.9
  246.3 20.2 %layer_backward.7 = (bf16[2,256,3072]{2,1,0:T(8,128)(2,1)}, bf16[2,256,768]{2,1,0:T(8,128)(2,1)}, bf16[2,256,6144]{2,1,0:T(8,128)(2,1)}, bf16[2,256,768]{2,1,0:T...) custom-call(s32[2]{0:T(128)} %pad_add_fusion.refs_0_, ...), custom_call_target="tpu_custom_call", output_to_operand_aliasing={{0}: (11, {}), {1}: (12, {}), {2}: (13, {}), {3}: (14, {}),... | custom-call | flops 8000000000 | bytes 30000000 | tf_op jit(solution)/shard_map/layer_backward/pallas_call | solution.py:342
  266.5 0.8 reduce_sum.9
  267.5 3.4 bitcast_convert_fusion.3
  270.9 2.4 copy.120
  273.3 4.0 bitcast_convert_fusion.1
  277.3 2.4 copy.118
  279.8 1.0 copy.131
  281.6 3.9 fusion.1
  285.5 1.2 constant_dynamic-update-slice_fusion.3
  286.7 7.7 %fusion = bf16[768,12416]{1,0:T(8,128)(2,1)} fusion(bf16[768,12416]{1,0:T(8,128)(2,1)} %constant_dynamic-update-slice_fusion.3, bf16[2,256,768]{2,1,0:T(8,128)(2,1)S(1)} %copy-done, bf16[2,256,6144]{2,1,0:T(8,128)(2,1)S(1)} %bitcast.79), kind=kOutput, calls=%fused_computation.1 | convolution fusion | flops 4836556800 | bytes 16515072 | tf_op jit(solution)/shard_map/dot_general | solution.py:41
  294.3 2.5 constant_dynamic-update-slice_fusion.2
  296.8 0.8 pad_dynamic-update-slice_fusion
  297.7 195.6 %reduce-scatter.2.cloned.1.call-done = bf16[48,12416]{1,0:T(8,128)(2,1)} async-done(((bf16[768,12416]{1,0:T(8,128)(2,1)}), bf16[48,12416]{1,0:T(8,128)(2,1)}) %reduce-scatter.2.cloned.1.call-update) | async-done | bytes 1191952 | tf_op jit(solution)/shard_map/reduce_scatter | solution.py:479
  493.3 1.4 convert_element_type.78
  494.8 0.7 slice_bitcast_fusion.6
  495.4 0.8 slice_bitcast_fusion.1
  496.2 1.1 slice_bitcast_fusion
  497.3 1.0 slice.63
  498.6 0.9 copy.121
  (51 shorter events, 4.3 us)
Async XLA Ops:
  7.2 3.4 copy-start.13
  7.2 3.4 copy-start.6
  7.2 107.3 %all-gather.2.cloned.1.call-start = ((), (), s32[]{:S(2)}) async-start(), calls=%async_computation.1 | async-start | bytes 20262912 | tf_op jit(solution)/shard_map/all_gather | solution.py:438
  9.5 3.0 copy-start.7
  10.7 2.7 copy-start.8
  10.7 1.0 copy-start.5
  11.8 481.5 %reduce-scatter.2.cloned.1.call-start = ((), (), s32[]{:S(2)}) async-start(), calls=%async_computation.2 | async-start | bytes 20262912 | tf_op jit(solution)/shard_map/reduce_scatter | solution.py:479
  150.1 16.6 %collective-permute-start.1 = (bf16[256,768]{1,0:T(8,128)(2,1)}, bf16[256,768]{1,0:T(8,128)(2,1)S(1)}, u32[]{:S(2)}, u32[]{:S(2)}) collective-permute-start(bf16[256,768]{1,0:T(8,128)(2,1)} %get-tuple-element.86), channel_id=1, source_target_pairs={{0,16},{1,17},{2,18},{3,19},{4,20},{5,21},{6,22},{7,23},{8,24},{9,... | collective-permute-start | bytes 1179656 | tf_op jit(solution)/shard_map/ppermute | solution.py:444
  165.4 10.7 %collective-permute-start = (bf16[256,768]{1,0:T(8,128)(2,1)}, bf16[256,768]{1,0:T(8,128)(2,1)S(1)}, u32[]{:S(2)}, u32[]{:S(2)}) collective-permute-start(bf16[256,768]{1,0:T(8,128)(2,1)} %get-tuple-element.85), channel_id=1, source_target_pairs={{0,16},{1,17},{2,18},{3,19},{4,20},{5,21},{6,22},{7,23},{8,24},{9,... | collective-permute-start | bytes 1179656 | tf_op jit(solution)/shard_map/ppermute | solution.py:444
  166.7 0.7 copy-start.10
  176.1 0.7 copy-start.11
  191.7 32.2 %collective-permute-start.3 = (bf16[256,768]{1,0:T(8,128)(2,1)}, bf16[256,768]{1,0:T(8,128)(2,1)S(1)}, u32[]{:S(2)}, u32[]{:S(2)}) collective-permute-start(bf16[256,768]{1,0:T(8,128)(2,1)} %get-tuple-element.120), channel_id=1, source_target_pairs={{16,0},{17,1},{18,2},{19,3},{20,4},{21,5},{22,6},{23,7},{24,8},{25... | collective-permute-start | bytes 1179656 | tf_op jit(solution)/shard_map/ppermute | solution.py:444
  200.5 45.0 %collective-permute-start.2 = (bf16[256,768]{1,0:T(8,128)(2,1)}, bf16[256,768]{1,0:T(8,128)(2,1)S(1)}, u32[]{:S(2)}, u32[]{:S(2)}) collective-permute-start(bf16[256,768]{1,0:T(8,128)(2,1)} %get-tuple-element.119), channel_id=1, source_target_pairs={{16,0},{17,1},{18,2},{19,3},{20,4},{21,5},{22,6},{23,7},{24,8},{25... | collective-permute-start | bytes 1179656 | tf_op jit(solution)/shard_map/ppermute | solution.py:444
  223.9 0.7 copy-start.12
  245.5 0.7 copy-start.9
  267.5 5.8 %copy-start.1 = (bf16[2,256,3072]{2,1,0:T(8,128)(2,1)S(1)}, bf16[2,256,3072]{2,1,0:T(8,128)(2,1)}, u32[]{:S(2)}) copy-start(bf16[2,256,3072]{2,1,0:T(8,128)(2,1)} %get-tuple-element.141) | copy-start | bytes 9437188
  279.8 1.7 copy-start.2
  279.8 1.8 copy-start.3
  279.8 6.8 %slice-start = ((s8[6291456]{0:T(1024)(128)(4,1)}), s8[2097152]{0:T(1024)(128)(4,1)S(1)}, s32[]{:S(2)}) async-start(s8[6291456]{0:T(1024)(128)(4,1)} %bitcast.78), calls=%async_computation.3 | async-start | bytes 4194304
  281.6 3.9 copy-start.4
  281.6 5.0 slice-start.1
  281.6 5.0 copy-start
Sparse Core Ops, SparseCore 0:
  11.9 102.5 all-gather.1
  297.8 195.4 reduce-scatter.1

commit v2 on v1

v2 whole, which is shorter than its diff:
```python
import functools

import jax
import jax.numpy as jnp
from jax import lax
from jax.experimental import pallas as pl
from jax.experimental.pallas import tpu as pltpu
from jax.sharding import PartitionSpec as P

D = 768
HEADS = 12
HEAD = 64
FF = 3072
SEQ = 256
MICRO = 2
TOKENS = 2 * MICRO * SEQ
EPSILON = 1e-05
FAR = 1e30
INV_SQRT_2PI = 0.3989422804014327
ROOT_HALF = 2.0 ** (-0.5)

COL_OUT = 3 * D
COL_GU = 4 * D
COL_DOWN = COL_GU + 2 * FF
COL_NORM = COL_DOWN + FF
WIDE = COL_NORM + 128

CHUNK = 768
CHUNKS = FF // CHUNK
ROWS = 48
BF = jnp.bfloat16
F32 = jnp.float32
NN = (((1,), (0,)), ((), ()))
NT = (((1,), (1,)), ((), ()))
TN = (((0,), (0,)), ((), ()))
SLOPES = [2.0 ** (-8.0 * (h + 1) / HEADS) for h in range(HEADS)]

VMEM_LIMIT = 64 << 20
ANY = pl.BlockSpec(memory_space=pl.ANY)
SMEM = pl.BlockSpec(memory_space=pltpu.SMEM)


def matmul(left, right, dims=NN):
    return lax.dot_general(left, right, dims, preferred_element_type=F32)


def begin(source, target, semaphore):
    copy = pltpu.make_async_copy(source, target, semaphore)
    copy.start()
    return copy


def own_window(given, micro):
    return given if len(given.shape) == 2 else given.at[micro]


def row_mean(values):
    return jnp.mean(values, axis=-1, keepdims=True)


def norm_forward(values, gain, bias):
    center = values - row_mean(values)
    inverse = lax.rsqrt(row_mean(center * center) + EPSILON)
    normed = center * inverse
    return normed * gain + bias, normed, inverse


def norm_backward(upstream, normed, inverse, gain):
    scaled = upstream * gain
    return inverse * (scaled - row_mean(scaled) - normed * row_mean(scaled * normed))


def forward_window(
    ids, lengths, given, wide, down, norms,
    left_out, qkv_out, probs_out, n1_out, h1_out, n2_out, inv_out, layer_out, hop_out,
    w_qkv, w_out, w_gu, w_down, x, qkv, probs, context, n1, h1, n2, inv, result, norm, left,
    w_sem, o_sem, i_sem, *, micro, direct,
):
    window = ids[1]
    copies = {}
    copies["x"] = begin(own_window(given, micro), x, i_sem.at[0])
    for k in range(3):
        cols = pl.ds(D * k, D)
        copies["qkv", k] = begin(wide.at[:, cols], w_qkv.at[:, cols], w_sem.at[k])
    copies["norm"] = begin(norms, norm, i_sem.at[1])

    def fetch_down(j, base):
        owners = down.at[pl.ds(4 * j, 4)]
        for q in range(4):
            source = owners.at[:, :, pl.ds(COL_DOWN + D * q, D)] if direct else owners.at[:, q]
            copies["down", j, q] = begin(
                source, w_down.at[j, :, q], w_sem.at[base + 4 * j + q]
            )

    def fetch_chunk(j):
        gate = wide.at[:, pl.ds(COL_GU + j * CHUNK, CHUNK)]
        rise = wide.at[:, pl.ds(COL_GU + FF + j * CHUNK, CHUNK)]
        copies["gate", j] = begin(gate, w_gu.at[j], w_sem.at[4 + j])
        copies["up", j] = begin(rise, w_gu.at[CHUNKS + j], w_sem.at[4 + CHUNKS + j])
        fetch_down(j, 4 + 2 * CHUNKS)

    flushed = []

    def flush(source, target):
        flushed.append(begin(source, target, o_sem.at[len(flushed)]))

    row_place = lax.broadcasted_iota(jnp.int32, (SEQ, SEQ), 0)
    key_place = lax.broadcasted_iota(jnp.int32, (SEQ, SEQ), 1)
    distance = jnp.abs(row_place - key_place).astype(F32)
    distance = jnp.where(key_place < lengths[micro, window], distance, FAR)
    lane = lax.broadcasted_iota(jnp.int32, (SEQ, 128), 1)
    first = lane < HEAD
    copies["x"].wait()
    rows_in = x[...]


    def flush_turned(part, values):
        rows = pl.ds(D * part, D)
        left[rows] = values.T
        flush(left.at[rows], left_out.at[rows])

    flush_turned(0, rows_in)
    for k in range(3):
        copies["qkv", k].wait()
        if k == 1:
            copies["out"] = begin(wide.at[:, pl.ds(COL_OUT, D)], w_out, w_sem.at[3])
            fetch_chunk(0)
        if k == 2:
            for j in range(1, CHUNKS):
                fetch_chunk(j)
        cols = pl.ds(D * k, D)
        qkv[:, cols] = matmul(rows_in, w_qkv[:, cols]).astype(BF)
    flush(qkv, qkv_out)
    for pair in range(HEADS // 2):
        query = qkv[:, pl.ds(128 * pair, 128)] * jnp.asarray(HEAD ** (-0.5), BF)
        key = qkv[:, pl.ds(D + 128 * pair, 128)]
        value = qkv[:, pl.ds(2 * D + 128 * pair, 128)]
        total = None
        for side in range(2):
            head = 2 * pair + side
            keep = first if side == 0 else ~first
            own_query = jnp.where(keep, query, jnp.zeros_like(query))
            own_value = jnp.where(keep, value, jnp.zeros_like(value))
            scores = matmul(own_query, key, NT) - distance * SLOPES[head]
            peak = jnp.max(scores, axis=-1, keepdims=True)
            grown = jnp.exp(scores - peak)
            share = 1.0 / jnp.sum(grown, axis=-1, keepdims=True)
            low_probs = (grown * share).astype(BF)
            probs[head] = low_probs
            mixed = matmul(low_probs, own_value)
            total = mixed if total is None else total + mixed
        context[:, pl.ds(128 * pair, 128)] = total.astype(BF)
    flush(probs, probs_out)
    flush_turned(1, context[...])
    copies["out"].wait()
    copies["norm"].wait()
    summed = rows_in.astype(F32) + matmul(context[...], w_out[...])
    hidden, normed, inverse_one = norm_forward(summed, norm[0:1, :], norm[2:3, :])
    n1[...] = normed
    flush(n1, n1_out)
    low_hidden = hidden.astype(BF)
    h1[...] = low_hidden
    flush(h1, h1_out)
    flush_turned(2, low_hidden)
    for j in range(CHUNKS):
        copies["gate", j].wait()
        copies["up", j].wait()
        gate = matmul(low_hidden, w_gu[j])
        rise = matmul(low_hidden, w_gu[CHUNKS + j])
        gated = (gate * (0.5 * (1.0 + lax.erf(gate * ROOT_HALF))) * rise).astype(BF)
        for q in range(4):
            copies["down", j, q].wait()
        hidden = hidden + matmul(gated, w_down[j].reshape(CHUNK, D))
    final, normed, inverse_two = norm_forward(hidden, norm[1:2, :], norm[3:4, :])
    result[...] = final.astype(BF)
    flush(result, hop_out)
    flush(result, layer_out)
    n2[...] = normed
    flush(n2, n2_out)
    inv[...] = jnp.where(first, inverse_one, inverse_two)
    flush(inv, inv_out)
    for copy in flushed:
        copy.wait()


def backward_hidden(
    ids, given, wide, down, norms, n1_in, h1_in, n2_in, inv_in, hidden_out, gate_out, up_out,
    w_gu, w_down, upstream, n1, h1, n2, inv, norm, gated, down_grad, gu_grad, norm_grad,
    low_norm, w_sem, o_sem, i_sem, *, micro, direct, ahead,
):
    arriving = begin(own_window(given, micro), upstream, i_sem.at[0])
    normed_two = begin(n2_in.at[micro], n2, i_sem.at[1])
    inverses = begin(inv_in.at[micro], inv, i_sem.at[2])
    gains = begin(norms, norm, i_sem.at[3])
    hidden = begin(h1_in.at[micro], h1, i_sem.at[4])
    copies = {}

    def fetch_down(j, base):
        owners = down.at[pl.ds(4 * j, 4)]
        for q in range(4):
            source = owners.at[:, :, pl.ds(COL_DOWN + D * q, D)] if direct else owners.at[:, q]
            copies["down", j, q] = begin(
                source, w_down.at[j, :, q], w_sem.at[base + 4 * j + q]
            )

    def fetch_chunk(j):
        gate = wide.at[:, pl.ds(COL_GU + j * CHUNK, CHUNK)]
        rise = wide.at[:, pl.ds(COL_GU + FF + j * CHUNK, CHUNK)]
        copies["gate", j] = begin(gate, w_gu.at[j], w_sem.at[j])
        copies["up", j] = begin(rise, w_gu.at[CHUNKS + j], w_sem.at[CHUNKS + j])
        fetch_down(j, 2 * CHUNKS)

    fetch_chunk(0)
    flushed = []

    def flush(source, target):
        flushed.append(begin(source, target, o_sem.at[len(flushed)]))

    arriving.wait()
    normed_two.wait()
    inverses.wait()
    gains.wait()
    up = upstream[...].astype(F32)
    normed = n2[...]
    grad_two = norm_backward(up, normed, inv[:, HEAD : HEAD + 1], norm[1:2, :])
    norm_grad[...] = jnp.zeros_like(norm_grad)
    norm_grad[1:2, :] = jnp.sum(up * normed, axis=0, keepdims=True)
    norm_grad[3:4, :] = jnp.sum(up, axis=0, keepdims=True)
    low_grad = grad_two.astype(BF)
    down_grad[...] = low_grad.T
    flush(down_grad, hidden_out.at[pl.ds(FF, D)])
    hidden.wait()
    low_hidden = h1[...]
    total = grad_two
    for j in range(CHUNKS):
        copies["gate", j].wait()
        copies["up", j].wait()
        if j + 1 < CHUNKS:
            fetch_chunk(j + 1)
        else:
            first_norm = begin(n1_in.at[micro], n1, i_sem.at[5])
            ahead()
        gate = matmul(low_hidden, w_gu[j])
        rise = matmul(low_hidden, w_gu[CHUNKS + j])
        for q in range(4):
            copies["down", j, q].wait()
        gated_grad = matmul(low_grad, w_down[j].reshape(CHUNK, D), NT)
        cdf = 0.5 * (1.0 + lax.erf(gate * ROOT_HALF))
        density = jnp.exp(-0.5 * gate * gate) * INV_SQRT_2PI
        bent = gate * cdf
        cols = pl.ds(j * CHUNK, CHUNK)
        late_cols = pl.ds(FF + j * CHUNK, CHUNK)
        gated[cols] = (bent * rise).astype(BF).T
        flush(gated.at[cols], hidden_out.at[cols])
        gate_grad = (gated_grad * rise * (cdf + gate * density)).astype(BF)
        rise_grad = (gated_grad * bent).astype(BF)
        gu_grad[:, cols] = gate_grad
        gu_grad[:, late_cols] = rise_grad
        flush(gu_grad.at[:, cols], gate_out.at[:, cols])
        flush(gu_grad.at[:, late_cols], up_out.at[:, cols])
        total = total + matmul(gate_grad, w_gu[j], NT) + matmul(rise_grad, w_gu[CHUNKS + j], NT)
    first_norm.wait()
    normed = n1[...]
    grad_one = norm_backward(total, normed, inv[:, 0:1], norm[0:1, :])
    norm_grad[0:1, :] = jnp.sum(total * normed, axis=0, keepdims=True)
    norm_grad[2:3, :] = jnp.sum(total, axis=0, keepdims=True)
    low_norm[...] = norm_grad[...].astype(BF)
    for k in range(3):
        source = low_norm.at[:, pl.ds(SEQ * k, SEQ)]
        flush(source, hidden_out.at[pl.ds(FF + D + 16 * k, 16)])
    return grad_one, flushed


def fetch_attention(wide, qkv_in, probs_in, w_qkv, w_out, qkv, probs, w_sem, i_sem, micro):
    copies = [
        begin(wide.at[:, pl.ds(COL_OUT, D)], w_out, w_sem.at[0]),
        begin(probs_in.at[micro], probs, i_sem.at[0]),
        begin(qkv_in.at[micro], qkv, i_sem.at[1]),
    ]
    for k in range(3):
        cols = pl.ds(D * k, D)
        copies.append(begin(wide.at[:, cols], w_qkv.at[:, cols], w_sem.at[1 + k]))
    return copies


def backward_attention(
    grad_one, copies, qk_out, vc_out, grad_out, hop_out,
    w_qkv, w_out, qkv, probs, attn_grad, context_grad, qkv_grad, grad, result,
    o_sem, *, micro,
):
    flushed = []

    def flush(source, target):
        flushed.append(begin(source, target, o_sem.at[len(flushed)]))

    low_attn = grad_one.astype(BF)
    attn_grad[...] = low_attn
    flush(attn_grad, vc_out.at[:, pl.ds(D, D)])
    copies[0].wait()
    context_grad[...] = matmul(low_attn, w_out[...], NT).astype(BF)
    copies[1].wait()
    copies[2].wait()
    first = lax.broadcasted_iota(jnp.int32, (SEQ, 128), 1) < HEAD
    root = jnp.asarray(HEAD ** (-0.5), BF)
    for pair in range(HEADS // 2):
        query = qkv[:, pl.ds(128 * pair, 128)] * root
        key = qkv[:, pl.ds(D + 128 * pair, 128)]
        value = qkv[:, pl.ds(2 * D + 128 * pair, 128)]
        upper = context_grad[:, pl.ds(128 * pair, 128)]
        query_across = query.T
        upper_across = upper.T
        query_sum, key_parts, value_parts = None, [], []
        for side in range(2):
            keep = first if side == 0 else ~first
            own_upper = jnp.where(keep, upper, jnp.zeros_like(upper))
            own_key = jnp.where(keep, key * root, jnp.zeros_like(key))
            low_probs = probs[2 * pair + side]
            wide_probs = low_probs.astype(F32)
            weighted = wide_probs * matmul(own_upper, value, NT)
            inner = jnp.sum(weighted, axis=-1, keepdims=True)
            score_grad = (weighted - wide_probs * inner).astype(BF)
            part = matmul(score_grad, own_key)
            query_sum = part if query_sum is None else query_sum + part
            rows = slice(HEAD * side, HEAD * (side + 1))
            key_parts.append(matmul(query_across[rows], score_grad))
            value_parts.append(matmul(upper_across[rows], low_probs))
        qkv_grad[:, pl.ds(128 * pair, 128)] = query_sum.astype(BF)
        key_grad = jnp.concatenate(key_parts, axis=0).T
        qkv_grad[:, pl.ds(D + 128 * pair, 128)] = key_grad.astype(BF)
        value_grad = jnp.concatenate(value_parts, axis=0).T
        qkv_grad[:, pl.ds(2 * D + 128 * pair, 128)] = value_grad.astype(BF)
    flush(qkv_grad.at[:, pl.ds(0, 2 * D)], qk_out)
    flush(qkv_grad.at[:, pl.ds(2 * D, D)], vc_out.at[:, pl.ds(0, D)])
    input_grad = grad_one
    for k in range(3):
        copies[3 + k].wait()
        cols = pl.ds(D * k, D)
        input_grad = input_grad + matmul(qkv_grad[:, cols], w_qkv[:, cols], NT)
    result[...] = input_grad.astype(BF)
    flush(result, hop_out)
    grad[...] = input_grad
    flush(grad, grad_out)
    return flushed


def backward_window(
    ids, given, wide, down, norms, qkv_in, probs_in, n1_in, h1_in, n2_in, inv_in,
    hidden_out, gate_out, up_out, qk_out, vc_out, grad_out, hop_out,
    w_gu, w_down, upstream, n1, h1, n2, inv, norm, gated, down_grad, gu_grad, norm_grad, low_norm,
    w_qkv, w_out, qkv, probs, attn_grad, context_grad, qkv_grad, grad, result,
    w_sem, o_sem, i_sem, *, micro, direct,
):
    copies = []

    def ahead():
        copies.extend(
            fetch_attention(
                wide, qkv_in, probs_in, w_qkv, w_out, qkv, probs,
                w_sem.at[pl.ds(6 * CHUNKS, 4)], i_sem.at[pl.ds(6, 2)], micro,
            )
        )

    grad_one, flushed = backward_hidden(
        ids, given, wide, down, norms, n1_in, h1_in, n2_in, inv_in, hidden_out, gate_out, up_out,
        w_gu, w_down, upstream, n1, h1, n2, inv, norm, gated, down_grad, gu_grad, norm_grad,
        low_norm, w_sem, o_sem, i_sem, micro=micro, direct=direct, ahead=ahead,
    )
    flushed += backward_attention(
        grad_one, copies, qk_out, vc_out, grad_out, hop_out,
        w_qkv, w_out, qkv, probs, attn_grad, context_grad, qkv_grad, grad, result,
        o_sem.at[pl.ds(HIDDEN_STORES, 5)], micro=micro,
    )
    for copy in flushed:
        copy.wait()


def backward_first_half(
    ids, given, wide, down, norms, n1_in, h1_in, n2_in, inv_in,
    hidden_out, gate_out, up_out, half_out,
    w_gu, w_down, upstream, n1, h1, n2, inv, norm, gated, down_grad, gu_grad, norm_grad, low_norm,
    half, w_sem, o_sem, i_sem, *, micro, direct,
):
    grad_one, flushed = backward_hidden(
        ids, given, wide, down, norms, n1_in, h1_in, n2_in, inv_in, hidden_out, gate_out, up_out,
        w_gu, w_down, upstream, n1, h1, n2, inv, norm, gated, down_grad, gu_grad, norm_grad,
        low_norm, w_sem, o_sem, i_sem, micro=micro, direct=direct, ahead=lambda: None,
    )
    half[...] = grad_one
    flushed.append(begin(half, half_out, o_sem.at[HIDDEN_STORES]))
    for copy in flushed:
        copy.wait()


def backward_second_half(
    ids, given, wide, qkv_in, probs_in,
    qk_out, vc_out, grad_out, hop_out,
    half, w_qkv, w_out, qkv, probs, attn_grad, context_grad, qkv_grad, grad, result,
    w_sem, o_sem, i_sem, *, micro,
):
    arriving = begin(given, half, i_sem.at[2])
    copies = fetch_attention(
        wide, qkv_in, probs_in, w_qkv, w_out, qkv, probs, w_sem, i_sem, micro
    )
    arriving.wait()
    flushed = backward_attention(
        half[...], copies, qk_out, vc_out, grad_out, hop_out,
        w_qkv, w_out, qkv, probs, attn_grad, context_grad, qkv_grad, grad, result,
        o_sem, micro=micro,
    )
    for copy in flushed:
        copy.wait()


FORWARD_KEPT = (
    (True, 3 * D, SEQ, BF),
    (True, SEQ, 3 * D, BF),
    (True, HEADS, SEQ, SEQ, BF),
    (True, SEQ, D, F32),
    (True, SEQ, D, BF),
    (True, SEQ, D, F32),
    (True, SEQ, 128, F32),
    (True, SEQ, D, BF),
)
HIDDEN_KEPT = ((False, FF + D + 48, SEQ, BF), (False, SEQ, FF, BF), (False, SEQ, FF, BF))
ATTENTION_KEPT = ((False, SEQ, 2 * D, BF), (False, SEQ, 2 * D, BF), (True, SEQ, D, F32))
HIDDEN_STORES = 3 * CHUNKS + 4
HIDDEN_WEIGHTS = (
    pltpu.VMEM((2 * CHUNKS, D, CHUNK), BF),
    pltpu.VMEM((CHUNKS, 4, 4, ROWS, D), BF),
)
ATTENTION_WEIGHTS = (pltpu.VMEM((D, 3 * D), BF), pltpu.VMEM((D, D), BF))
HIDDEN_SCRATCH = HIDDEN_WEIGHTS + (
    pltpu.VMEM((SEQ, D), BF),
    pltpu.VMEM((SEQ, D), F32),
    pltpu.VMEM((SEQ, D), BF),
    pltpu.VMEM((SEQ, D), F32),
    pltpu.VMEM((SEQ, 128), F32),
    pltpu.VMEM((8, D), F32),
    pltpu.VMEM((FF, SEQ), BF),
    pltpu.VMEM((D, SEQ), BF),
    pltpu.VMEM((SEQ, 2 * FF), BF),
    pltpu.VMEM((16, D), F32),
    pltpu.VMEM((16, D), BF),
)
ATTENTION_SCRATCH = ATTENTION_WEIGHTS + (
    pltpu.VMEM((SEQ, 3 * D), BF),
    pltpu.VMEM((HEADS, SEQ, SEQ), BF),
    pltpu.VMEM((SEQ, D), BF),
    pltpu.VMEM((SEQ, D), BF),
    pltpu.VMEM((SEQ, 3 * D), BF),
    pltpu.VMEM((SEQ, D), F32),
    pltpu.VMEM((SEQ, D), BF),
)
DMA = pltpu.SemaphoreType.DMA


def call_window(
    body, name, owner, micro, inputs, kept_shapes, sent, before, scratch, flops, small, gates=()
):
    count = len(kept_shapes)
    operands = tuple(inputs)
    aliases = {}
    for position, array in enumerate(before):
        if array is not None:
            aliases[len(operands)] = position
            operands += (array,)
    operands += tuple(gates)
    shapes = [
        jax.ShapeDtypeStruct((MICRO,) * shared + tuple(shape), dtype)
        for shared, *shape, dtype in kept_shapes
    ]
    shapes.append(jax.ShapeDtypeStruct((SEQ, D), sent))

    def kernel(*refs):
        @pl.when(refs[0][0] == owner)
        def _():
            outs = refs[len(operands) : len(operands) + count]
            views = [
                ref.at[micro] if shared else ref
                for ref, (shared, *_) in zip(outs, kept_shapes)
            ]
            body(*refs[: len(inputs)], *views, *refs[len(operands) + count :])

    return pl.pallas_call(
        kernel,
        out_shape=shapes,
        in_specs=[SMEM] * small + [ANY] * (len(operands) - small),
        out_specs=[ANY] * len(shapes),
        input_output_aliases=aliases,
        scratch_shapes=list(scratch),
        compiler_params=pltpu.CompilerParams(vmem_limit_bytes=VMEM_LIMIT),
        cost_estimate=pl.CostEstimate(
            flops=flops, bytes_accessed=flops // 200, transcendentals=flops // 4000
        ),
        name=name,
    )(*operands)


def forward_call(owner, micro, direct, ids, lengths, given, wide, down, norms, before):
    scratch = (
        ATTENTION_WEIGHTS
        + HIDDEN_WEIGHTS
        + (
            pltpu.VMEM((SEQ, D), BF),
            pltpu.VMEM((SEQ, 3 * D), BF),
            pltpu.VMEM((HEADS, SEQ, SEQ), BF),
            pltpu.VMEM((SEQ, D), BF),
            pltpu.VMEM((SEQ, D), F32),
            pltpu.VMEM((SEQ, D), BF),
            pltpu.VMEM((SEQ, D), F32),
            pltpu.VMEM((SEQ, 128), F32),
            pltpu.VMEM((SEQ, D), BF),
            pltpu.VMEM((8, D), F32),
            pltpu.VMEM((3 * D, SEQ), BF),
            DMA((4 + 6 * CHUNKS,)),
            DMA((12,)),
            DMA((2,)),
        )
    )
    return call_window(
        functools.partial(forward_window, micro=micro, direct=direct),
        "layer_forward",
        owner,
        micro,
        (ids, lengths, given, wide, down, norms),
        FORWARD_KEPT,
        BF,
        before,
        scratch,
        5_000_000_000,
        2,
    )


def backward_call(owner, micro, direct, ids, given, wide, down, norms, stash, before, gates):
    return call_window(
        functools.partial(backward_window, micro=micro, direct=direct),
        "layer_backward",
        owner,
        micro,
        (ids, given, wide, down, norms) + tuple(stash),
        HIDDEN_KEPT + ATTENTION_KEPT,
        BF,
        before,
        HIDDEN_SCRATCH
        + ATTENTION_SCRATCH
        + (DMA((4 + 6 * CHUNKS,)), DMA((HIDDEN_STORES + 5,)), DMA((8,))),
        8_000_000_000,
        1,
        gates,
    )


def first_half_call(
    owner, micro, direct, ids, given, wide, down, norms, stash, before, gates
):
    return call_window(
        functools.partial(backward_first_half, micro=micro, direct=direct),
        "backward_hidden",
        owner,
        micro,
        (ids, given, wide, down, norms) + tuple(stash),
        HIDDEN_KEPT,
        F32,
        before,
        HIDDEN_SCRATCH
        + (
            pltpu.VMEM((SEQ, D), F32),
            DMA((6 * CHUNKS,)),
            DMA((HIDDEN_STORES + 1,)),
            DMA((6,)),
        ),
        60_000_000_000,
        1,
        gates,
    )


def second_half_call(owner, micro, ids, given, wide, stash, before, gates):
    return call_window(
        functools.partial(backward_second_half, micro=micro),
        "backward_attention",
        owner,
        micro,
        (ids, given, wide) + tuple(stash),
        ATTENTION_KEPT,
        BF,
        before,
        (pltpu.VMEM((SEQ, D), F32),) + ATTENTION_SCRATCH + (DMA((4,)), DMA((5,)), DMA((3,))),
        1000,
        1,
        gates,
    )


def pack(w_qkv, w_out, w_gate_up, w_down, norm_gain, norm_bias):
    rows = w_qkv.shape[0]
    split_down = w_down.reshape(4, rows, D).transpose(1, 0, 2).reshape(rows, FF)
    norms = jnp.concatenate([norm_gain, norm_bias], axis=0).T
    norms = jnp.pad(norms, ((0, 0), (0, 128 - 4)))
    return jnp.concatenate([w_qkv, w_out, w_gate_up, split_down, norms], axis=1)


BIT_CORE, BIT_X, BIT_NEAR, BIT_FAR = 1, 2, 4, 8


def weight_grad_kernel(ids, terms, norm_ins, sent, kept, scratch, *, rows, order, turned):
    buffers, result, i_sem, o_sem = scratch[:4]
    columns, pieces, count = 0, [], 0

    def fetch(source, target):
        nonlocal count
        count += 1
        return begin(source, target, i_sem.at[count - 1])

    owned = []
    for place in range(8):
        relative = sum(bit for k, bit in enumerate(order) if not (place >> (2 - k)) & 1)
        owned.append(ids[1] ^ relative)
    for term, (lefts, rights) in enumerate(terms):
        left_buffer, right_buffer = buffers[term]
        whole = []
        for k, left in enumerate(lefts):
            for place in range(8):
                source = left.at[pl.ds(pl.multiple_of(owned[place] * rows, 16), rows)]
                target = left_buffer.at[place, :, pl.ds(SEQ * k, SEQ)]
                whole.append(fetch(source, target))
        for start in range(0, D if turned else right_buffer.shape[1], D):
            cols = pl.ds(start, D)
            parts = []
            for k, right in enumerate(rights):
                tokens = pl.ds(SEQ * k, SEQ)
                if turned:
                    parts.append(fetch(right, right_buffer.at[:, tokens]))
                else:
                    parts.append(fetch(right.at[:, cols], right_buffer.at[tokens, cols]))
            pieces.append((term, start, whole, parts, columns))
            columns += D
            whole = []
    if norm_ins:
        norm_buffer, norm_turned, norm_sem = scratch[4:]
        norm_loads = [
            begin(source.at[pl.ds(16 * k, 16)], norm_buffer.at[n, :, pl.ds(SEQ * k, SEQ)], norm_sem.at[n, k])
            for n, source in enumerate(norm_ins)
            for k in range(3)
        ]
    stores = []

    def store(first, count, cols):
        target = sent if first < 4 else kept
        source = result.at[pl.ds(first, count), :, cols]
        place = target.at[pl.ds(first % 4, count), :, cols]
        stores.append(begin(source, place, o_sem.at[len(stores)]))

    group = 192 // rows
    for term, start, whole, parts, column in pieces:
        left_buffer, right_buffer = buffers[term]
        for load in whole + parts:
            load.wait()
        values = right_buffer[...] if turned else right_buffer[:, pl.ds(start, D)]
        cols = pl.ds(column, D)
        for first in range(0, 8, 2 * group):
            taken = left_buffer[pl.ds(first, 2 * group)].reshape(2 * group * rows, TOKENS)
            value = matmul(taken, values, NT if turned else NN).astype(BF)
            result[pl.ds(first, 2 * group), :, cols] = value.reshape(2 * group, rows, D)
            for half in range(2):
                store(first + group * half, group, cols)
    if norm_ins:
        for load in norm_loads:
            load.wait()
        total = sum(norm_buffer[n].astype(F32) for n in range(4))
        total = jnp.concatenate([total, jnp.zeros((112, D), F32)], axis=0).T.astype(BF)
        norm_turned[...] = total.reshape(16, rows, 128)
        cols = pl.ds(columns, 128)
        for place in range(8):
            result[place, :, cols] = norm_turned[owned[place]]
        store(0, 4, cols)
        store(4, 4, cols)
    for copy in stores:
        copy.wait()


def weight_grad(ids, pairs, rows, order, gates, norms=None, turned=False):
    width = 0
    arrays, scratch = [], []

    def position(array):
        for k, known in enumerate(arrays):
            if known is array:
                return k
        arrays.append(array)
        return len(arrays) - 1

    def placed(side):
        return [(position(array), micro) for array, micro in side[0]], side[1]

    terms = [(placed(left), placed(right)) for left, right in pairs]
    norm_places = placed(norms) if norms else None
    loads, stores = 0, 0
    for _, (_, taken) in terms:
        size = taken.stop - taken.start
        shape = (size, TOKENS) if turned else (TOKENS, size)
        scratch += [pltpu.VMEM((8, rows, TOKENS), BF), pltpu.VMEM(shape, BF)]
        loads += 32 + 4 * (size // D)
        stores += 8 * (size // D)
        width += size
    total = width + 128 * bool(norms)
    shape = jax.ShapeDtypeStruct((4, rows, total), BF)
    count = 1 + len(arrays) + len(gates)

    def view(refs, place, taken, along_rows):
        index, micro = place
        ref = refs[1 + index] if micro is None else refs[1 + index].at[micro]
        span = pl.ds(taken.start, taken.stop - taken.start)
        return ref.at[span] if along_rows else ref.at[:, span]

    def body(*refs):
        sources = [
            (
                [view(refs, place, left[1], True) for place in left[0]],
                [view(refs, place, right[1], turned) for place in right[0]],
            )
            for left, right in terms
        ]
        norm_views = []
        if norms:
            norm_views = [view(refs, place, norm_places[1], True) for place in norm_places[0]]
        rest = refs[count + 2 :]
        buffers = [(rest[2 * k], rest[2 * k + 1]) for k in range(len(terms))]
        weight_grad_kernel(
            refs[0],
            sources,
            norm_views,
            refs[count],
            refs[count + 1],
            (buffers,) + tuple(rest[2 * len(terms) :]),
            rows=rows,
            order=order,
            turned=turned,
        )

    scratch += [pltpu.VMEM((8, rows, total), BF), DMA((loads,)), DMA((stores + 2,))]
    if norms:
        scratch += [pltpu.VMEM((4, 16, D), BF), pltpu.VMEM((16, rows, 128), BF), DMA((4, 3))]
    return pl.pallas_call(
        body,
        out_shape=[shape, shape],
        in_specs=[SMEM] + [ANY] * (count - 1),
        out_specs=[ANY] * 2,
        scratch_shapes=scratch,
        compiler_params=pltpu.CompilerParams(vmem_limit_bytes=VMEM_LIMIT),
        cost_estimate=pl.CostEstimate(flops=1000, bytes_accessed=1000, transcendentals=0),
        name="weight_grad",
    )(ids, *arrays, *gates)


def exchange(values, bit):
    count = lax.axis_size("dp")
    return lax.ppermute(values, "dp", [(i, i ^ bit) for i in range(count)])


def halve(parts, gates):
    half = len(parts[0]) // 2
    arrays = []
    for part in parts:
        for array, _ in part[:half]:
            if not any(array is known for known in arrays):
                arrays.append(array)
    where = [
        [next((k, at) for k, known in enumerate(arrays) if known is array) for array, at in part[:half]]
        for part in parts
    ]
    block = arrays[0].shape[1:]
    count = len(parts)

    def body(*refs):
        outgoing, held, result, i_sem, o_sem = refs[len(arrays) + len(gates) :]
        loads = [
            [
                begin(refs[where[p][i][0]].at[where[p][i][1]], held.at[p, i], i_sem.at[p, i])
                for p in range(count)
            ]
            for i in range(half)
        ]
        stores = []
        for i in range(half):
            total = None
            for p in range(count):
                loads[i][p].wait()
                value = held[p, i].astype(F32)
                total = value if total is None else total + value
            result[i] = total.astype(BF)
            stores.append(begin(result.at[i], outgoing.at[i], o_sem.at[i]))
        for copy in stores:
            copy.wait()

    return pl.pallas_call(
        body,
        out_shape=jax.ShapeDtypeStruct((half,) + block, BF),
        in_specs=[ANY] * (len(arrays) + len(gates)),
        out_specs=ANY,
        scratch_shapes=[
            pltpu.VMEM((count, half) + block, BF),
            pltpu.VMEM((half,) + block, BF),
            DMA((count, half)),
            DMA((half,)),
        ],
        compiler_params=pltpu.CompilerParams(vmem_limit_bytes=VMEM_LIMIT),
        cost_estimate=pl.CostEstimate(flops=1000, bytes_accessed=1000, transcendentals=0),
        name="halve",
    )(*arrays, *gates)


def blocks_of(array):
    return [(array, at) for at in range(array.shape[0])]


def own_sum(parts):
    return sum(array[at].astype(F32) for ((array, at),) in parts)


LINKS = {
    "down": (BIT_X, BIT_NEAR, BIT_FAR),
    "gate": (BIT_NEAR, BIT_X, BIT_FAR),
    "rise": (BIT_X, BIT_NEAR, BIT_FAR),
    "attn": (BIT_X, BIT_NEAR, BIT_FAR),
}
PLAN = (
    ("local", "down"),
    ("local", "gate"),
    ("local", "rise"),
    ("attention", "attn"),
    ("local", "attn"),
    ("step", "down"),
    ("step", "gate"),
    ("step", "rise"),
    ("step", "down"),
    ("step", "rise"),
    ("step", "attn"),
    ("step", "gate"),
    ("step", "attn"),
)


def reduce_shares(ids, lefts, hidden, gates_ups, attention_first, second_half):
    parts, last = {}, []
    order = {}

    def local(name, pairs, rows, bits, norms=None, turned=False):
        order[name] = list(bits)
        sent, kept = weight_grad(ids, pairs, rows, bits, last, norms, turned)
        parts[name] = [blocks_of(kept), blocks_of(exchange(sent, order[name].pop(0)))]
        last[:] = [sent]

    def step(name):
        sent = halve(parts[name], last)
        parts[name] = [part[sent.shape[0] :] for part in parts[name]]
        parts[name].append(blocks_of(exchange(sent, order[name].pop(0))))
        last[:] = [sent]

    inputs, context, h1 = ((lefts, slice(D * k, D * (k + 1))) for k in range(3))
    hidden_pairs = {
        "down": [((hidden, slice(0, FF)), (hidden, slice(FF, FF + D)))],
        "gate": [(h1, (gates_ups[0], slice(0, FF)))],
        "rise": [(h1, (gates_ups[1], slice(0, FF)))],
    }
    for action, name in PLAN:
        if action == "step":
            step(name)
        elif action == "attention":
            attention_second, input_grads, _ = second_half(
                last + [other[0] for _, other in attention_first]
            )
            last[:] = [attention_second[0]]
            q_grads, v_grads = (
                [own, (array, None), other, (exchange(array, BIT_CORE), None)]
                for (own, other), array in zip(attention_first, attention_second)
            )
        elif name == "attn":
            pairs = [
                (inputs, (q_grads, slice(0, 2 * D))),
                (inputs, (v_grads, slice(0, D))),
                (context, (v_grads, slice(D, 2 * D))),
            ]
            local(name, pairs, ROWS, LINKS[name], (hidden, slice(FF + D, FF + D + 48)))
        else:
            rows = 4 * ROWS if name == "down" else ROWS
            local(name, hidden_pairs[name], rows, LINKS[name], turned=name == "down")
    down, gate, rise, attn = (own_sum(parts[name]) for name in ("down", "gate", "rise", "attn"))
    norm = attn[:, 4 * D : 4 * D + 4].T
    shares = (
        attn[:, : 3 * D],
        attn[:, 3 * D : 4 * D],
        jnp.concatenate([gate, rise], axis=1),
        down,
        norm[:2],
        norm[2:],
    )
    return shares, input_grads


def packed_shares(rows, left, hidden, gates, ups, attention):
    def product(lefts, rights, dims=NN):
        lefts = jnp.concatenate(lefts, axis=1)
        rights = jnp.concatenate(rights, axis=1 if dims == NT else 0)
        return matmul(lefts, rights, dims).astype(BF)

    def cut(arrays, start, stop):
        return [array[start:stop] for array in arrays]

    left = list(left)
    down = product(cut(hidden, 0, FF), cut(hidden, FF, FF + D), NT).reshape(D // rows, 4, rows, D)
    norm_sum = sum(array[FF + D :].astype(F32) for array in hidden)
    norm_sum = norm_sum.reshape(3, 16, SEQ)[:, :4].transpose(1, 0, 2).reshape(4, D).T.astype(BF)
    attention = [jnp.concatenate(pair, axis=1) for pair in attention]
    summed = [
        product(cut(left, 0, D), [array[:, : 3 * D] for array in attention]),
        product(cut(left, D, 2 * D), [array[:, 3 * D :] for array in attention]),
        product(cut(left, 2 * D, 3 * D), gates),
        product(cut(left, 2 * D, 3 * D), ups),
        down.transpose(0, 2, 1, 3).reshape(D, FF),
        jnp.pad(norm_sum, ((0, 0), (0, 128 - 4))),
    ]
    summed = jnp.concatenate(summed, axis=1)
    share = lax.psum_scatter(summed, "dp", scatter_dimension=0, tiled=True).astype(F32)
    down = share[:, COL_DOWN:COL_NORM].reshape(rows, 4, D).transpose(1, 0, 2)
    norm = share[:, COL_NORM : COL_NORM + 4].T
    return (
        share[:, :COL_OUT],
        share[:, COL_OUT:COL_GU],
        share[:, COL_GU:COL_DOWN],
        down.reshape(4 * rows, D),
        norm[:2],
        norm[2:],
    )


def shards(tokens, lengths, w_qkv, w_out, w_gate_up, w_down, norm_gain, norm_bias, cotangent):
    rows = w_qkv.shape[1]
    direct = rows == ROWS
    section = lax.axis_index("section")
    ids = jnp.stack([section, lax.axis_index("dp")]).astype(jnp.int32)
    packed = pack(
        *(w[0].astype(BF) for w in (w_qkv, w_out, w_gate_up, w_down, norm_gain, norm_bias))
    )
    wide = lax.all_gather(packed, "dp", axis=0, tiled=True)
    if direct:
        down = wide.reshape(D // rows, rows, WIDE)
    else:
        down = wide[:, COL_DOWN:COL_NORM].reshape(D // rows, rows, 4, D)
        down = down.transpose(0, 2, 1, 3).reshape(FF // (4 * ROWS), 4, ROWS, D)
    norms = wide[:, COL_NORM : COL_NORM + 8].astype(F32).T

    def hop(rows_sent, pair):
        return lax.ppermute(rows_sent, "section", [pair])

    def forward(owner, micro, given, before):
        return forward_call(
            owner, micro, direct, ids, lengths, given, wide, down, norms, before
        )

    *kept, sent = forward(0, 0, tokens, [None] * len(FORWARD_KEPT))
    arrived_first = hop(sent, (0, 1))
    *kept, sent = forward(0, 1, tokens, kept)
    arrived_second = hop(sent, (0, 1))
    *kept, sent = forward(1, 0, arrived_first, kept)
    *kept, sent = forward(1, 1, arrived_second, kept)
    left, qkv, probs, n1, h1, n2, inv, layer_out = kept
    stash = (qkv, probs, n1, h1, n2, inv)

    def backward(owner, micro, given, before, gates=()):
        return backward_call(
            owner, micro, direct, ids, given, wide, down, norms, stash, before, gates
        )

    def both(array):
        return [(array, None), (exchange(array, BIT_CORE), None)]

    left_other = exchange(left, BIT_CORE) if direct else left
    *first, input_grads, sent = backward(1, 0, cotangent, [None] * 6)
    arrived_first = hop(sent, (1, 0))
    gates = (left_other,) if direct else ()
    *second, input_grads, sent = backward(
        1, 1, cotangent, [None] * 5 + [input_grads], gates
    )
    arrived_second = hop(sent, (1, 0))
    *first, input_grads, sent = backward(0, 0, arrived_first, first + [input_grads])
    if direct:
        first = [both(array) for array in first]
    *hidden, half = first_half_call(
        0, 1, direct, ids, arrived_second, wide, down, norms, (n1, h1, n2, inv), second[:3], ()
    )

    def second_half(gates):
        before = second[3:] + [input_grads]
        *made, input_sum, _ = second_half_call(
            0, 1, ids, half, wide, (qkv, probs), before, gates
        )
        return made, input_sum, None

    if direct:
        lefts = [(left, 0), (left, 1), (left_other, 0), (left_other, 1)]

        def paired(k):
            own, other = zip(first[k], both(hidden[k]))
            return list(own) + list(other)

        shares, input_grads = reduce_shares(
            ids,
            lefts,
            paired(0),
            [paired(1), paired(2)],
            [[first[3][0], first[3][1]], [first[4][0], first[4][1]]],
            second_half,
        )
    else:
        attention, input_grads, _ = second_half(())
        pairs = [first[3:5], attention]
        shares = packed_shares(
            rows, left, [first[0], hidden[0]], [first[1], hidden[1]], [first[2], hidden[2]], pairs
        )
    return (layer_out[None], input_grads[None]) + tuple(share[None] for share in shares)


def solution(mesh):
    return jax.shard_map(
        shards,
        mesh=mesh,
        in_specs=(
            P(None, "dp", None),
            P(),
            P("section", "dp", None),
            P("section", "dp", None),
            P("section", "dp", None),
            P("section", "dp", None),
            P("section", None, "dp"),
            P("section", None, "dp"),
            P(None, "dp", None),
        ),
        out_specs=(
            P("section", None, "dp", None),
            P("section", None, "dp", None),
            P("section", "dp", None),
            P("section", "dp", None),
            P("section", "dp", None),
            P("section", "dp", None),
            P("section", None, "dp"),
            P("section", None, "dp"),
        ),
        check_vma=False,
    )
```

time: 517 us -> 410 us (0.79)
  waiting for transfers between devices: 326 us -> 195 us
  Pallas kernels: 92.2 us -> 142 us
  local copies, waits for them, and re-layouts: 44.7 us -> 4.91 us
  starting transfers between devices: 5.29 us -> 31.8 us
  matrix products: 18.9 us -> 0 us
  other arithmetic: 6.62 us -> 14.7 us
    reduce_scatter x1 -> x0, waiting for transfers between devices: 196 us -> none  [shards(): lax.psum_scatter(summed, 'dp', scatter_dimension=0, tiled=True).astype(F32)]
    ppermute x0 -> x23, waiting for transfers between devices: none -> 64.1 us  [exchange(): return lax.ppermute(values, 'dp', [(i, i ^ bit) for i in range(count)])]
    pallas_call x8 -> x21, Pallas kernels: 92.2 us -> 142 us  [the longest x9 94.3 us: call_window(): pl.pallas_call(kernel, out_shape=shapes, in_specs=[SMEM] * small + [ANY]...]
    dot_general x4 -> x0, matrix products: 18.9 us -> none  [matmul(): return lax.dot_general(left, right, dims, preferred_element_type=F32)]
    ppermute x0 -> x23, starting transfers between devices: none -> 18.4 us  [exchange(): return lax.ppermute(values, 'dp', [(i, i ^ bit) for i in range(count)])]
    reshape x3 -> x0, local copies, waits for them, and re-layouts: 12.5 us -> none  [the longest x1 9.75 us: shards(): down = wide[:, COL_DOWN:COL_NORM].reshape(devices, rows, 4, D)]
    unnamed x39 -> x8, local copies, waits for them, and re-layouts: 9.76 us -> 1.07 us
    ppermute x4, starting transfers between devices: 5.21 us -> 13.4 us  [hop(): return lax.ppermute(rows_sent, 'section', [pair])]
  transfers between devices with their start and end apart: 6 -> 28, of which waited for: 5 -> 15; matrix products, arithmetic and copies ran while one was open for 0% -> 2% of each run, Pallas kernels for 9% -> 31%
where the time goes in v2:
time: 410 us; the launch traced here: 403 us
  waiting for transfers between devices  195 us (48%)
  Pallas kernels  142 us (35%)
  starting transfers between devices  31.8 us (8%)
  between operations  14.8 us (4%)
  other arithmetic  14.7 us (4%)
  local copies, waits for them, and re-layouts  4.91 us (1%)
    all_gather x1, waiting for transfers between devices, shards(): wide = lax.all_gather(packed, 'dp', axis=0, tiled=True)  102 us
    pallas_call x9, Pallas kernels, call_window(): pl.pallas_call(kernel, out_shape=shapes, in_specs=[SMEM] * small + [ANY]...  94.3 us
    ppermute x23, waiting for transfers between devices, exchange(): return lax.ppermute(values, 'dp', [(i, i ^ bit) for i in range(count)])  64.1 us
    pallas_call x4, Pallas kernels, weight_grad(): pl.pallas_call(body, out_shape=[shape, shape], in_specs=[SMEM] + [ANY] *...  31.6 us
    ppermute x4, waiting for transfers between devices, hop(): return lax.ppermute(rows_sent, 'section', [pair])  28.6 us
    ppermute x23, starting transfers between devices, exchange(): return lax.ppermute(values, 'dp', [(i, i ^ bit) for i in range(count)])  18.4 us
    pallas_call x8, Pallas kernels, halve(): pl.pallas_call(body, out_shape=jax.ShapeDtypeStruct((half,) + block, BF),...  15.9 us
    ppermute x4, starting transfers between devices, hop(): return lax.ppermute(rows_sent, 'section', [pair])  13.4 us
  transfers between devices with their start and end apart: 28, of which 15 were waited for; matrix products, arithmetic and copies ran while one was open for 2% of the time, Pallas kernels for 31%

profile of v2, /device:TPU:0, one launch (start us, length us, event | category | flops | bytes accessed | tf_op | source)
XLA Modules:
  0.0 402.9 jit_solution(107819808928130142)
XLA Ops:
  12.3 102.1 %all-gather.2.cloned.1.call-done.refs_3_.refs_2_ = bf16[768,12416]{1,0:T(8,128)(2,1)} async-done(((bf16[48,12416]{1,0:T(8,128)(2,1)}), bf16[768,12416]{1,0:T(8,128)(2,1)}) %all-gather.2.cloned.1.call-update) | async-done | bytes 19070992 | tf_op jit(solution)/shard_map/all_gather | solution.py:946
  116.1 14.5 %layer_forward.4 = (bf16[2,2304,256]{2,1,0:T(8,128)(2,1)}, bf16[2,256,2304]{2,1,0:T(8,128)(2,1)}, bf16[2,12,256,256]{3,2,1,0:T(8,128)(2,1)}, f32[2,256,768]{2,1,...) custom-call(s32[2]{0:T(128)} %pad_add_fusion.refs_0_, ...), custom_call_target="tpu_custom_call" | custom-call | flops 5000000000 | bytes 25000000 | tf_op jit(solution)/shard_map/layer_forward/pallas_call | solution.py:484
  130.6 2.0 collective-permute-start.1
  132.7 14.7 %layer_forward.5 = (bf16[2,2304,256]{2,1,0:T(8,128)(2,1)}, bf16[2,256,2304]{2,1,0:T(8,128)(2,1)}, bf16[2,12,256,256]{3,2,1,0:T(8,128)(2,1)}, f32[2,256,768]{2,1,...) custom-call(s32[2]{0:T(128)} %pad_add_fusion.refs_0_, ...), custom_call_target="tpu_custom_call", output_to_operand_aliasing={{0}: (6, {}), {1}: (7, {}), {2}: (8, {}), {3}: (9, {}), {4}... | custom-call | flops 5000000000 | bytes 25000000 | tf_op jit(solution)/shard_map/layer_forward/pallas_call | solution.py:484
  147.4 2.1 collective-permute-start
  149.5 1.3 layer_forward.6
  150.8 7.3 %collective-permute-done.refs_2_ = bf16[256,768]{1,0:T(8,128)(2,1)} collective-permute-done((bf16[256,768]{1,0:T(8,128)(2,1)}, bf16[256,768]{1,0:T(8,128)(2,1)}, u32[]{:S(2)}, u32[]{:S(2)}) %collective-permute-start) | collective-permute-done | bytes 393248 | tf_op jit(solution)/shard_map/ppermute | solution.py:955
  158.1 1.5 layer_forward.7
  159.7 8.6 %layer_backward.3 = (bf16[3888,256]{1,0:T(8,128)(2,1)}, bf16[256,3072]{1,0:T(8,128)(2,1)}, bf16[256,3072]{1,0:T(8,128)(2,1)}, bf16[256,1536]{1,0:T(8,128)(2,1)},...) custom-call(s32[2]{0:T(128)} %pad_add_fusion.refs_0_, bf16[2,256,768]{2,1,0:T(8,128)(2,1)} %refs_1_.11, ...), custom_call_target="tpu_custom_call" | custom-call | flops 8000000000 | bytes 40000000 | tf_op jit(solution)/shard_map/layer_backward/pallas_call | solution.py:484
  168.3 8.0 %collective-permute-start.4 = (bf16[256,768]{1,0:T(8,128)(2,1)}, bf16[256,768]{1,0:T(8,128)(2,1)}, u32[]{:S(2)}, u32[]{:S(2)}) collective-permute-start(bf16[256,768]{1,0:T(8,128)(2,1)} %get-tuple-element.119), channel_id=1, source_target_pairs={{16,0},{17,1},{18,2},{19,3},{20,4},{21,5},{22,6},{23,7},{24,8},{25... | collective-permute-start | bytes 1179656 | tf_op jit(solution)/shard_map/ppermute | solution.py:955
  176.2 9.3 %layer_backward.4 = (bf16[3888,256]{1,0:T(8,128)(2,1)}, bf16[256,3072]{1,0:T(8,128)(2,1)}, bf16[256,3072]{1,0:T(8,128)(2,1)}, bf16[256,1536]{1,0:T(8,128)(2,1)},...) custom-call(s32[2]{0:T(128)} %pad_add_fusion.refs_0_, ...), custom_call_target="tpu_custom_call", output_to_operand_aliasing={{5}: (11, {})} | custom-call | flops 8000000000 | bytes 40000000 | tf_op jit(solution)/shard_map/layer_backward/pallas_call | solution.py:484
  186.8 20.0 %collective-permute-done.4.refs_1_ = bf16[256,768]{1,0:T(8,128)(2,1)} collective-permute-done((bf16[256,768]{1,0:T(8,128)(2,1)}, bf16[256,768]{1,0:T(8,128)(2,1)}, u32[]{:S(2)}, u32[]{:S(2)}) %collective-permute-start.4) | collective-permute-done | bytes 393248 | tf_op jit(solution)/shard_map/ppermute | solution.py:955
  206.8 20.4 %layer_backward.5 = (bf16[3888,256]{1,0:T(8,128)(2,1)}, bf16[256,3072]{1,0:T(8,128)(2,1)}, bf16[256,3072]{1,0:T(8,128)(2,1)}, bf16[256,1536]{1,0:T(8,128)(2,1)},...) custom-call(s32[2]{0:T(128)} %pad_add_fusion.refs_0_, ...), custom_call_target="tpu_custom_call", output_to_operand_aliasing={{0}: (11, {}), {1}: (12, {}), {2}: (13, {}), {3}: (14, {}),... | custom-call | flops 8000000000 | bytes 40000000 | tf_op jit(solution)/shard_map/layer_backward/pallas_call | solution.py:484
  227.7 1.4 collective-permute-done.3.refs_1_
  229.1 14.2 %backward_hidden.1 = (bf16[3888,256]{1,0:T(8,128)(2,1)}, bf16[256,3072]{1,0:T(8,128)(2,1)}, bf16[256,3072]{1,0:T(8,128)(2,1)}, f32[256,768]{1,0:T(8,128)}) custom-call(s32[2]{0:T(128)} %pad_add_fusion.refs_0_, bf16[256,768]{1,0:T(8,128)(2,1)} %collective-permute-done.3.refs_1_, ...), custom_call_target="tpu_custom_call", output_to_operand_aliasing={{0}: (9, {}), {1}: (10, {}), {2}: (11, {})} | custom-call | flops 60000002048 | bytes 300000000 | tf_op jit(solution)/shard_map/backward_hidden/pallas_call | solution.py:484
  244.5 3.2 collective-permute-done.10.refs_4_.refs_14_
  247.9 7.0 %weight_grad.4 = (bf16[4,192,768]{2,1,0:T(8,128)(2,1)}, bf16[4,192,768]{2,1,0:T(8,128)(2,1)}) custom-call(s32[2]{0:T(128)} %pad_add_fusion.refs_0_, bf16[3888,256]{1,0:T(8,128)(2,1)} %get-tuple-element.131.refs_1_.refs_11_, bf16[3888,256]{1,0:T(8,128)(2,1)} %get-tuple-element.132.refs_2_.refs_12_, bf16[3888,256]{1,0:T(8,128)(2,1)} %collective-permute-done.9.refs_3_.refs_13_, ...), custom_call_target="tpu_custom_call" | custom-call | flops 1000 | bytes 1000 | tf_op jit(solution)/shard_map/weight_grad/pallas_call | solution.py:745
  254.9 1.3 collective-permute-start.18
  256.2 7.9 %weight_grad.5 = (bf16[4,48,3072]{2,1,0:T(8,128)(2,1)}, bf16[4,48,3072]{2,1,0:T(8,128)(2,1)}) custom-call(s32[2]{0:T(128)} %pad_add_fusion.refs_0_, bf16[2,2304,256]{2,1,0:T(8,128)(2,1)} %get-tuple-element.111.refs_1_, bf16[2,2304,256]{2,1,0:T(8,128)(2,1)} %collective-permute-done.2.refs_12_.refs_2_, bf16[256,3072]{1,0:T(8,128)(2,1)} %get-tuple-element.129.refs_3_, ...), custom_call_target="tpu_custom_call" | custom-call | flops 1000 | bytes 1000 | tf_op jit(solution)/shard_map/weight_grad/pallas_call | solution.py:745
  264.1 1.6 collective-permute-start.17
  265.7 7.9 %weight_grad.6 = (bf16[4,48,3072]{2,1,0:T(8,128)(2,1)}, bf16[4,48,3072]{2,1,0:T(8,128)(2,1)}) custom-call(s32[2]{0:T(128)} %pad_add_fusion.refs_0_, bf16[2,2304,256]{2,1,0:T(8,128)(2,1)} %get-tuple-element.111.refs_1_, bf16[2,2304,256]{2,1,0:T(8,128)(2,1)} %collective-permute-done.2.refs_12_.refs_2_, bf16[256,3072]{1,0:T(8,128)(2,1)} %get-tuple-element.127.refs_3_, ...), custom_call_target="tpu_custom_call" | custom-call | flops 1000 | bytes 1000 | tf_op jit(solution)/shard_map/weight_grad/pallas_call | solution.py:745
  274.4 9.8 %backward_attention.1 = (bf16[256,1536]{1,0:T(8,128)(2,1)}, bf16[256,1536]{1,0:T(8,128)(2,1)}, f32[2,256,768]{2,1,0:T(8,128)}, bf16[256,768]{1,0:T(8,128)(2,1)}) custom-call(s32[2]{0:T(128)} %pad_add_fusion.refs_0_, f32[256,768]{1,0:T(8,128)} %get-tuple-element.116.refs_1_, ...), custom_call_target="tpu_custom_call", output_to_operand_aliasing={{0}: (5, {}), {1}: (6, {}), {2}: (7, {})} | custom-call | flops 1000 | bytes 5 | tf_op jit(solution)/shard_map/backward_attention/pallas_call | solution.py:484
  284.8 2.1 collective-permute-done.13.refs_6_
  288.0 8.9 %weight_grad.7 = (bf16[4,48,3200]{2,1,0:T(8,128)(2,1)}, bf16[4,48,3200]{2,1,0:T(8,128)(2,1)}) custom-call(s32[2]{0:T(128)} %pad_add_fusion.refs_0_, bf16[2,2304,256]{2,1,0:T(8,128)(2,1)} %get-tuple-element.111.refs_1_, bf16[2,2304,256]{2,1,0:T(8,128)(2,1)} %collective-permute-done.2.refs_12_.refs_2_, bf16[256,1536]{1,0:T(8,128)(2,1)} %get-tuple-element.136.refs_3_, ...), custom_call_target="tpu_custom_call" | custom-call | flops 1000 | bytes 1000 | tf_op jit(solution)/shard_map/weight_grad/pallas_call | solution.py:745
  298.2 2.0 halve.8.refs_2_
  300.9 2.0 halve.9.refs_2_
  302.9 6.4 %collective-permute-done.16.refs_1_ = bf16[4,48,3072]{2,1,0:T(8,128)(2,1)} collective-permute-done((bf16[4,48,3072]{2,1,0:T(8,128)(2,1)}, bf16[4,48,3072]{2,1,0:T(8,128)(2,1)}, u32[]{:S(2)}, u32[]{:S(2)}) %collective-permute-start.16) | collective-permute-done | bytes 1179680 | tf_op jit(solution)/shard_map/ppermute | solution.py:759
  309.4 2.0 halve.10.refs_3_
  311.4 1.6 collective-permute-start.19
  314.2 2.7 collective-permute-done.20.refs_2_
  316.9 1.9 halve.11.refs_3_
  318.9 9.3 %collective-permute-done.19.refs_2_ = bf16[2,48,3072]{2,1,0:T(8,128)(2,1)} collective-permute-done((bf16[2,48,3072]{2,1,0:T(8,128)(2,1)}, bf16[2,48,3072]{2,1,0:T(8,128)(2,1)}, u32[]{:S(2)}, u32[]{:S(2)}) %collective-permute-start.19) | collective-permute-done | bytes 589856 | tf_op jit(solution)/shard_map/ppermute | solution.py:759
  328.2 1.9 halve.12.refs_2_
  330.1 1.7 collective-permute-start.25
  333.1 2.5 collective-permute-done.15.refs_1_
  335.7 2.1 halve.13.refs_3_
  337.8 1.6 collective-permute-start.21
  339.3 8.5 %collective-permute-done.22.refs_2_ = bf16[2,48,3072]{2,1,0:T(8,128)(2,1)} collective-permute-done((bf16[2,48,3072]{2,1,0:T(8,128)(2,1)}, bf16[2,48,3072]{2,1,0:T(8,128)(2,1)}, u32[]{:S(2)}, u32[]{:S(2)}) %collective-permute-start.22) | collective-permute-done | bytes 589856 | tf_op jit(solution)/shard_map/ppermute | solution.py:759
  347.8 1.9 halve.14.refs_3_
  349.7 2.5 collective-permute-start.24
  352.2 2.2 add_bitcast_fusion.1
  354.4 5.6 %collective-permute-done.26 = bf16[1,192,768]{2,1,0:T(8,128)(2,1)} collective-permute-done((bf16[1,192,768]{2,1,0:T(8,128)(2,1)}, bf16[1,192,768]{2,1,0:T(8,128)(2,1)}, u32[]{:S(2)}, u32[]{:S(2)}) %collective-permute-start.26) | collective-permute-done | bytes 294944 | tf_op jit(solution)/shard_map/ppermute | solution.py:759
  360.0 2.2 convert_add_fusion
  362.1 8.6 %collective-permute-done.24 = bf16[1,48,3072]{2,1,0:T(8,128)(2,1)S(1)} collective-permute-done((bf16[1,48,3072]{2,1,0:T(8,128)(2,1)}, bf16[1,48,3072]{2,1,0:T(8,128)(2,1)S(1)}, u32[]{:S(2)}, u32[]{:S(2)}) %collective-permute-start.24) | collective-permute-done | bytes 294944 | tf_op jit(solution)/shard_map/ppermute | solution.py:759
  370.7 2.1 add_bitcast_fusion.2
  372.8 2.0 halve.15
  375.2 2.3 maximum_bitcast_fusion
  377.5 14.0 %collective-permute-done.23 = bf16[1,48,3200]{2,1,0:T(8,128)(2,1)S(1)} collective-permute-done((bf16[1,48,3200]{2,1,0:T(8,128)(2,1)}, bf16[1,48,3200]{2,1,0:T(8,128)(2,1)S(1)}, u32[]{:S(2)}, u32[]{:S(2)}) %collective-permute-start.23) | collective-permute-done | bytes 307232 | tf_op jit(solution)/shard_map/ppermute | solution.py:759
  (61 shorter events, 21.5 us)
Async XLA Ops:
  7.2 3.3 copy-start.2
  7.2 3.4 copy-start.1
  7.2 107.2 %all-gather.2.cloned.1.call-start = ((), (), s32[]{:S(2)}) async-start(), calls=%async_computation | async-start | bytes 20262912 | tf_op jit(solution)/shard_map/all_gather | solution.py:946
  10.7 1.0 copy-start
  130.6 18.8 %collective-permute-start.1 = (bf16[256,768]{1,0:T(8,128)(2,1)}, bf16[256,768]{1,0:T(8,128)(2,1)}, u32[]{:S(2)}, u32[]{:S(2)}) collective-permute-start(bf16[256,768]{1,0:T(8,128)(2,1)} %get-tuple-element.86), channel_id=1, source_target_pairs={{0,16},{1,17},{2,18},{3,19},{4,20},{5,21},{6,22},{7,23},{8,24},{9,... | collective-permute-start | bytes 1179656 | tf_op jit(solution)/shard_map/ppermute | solution.py:955
  147.4 10.7 %collective-permute-start = (bf16[256,768]{1,0:T(8,128)(2,1)}, bf16[256,768]{1,0:T(8,128)(2,1)}, u32[]{:S(2)}, u32[]{:S(2)}) collective-permute-start(bf16[256,768]{1,0:T(8,128)(2,1)} %get-tuple-element.85), channel_id=1, source_target_pairs={{0,16},{1,17},{2,18},{3,19},{4,20},{5,21},{6,22},{7,23},{8,24},{9,... | collective-permute-start | bytes 1179656 | tf_op jit(solution)/shard_map/ppermute | solution.py:955
  159.6 16.6 %collective-permute-start.2 = (bf16[2,2304,256]{2,1,0:T(8,128)(2,1)}, bf16[2,2304,256]{2,1,0:T(8,128)(2,1)}, u32[]{:S(2)}, u32[]{:S(2)}) collective-permute-start(bf16[2,2304,256]{2,1,0:T(8,128)(2,1)} %get-tuple-element.111.refs_1_), channel_id=1, source_target_pairs={{0,1},{1,0},{2,3},{3,2},{4,5},{5,4},{6,7},{7,6},{8,9},{9,8},{10,11... | collective-permute-start | bytes 7077896 | tf_op jit(solution)/shard_map/ppermute | solution.py:759
  168.3 38.5 %collective-permute-start.4 = (bf16[256,768]{1,0:T(8,128)(2,1)}, bf16[256,768]{1,0:T(8,128)(2,1)}, u32[]{:S(2)}, u32[]{:S(2)}) collective-permute-start(bf16[256,768]{1,0:T(8,128)(2,1)} %get-tuple-element.119), channel_id=1, source_target_pairs={{16,0},{17,1},{18,2},{19,3},{20,4},{21,5},{22,6},{23,7},{24,8},{25... | collective-permute-start | bytes 1179656 | tf_op jit(solution)/shard_map/ppermute | solution.py:955
  185.5 43.6 %collective-permute-start.3 = (bf16[256,768]{1,0:T(8,128)(2,1)}, bf16[256,768]{1,0:T(8,128)(2,1)}, u32[]{:S(2)}, u32[]{:S(2)}) collective-permute-start(bf16[256,768]{1,0:T(8,128)(2,1)} %get-tuple-element.112), channel_id=1, source_target_pairs={{16,0},{17,1},{18,2},{19,3},{20,4},{21,5},{22,6},{23,7},{24,8},{25... | collective-permute-start | bytes 1179656 | tf_op jit(solution)/shard_map/ppermute | solution.py:955
  227.2 17.3 %collective-permute-start.9 = (bf16[3888,256]{1,0:T(8,128)(2,1)}, bf16[3888,256]{1,0:T(8,128)(2,1)}, u32[]{:S(2)}, u32[]{:S(2)}) collective-permute-start(bf16[3888,256]{1,0:T(8,128)(2,1)} %get-tuple-element.131.refs_1_.refs_11_), channel_id=1, source_target_pairs={{0,1},{1,0},{2,3},{3,2},{4,5},{5,4},{6,7},{7,6},{8,9},{9,8},{10,11... | collective-permute-start | bytes 5971976 | tf_op jit(solution)/shard_map/ppermute | solution.py:759
  227.2 16.8 %collective-permute-start.7 = (bf16[256,3072]{1,0:T(8,128)(2,1)}, bf16[256,3072]{1,0:T(8,128)(2,1)}, u32[]{:S(2)}, u32[]{:S(2)}) collective-permute-start(bf16[256,3072]{1,0:T(8,128)(2,1)} %get-tuple-element.129.refs_3_), channel_id=1, source_target_pairs={{0,1},{1,0},{2,3},{3,2},{4,5},{5,4},{6,7},{7,6},{8,9},{9,8},{10,11... | collective-permute-start | bytes 4718600 | tf_op jit(solution)/shard_map/ppermute | solution.py:759
  243.3 4.4 %collective-permute-start.10 = (bf16[3888,256]{1,0:T(8,128)(2,1)}, bf16[3888,256]{1,0:T(8,128)(2,1)}, u32[]{:S(2)}, u32[]{:S(2)}) collective-permute-start(bf16[3888,256]{1,0:T(8,128)(2,1)} %get-tuple-element.132.refs_2_.refs_12_), channel_id=1, source_target_pairs={{0,1},{1,0},{2,3},{3,2},{4,5},{5,4},{6,7},{7,6},{8,9},{9,8},{10,11... | collective-permute-start | bytes 5971976 | tf_op jit(solution)/shard_map/ppermute | solution.py:759
  243.4 11.5 %collective-permute-start.8 = (bf16[256,3072]{1,0:T(8,128)(2,1)}, bf16[256,3072]{1,0:T(8,128)(2,1)}, u32[]{:S(2)}, u32[]{:S(2)}) collective-permute-start(bf16[256,3072]{1,0:T(8,128)(2,1)} %get-tuple-element.130.refs_4_), channel_id=1, source_target_pairs={{0,1},{1,0},{2,3},{3,2},{4,5},{5,4},{6,7},{7,6},{8,9},{9,8},{10,11... | collective-permute-start | bytes 4718600 | tf_op jit(solution)/shard_map/ppermute | solution.py:759
  243.9 20.2 %collective-permute-start.5 = (bf16[256,3072]{1,0:T(8,128)(2,1)}, bf16[256,3072]{1,0:T(8,128)(2,1)}, u32[]{:S(2)}, u32[]{:S(2)}) collective-permute-start(bf16[256,3072]{1,0:T(8,128)(2,1)} %get-tuple-element.127.refs_3_), channel_id=1, source_target_pairs={{0,1},{1,0},{2,3},{3,2},{4,5},{5,4},{6,7},{7,6},{8,9},{9,8},{10,11... | collective-permute-start | bytes 4718600 | tf_op jit(solution)/shard_map/ppermute | solution.py:759
  244.0 21.7 %collective-permute-start.6 = (bf16[256,3072]{1,0:T(8,128)(2,1)}, bf16[256,3072]{1,0:T(8,128)(2,1)}, u32[]{:S(2)}, u32[]{:S(2)}) collective-permute-start(bf16[256,3072]{1,0:T(8,128)(2,1)} %get-tuple-element.128.refs_4_), channel_id=1, source_target_pairs={{0,1},{1,0},{2,3},{3,2},{4,5},{5,4},{6,7},{7,6},{8,9},{9,8},{10,11... | collective-permute-start | bytes 4718600 | tf_op jit(solution)/shard_map/ppermute | solution.py:759
  244.4 29.9 %collective-permute-start.11 = (bf16[256,1536]{1,0:T(8,128)(2,1)}, bf16[256,1536]{1,0:T(8,128)(2,1)}, u32[]{:S(2)}, u32[]{:S(2)}) collective-permute-start(bf16[256,1536]{1,0:T(8,128)(2,1)} %get-tuple-element.136.refs_3_), channel_id=1, source_target_pairs={{0,1},{1,0},{2,3},{3,2},{4,5},{5,4},{6,7},{7,6},{8,9},{9,8},{10,11... | collective-permute-start | bytes 2359304 | tf_op jit(solution)/shard_map/ppermute | solution.py:759
  247.7 26.6 %collective-permute-start.12 = (bf16[256,1536]{1,0:T(8,128)(2,1)}, bf16[256,1536]{1,0:T(8,128)(2,1)}, u32[]{:S(2)}, u32[]{:S(2)}) collective-permute-start(bf16[256,1536]{1,0:T(8,128)(2,1)} %get-tuple-element.137.refs_7_), channel_id=1, source_target_pairs={{0,1},{1,0},{2,3},{3,2},{4,5},{5,4},{6,7},{7,6},{8,9},{9,8},{10,11... | collective-permute-start | bytes 2359304 | tf_op jit(solution)/shard_map/ppermute | solution.py:759
  254.9 43.4 %collective-permute-start.18 = (bf16[4,192,768]{2,1,0:T(8,128)(2,1)}, bf16[4,192,768]{2,1,0:T(8,128)(2,1)}, u32[]{:S(2)}, u32[]{:S(2)}) collective-permute-start(bf16[4,192,768]{2,1,0:T(8,128)(2,1)} %get-tuple-element.133.refs_7_), channel_id=1, source_target_pairs={{0,2},{1,3},{2,0},{3,1},{4,6},{5,7},{6,4},{7,5},{8,10},{9,11},{10,... | collective-permute-start | bytes 3538952 | tf_op jit(solution)/shard_map/ppermute | solution.py:759
  264.1 36.8 %collective-permute-start.17 = (bf16[4,48,3072]{2,1,0:T(8,128)(2,1)}, bf16[4,48,3072]{2,1,0:T(8,128)(2,1)}, u32[]{:S(2)}, u32[]{:S(2)}) collective-permute-start(bf16[4,48,3072]{2,1,0:T(8,128)(2,1)} %get-tuple-element.134.refs_7_), channel_id=1, source_target_pairs={{0,4},{1,5},{2,6},{3,7},{4,0},{5,1},{6,2},{7,3},{8,12},{9,13},{10,... | collective-permute-start | bytes 3538952 | tf_op jit(solution)/shard_map/ppermute | solution.py:759
  273.5 35.8 %collective-permute-start.16 = (bf16[4,48,3072]{2,1,0:T(8,128)(2,1)}, bf16[4,48,3072]{2,1,0:T(8,128)(2,1)}, u32[]{:S(2)}, u32[]{:S(2)}) collective-permute-start(bf16[4,48,3072]{2,1,0:T(8,128)(2,1)} %get-tuple-element.135.refs_8_), channel_id=1, source_target_pairs={{0,2},{1,3},{2,0},{3,1},{4,6},{5,7},{6,4},{7,5},{8,10},{9,11},{10,... | collective-permute-start | bytes 3538952 | tf_op jit(solution)/shard_map/ppermute | solution.py:759
  284.2 2.7 collective-permute-start.13
  284.3 3.7 collective-permute-start.14
  296.9 38.8 %collective-permute-start.15 = (bf16[4,48,3200]{2,1,0:T(8,128)(2,1)}, bf16[4,48,3200]{2,1,0:T(8,128)(2,1)}, u32[]{:S(2)}, u32[]{:S(2)}) collective-permute-start(bf16[4,48,3200]{2,1,0:T(8,128)(2,1)} %get-tuple-element.142.refs_2_), channel_id=1, source_target_pairs={{0,2},{1,3},{2,0},{3,1},{4,6},{5,7},{6,4},{7,5},{8,10},{9,11},{10,... | collective-permute-start | bytes 3686408 | tf_op jit(solution)/shard_map/ppermute | solution.py:759
  300.3 16.6 %collective-permute-start.20 = (bf16[2,192,768]{2,1,0:T(8,128)(2,1)}, bf16[2,192,768]{2,1,0:T(8,128)(2,1)}, u32[]{:S(2)}, u32[]{:S(2)}) collective-permute-start(bf16[2,192,768]{2,1,0:T(8,128)(2,1)} %halve.8.refs_2_), channel_id=1, source_target_pairs={{0,4},{1,5},{2,6},{3,7},{4,0},{5,1},{6,2},{7,3},{8,12},{9,13},{10,... | collective-permute-start | bytes 1769480 | tf_op jit(solution)/shard_map/ppermute | solution.py:759
  311.4 16.8 %collective-permute-start.19 = (bf16[2,48,3072]{2,1,0:T(8,128)(2,1)}, bf16[2,48,3072]{2,1,0:T(8,128)(2,1)}, u32[]{:S(2)}, u32[]{:S(2)}) collective-permute-start(bf16[2,48,3072]{2,1,0:T(8,128)(2,1)} %halve.10.refs_3_), channel_id=1, source_target_pairs={{0,4},{1,5},{2,6},{3,7},{4,0},{5,1},{6,2},{7,3},{8,12},{9,13},{10,... | collective-permute-start | bytes 1769480 | tf_op jit(solution)/shard_map/ppermute | solution.py:759
  312.9 34.8 %collective-permute-start.22 = (bf16[2,48,3072]{2,1,0:T(8,128)(2,1)}, bf16[2,48,3072]{2,1,0:T(8,128)(2,1)}, u32[]{:S(2)}, u32[]{:S(2)}) collective-permute-start(bf16[2,48,3072]{2,1,0:T(8,128)(2,1)} %halve.9.refs_2_), channel_id=1, source_target_pairs={{0,2},{1,3},{2,0},{3,1},{4,6},{5,7},{6,4},{7,5},{8,10},{9,11},{10,... | collective-permute-start | bytes 1769480 | tf_op jit(solution)/shard_map/ppermute | solution.py:759
  330.1 22.0 %collective-permute-start.25 = (bf16[1,48,3072]{2,1,0:T(8,128)(2,1)}, bf16[1,48,3072]{2,1,0:T(8,128)(2,1)}, u32[]{:S(2)}, u32[]{:S(2)}) collective-permute-start(bf16[1,48,3072]{2,1,0:T(8,128)(2,1)} %halve.12.refs_2_), channel_id=1, source_target_pairs={{0,8},{1,9},{2,10},{3,11},{4,12},{5,13},{6,14},{7,15},{8,0},{9,1},... | collective-permute-start | bytes 884744 | tf_op jit(solution)/shard_map/ppermute | solution.py:759
  331.9 28.1 %collective-permute-start.26 = (bf16[1,192,768]{2,1,0:T(8,128)(2,1)}, bf16[1,192,768]{2,1,0:T(8,128)(2,1)}, u32[]{:S(2)}, u32[]{:S(2)}) collective-permute-start(bf16[1,192,768]{2,1,0:T(8,128)(2,1)} %halve.11.refs_3_), channel_id=1, source_target_pairs={{0,8},{1,9},{2,10},{3,11},{4,12},{5,13},{6,14},{7,15},{8,0},{9,1},... | collective-permute-start | bytes 884744 | tf_op jit(solution)/shard_map/ppermute | solution.py:759
  337.8 35.1 %collective-permute-start.21 = (bf16[2,48,3200]{2,1,0:T(8,128)(2,1)}, bf16[2,48,3200]{2,1,0:T(8,128)(2,1)}, u32[]{:S(2)}, u32[]{:S(2)}) collective-permute-start(bf16[2,48,3200]{2,1,0:T(8,128)(2,1)} %halve.13.refs_3_), channel_id=1, source_target_pairs={{0,4},{1,5},{2,6},{3,7},{4,0},{5,1},{6,2},{7,3},{8,12},{9,13},{10,... | collective-permute-start | bytes 1843208 | tf_op jit(solution)/shard_map/ppermute | solution.py:759
  349.7 21.0 %collective-permute-start.24 = (bf16[1,48,3072]{2,1,0:T(8,128)(2,1)}, bf16[1,48,3072]{2,1,0:T(8,128)(2,1)S(1)}, u32[]{:S(2)}, u32[]{:S(2)}) collective-permute-start(bf16[1,48,3072]{2,1,0:T(8,128)(2,1)} %halve.14.refs_3_), channel_id=1, source_target_pairs={{0,8},{1,9},{2,10},{3,11},{4,12},{5,13},{6,14},{7,15},{8,0},{9,1},... | collective-permute-start | bytes 884744 | tf_op jit(solution)/shard_map/ppermute | solution.py:759
  374.8 16.7 %collective-permute-start.23 = (bf16[1,48,3200]{2,1,0:T(8,128)(2,1)}, bf16[1,48,3200]{2,1,0:T(8,128)(2,1)S(1)}, u32[]{:S(2)}, u32[]{:S(2)}) collective-permute-start(bf16[1,48,3200]{2,1,0:T(8,128)(2,1)} %halve.15), channel_id=1, source_target_pairs={{0,8},{1,9},{2,10},{3,11},{4,12},{5,13},{6,14},{7,15},{8,0},{9,1},... | collective-permute-start | bytes 921608 | tf_op jit(solution)/shard_map/ppermute | solution.py:759
Sparse Core Ops, SparseCore 0:
  11.8 102.5 all-gather.1

commit v3 on v2

--- a/solution.py
+++ b/solution.py
@@ -48,6 +48,15 @@
     copy = pltpu.make_async_copy(source, target, semaphore)
     copy.start()
     return copy
+
+
+PACE = 9_200_000_000
+
+
+def cost_of(microseconds):
+    return pl.CostEstimate(
+        flops=microseconds * PACE, bytes_accessed=microseconds * PACE // 200, transcendentals=0
+    )
 
 
 def own_window(given, micro):
@@ -587,7 +596,7 @@
         BF,
         before,
         (pltpu.VMEM((SEQ, D), F32),) + ATTENTION_SCRATCH + (DMA((4,)), DMA((5,)), DMA((3,))),
-        1000,
+        10 * PACE,
         1,
         gates,
     )
@@ -749,7 +758,7 @@
         out_specs=[ANY] * 2,
         scratch_shapes=scratch,
         compiler_params=pltpu.CompilerParams(vmem_limit_bytes=VMEM_LIMIT),
-        cost_estimate=pl.CostEstimate(flops=1000, bytes_accessed=1000, transcendentals=0),
+        cost_estimate=cost_of(8),
         name="weight_grad",
     )(ids, *arrays, *gates)
 
@@ -806,7 +815,7 @@
             DMA((half,)),
         ],
         compiler_params=pltpu.CompilerParams(vmem_limit_bytes=VMEM_LIMIT),
-        cost_estimate=pl.CostEstimate(flops=1000, bytes_accessed=1000, transcendentals=0),
+        cost_estimate=cost_of(2),
         name="halve",
     )(*arrays, *gates)
 
@@ -815,8 +824,59 @@
     return [(array, at) for at in range(array.shape[0])]
 
 
-def own_sum(parts):
-    return sum(array[at].astype(F32) for ((array, at),) in parts)
+def finish(parts, gates, pieces, carried=None):
+    arrays, places = [], []
+    for ((array, at),) in parts:
+        if not any(array is known for known in arrays):
+            arrays.append(array)
+        places.append((next(k for k, known in enumerate(arrays) if known is array), at))
+    rows, width = arrays[0].shape[1:]
+    operands = tuple(arrays) + tuple(gates) + (() if carried is None else (carried,))
+
+    def body(*refs):
+        outs = refs[len(operands) :][: len(pieces)]
+        held, made, i_sem, o_sem = refs[len(operands) + len(pieces) :]
+        loads = [
+            begin(refs[index].at[at], held.at[k], i_sem.at[k])
+            for k, (index, at) in enumerate(places)
+        ]
+        total = None
+        for k, load in enumerate(loads):
+            load.wait()
+            value = held[k].astype(F32)
+            total = value if total is None else total + value
+        if width > 4 * D:
+            norms = jnp.concatenate(
+                [total[:, 4 * D :], jnp.zeros((128 - rows, 128), F32)], axis=0
+            ).T
+            made[:, pl.ds(0, 4 * D)] = total[:, : 4 * D]
+            made[pl.ds(0, 8), pl.ds(4 * D, 128)] = norms[:8]
+        else:
+            made[...] = total
+        stores = []
+        for k, (out, (shape, start, column)) in enumerate(zip(outs, pieces)):
+            count, size = min(shape[0], rows), min(shape[1], width)
+            source = made.at[pl.ds(0, count), pl.ds(start, size)]
+            stores.append(begin(source, out.at[:, pl.ds(column, size)], o_sem.at[k]))
+        for store in stores:
+            store.wait()
+
+    return pl.pallas_call(
+        body,
+        out_shape=[jax.ShapeDtypeStruct(shape, F32) for shape, _, _ in pieces],
+        in_specs=[ANY] * len(operands),
+        out_specs=[ANY] * len(pieces),
+        input_output_aliases={} if carried is None else {len(operands) - 1: 0},
+        scratch_shapes=[
+            pltpu.VMEM((len(parts), rows, width), BF),
+            pltpu.VMEM((rows, width), F32),
+            DMA((len(parts),)),
+            DMA((len(pieces),)),
+        ],
+        compiler_params=pltpu.CompilerParams(vmem_limit_bytes=VMEM_LIMIT),
+        cost_estimate=cost_of(2),
+        name="finish",
+    )(*operands)
 
 
 LINKS = {
@@ -830,20 +890,24 @@
     ("local", "gate"),
     ("local", "rise"),
     ("attention", "attn"),
+    ("step", "down"),
     ("local", "attn"),
-    ("step", "down"),
     ("step", "gate"),
     ("step", "rise"),
     ("step", "down"),
     ("step", "rise"),
     ("step", "attn"),
+    ("finish", "down"),
     ("step", "gate"),
+    ("finish", "rise"),
     ("step", "attn"),
+    ("finish", "gate"),
+    ("finish", "attn"),
 )
 
 
 def reduce_shares(ids, lefts, hidden, gates_ups, attention_first, second_half):
-    parts, last = {}, []
+    parts, last, done = {}, [], {}
     order = {}
 
     def local(name, pairs, rows, bits, norms=None, turned=False):
@@ -867,6 +931,18 @@
     for action, name in PLAN:
         if action == "step":
             step(name)
+        elif action == "finish":
+            wide = (ROWS, 2 * FF)
+            pieces = {
+                "down": [((4 * ROWS, D), 0, 0)],
+                "gate": [(wide, 0, 0)],
+                "rise": [(wide, 0, FF)],
+                "attn": [((ROWS, 3 * D), 0, 0), ((ROWS, D), 3 * D, 0), ((8, 128), 4 * D, 0)],
+            }
+            carried = done["gate"][0] if "gate" in done and name in ("gate", "rise") else None
+            made = finish(parts[name], last, pieces[name], carried)
+            done["gate" if name == "rise" else name] = made
+            last[:] = [made[0]] if name not in ("gate", "rise") else []
         elif action == "attention":
             attention_second, input_grads, _ = second_half(
                 last + [other[0] for _, other in attention_first]
@@ -886,13 +962,12 @@
         else:
             rows = 4 * ROWS if name == "down" else ROWS
             local(name, hidden_pairs[name], rows, LINKS[name], turned=name == "down")
-    down, gate, rise, attn = (own_sum(parts[name]) for name in ("down", "gate", "rise", "attn"))
-    norm = attn[:, 4 * D : 4 * D + 4].T
+    norm = done["attn"][2][:4, :ROWS]
     shares = (
-        attn[:, : 3 * D],
-        attn[:, 3 * D : 4 * D],
-        jnp.concatenate([gate, rise], axis=1),
-        down,
+        done["attn"][0],
+        done["attn"][1],
+        done["gate"][0],
+        done["down"][0],
         norm[:2],
         norm[2:],
     )

time: 410 us -> 399 us (0.973)
  other arithmetic: 14.7 us -> 4.58 us
  waiting for transfers between devices: 195 us -> 185 us
  Pallas kernels: 142 us -> 150 us
    ppermute x23, waiting for transfers between devices: 64.1 us -> 53.7 us  [exchange(): return lax.ppermute(values, 'dp', [(i, i ^ bit) for i in range(count)])]
    pallas_call x0 -> x4, Pallas kernels: none -> 8.58 us  [finish(): pl.pallas_call(body, out_shape=[jax.ShapeDtypeStruct(shape, F32) for shap...]
    add x4 -> x0, other arithmetic: 7.77 us -> none  [own_sum(): return sum((array[at].astype(F32) for (array, at), in parts))]
  transfers between devices with their start and end apart: 28 -> 28, of which waited for: 15 -> 14; matrix products, arithmetic and copies ran while one was open for 2% -> 0% of each run, Pallas kernels for 31% -> 34%
where the time goes in v3:
time: 399 us; the launch traced here: 391 us
  waiting for transfers between devices  185 us (46%)
  Pallas kernels  150 us (38%)
  starting transfers between devices  33 us (8%)
  between operations  14.9 us (4%)
  other arithmetic  4.58 us (1%)
    all_gather x1, waiting for transfers between devices, shards(): wide = lax.all_gather(packed, 'dp', axis=0, tiled=True)  102 us
    pallas_call x9, Pallas kernels, call_window(): pl.pallas_call(kernel, out_shape=shapes, in_specs=[SMEM] * small + [ANY]...  94.3 us
    ppermute x23, waiting for transfers between devices, exchange(): return lax.ppermute(values, 'dp', [(i, i ^ bit) for i in range(count)])  53.7 us
    pallas_call x4, Pallas kernels, weight_grad(): pl.pallas_call(body, out_shape=[shape, shape], in_specs=[SMEM] + [ANY] *...  31.4 us
    ppermute x4, waiting for transfers between devices, hop(): return lax.ppermute(rows_sent, 'section', [pair])  29.1 us
    ppermute x23, starting transfers between devices, exchange(): return lax.ppermute(values, 'dp', [(i, i ^ bit) for i in range(count)])  19.6 us
    pallas_call x8, Pallas kernels, halve(): pl.pallas_call(body, out_shape=jax.ShapeDtypeStruct((half,) + block, BF),...  15.9 us
    ppermute x4, starting transfers between devices, hop(): return lax.ppermute(rows_sent, 'section', [pair])  13.4 us
  transfers between devices with their start and end apart: 28, of which 14 were waited for; matrix products, arithmetic and copies ran while one was open for 0% of the time, Pallas kernels for 34%

profile of v3, /device:TPU:0, one launch (start us, length us, event | category | flops | bytes accessed | tf_op | source)
XLA Modules:
  0.0 391.1 jit_solution(9732347870648173817)
XLA Ops:
  12.3 102.1 %all-gather.2.cloned.1.call-done.refs_3_.refs_2_ = bf16[768,12416]{1,0:T(8,128)(2,1)} async-done(((bf16[48,12416]{1,0:T(8,128)(2,1)}), bf16[768,12416]{1,0:T(8,128)(2,1)}) %all-gather.2.cloned.1.call-update) | async-done | bytes 19070992 | tf_op jit(solution)/shard_map/all_gather | solution.py:1021
  116.1 14.5 %layer_forward.4 = (bf16[2,2304,256]{2,1,0:T(8,128)(2,1)}, bf16[2,256,2304]{2,1,0:T(8,128)(2,1)}, bf16[2,12,256,256]{3,2,1,0:T(8,128)(2,1)}, f32[2,256,768]{2,1,...) custom-call(s32[2]{0:T(128)} %pad_add_fusion.refs_0_, ...), custom_call_target="tpu_custom_call" | custom-call | flops 5000000000 | bytes 25000000 | tf_op jit(solution)/shard_map/layer_forward/pallas_call | solution.py:493
  130.7 2.0 collective-permute-start.1
  132.7 14.7 %layer_forward.5 = (bf16[2,2304,256]{2,1,0:T(8,128)(2,1)}, bf16[2,256,2304]{2,1,0:T(8,128)(2,1)}, bf16[2,12,256,256]{3,2,1,0:T(8,128)(2,1)}, f32[2,256,768]{2,1,...) custom-call(s32[2]{0:T(128)} %pad_add_fusion.refs_0_, ...), custom_call_target="tpu_custom_call", output_to_operand_aliasing={{0}: (6, {}), {1}: (7, {}), {2}: (8, {}), {3}: (9, {}), {4}... | custom-call | flops 5000000000 | bytes 25000000 | tf_op jit(solution)/shard_map/layer_forward/pallas_call | solution.py:493
  147.4 2.1 collective-permute-start
  149.5 1.3 layer_forward.6
  150.8 7.3 %collective-permute-done.refs_2_ = bf16[256,768]{1,0:T(8,128)(2,1)} collective-permute-done((bf16[256,768]{1,0:T(8,128)(2,1)}, bf16[256,768]{1,0:T(8,128)(2,1)}, u32[]{:S(2)}, u32[]{:S(2)}) %collective-permute-start) | collective-permute-done | bytes 393248 | tf_op jit(solution)/shard_map/ppermute | solution.py:1030
  158.1 1.5 layer_forward.7
  159.7 8.6 %layer_backward.3 = (bf16[3888,256]{1,0:T(8,128)(2,1)}, bf16[256,3072]{1,0:T(8,128)(2,1)}, bf16[256,3072]{1,0:T(8,128)(2,1)}, bf16[256,1536]{1,0:T(8,128)(2,1)},...) custom-call(s32[2]{0:T(128)} %pad_add_fusion.refs_0_, bf16[2,256,768]{2,1,0:T(8,128)(2,1)} %refs_1_.11, ...), custom_call_target="tpu_custom_call" | custom-call | flops 8000000000 | bytes 40000000 | tf_op jit(solution)/shard_map/layer_backward/pallas_call | solution.py:493
  168.3 8.0 %collective-permute-start.4 = (bf16[256,768]{1,0:T(8,128)(2,1)}, bf16[256,768]{1,0:T(8,128)(2,1)}, u32[]{:S(2)}, u32[]{:S(2)}) collective-permute-start(bf16[256,768]{1,0:T(8,128)(2,1)} %get-tuple-element.122), channel_id=1, source_target_pairs={{16,0},{17,1},{18,2},{19,3},{20,4},{21,5},{22,6},{23,7},{24,8},{25... | collective-permute-start | bytes 1179656 | tf_op jit(solution)/shard_map/ppermute | solution.py:1030
  176.2 9.3 %layer_backward.4 = (bf16[3888,256]{1,0:T(8,128)(2,1)}, bf16[256,3072]{1,0:T(8,128)(2,1)}, bf16[256,3072]{1,0:T(8,128)(2,1)}, bf16[256,1536]{1,0:T(8,128)(2,1)},...) custom-call(s32[2]{0:T(128)} %pad_add_fusion.refs_0_, ...), custom_call_target="tpu_custom_call", output_to_operand_aliasing={{5}: (11, {})} | custom-call | flops 8000000000 | bytes 40000000 | tf_op jit(solution)/shard_map/layer_backward/pallas_call | solution.py:493
  186.8 20.0 %collective-permute-done.4.refs_1_ = bf16[256,768]{1,0:T(8,128)(2,1)} collective-permute-done((bf16[256,768]{1,0:T(8,128)(2,1)}, bf16[256,768]{1,0:T(8,128)(2,1)}, u32[]{:S(2)}, u32[]{:S(2)}) %collective-permute-start.4) | collective-permute-done | bytes 393248 | tf_op jit(solution)/shard_map/ppermute | solution.py:1030
  206.8 20.4 %layer_backward.5 = (bf16[3888,256]{1,0:T(8,128)(2,1)}, bf16[256,3072]{1,0:T(8,128)(2,1)}, bf16[256,3072]{1,0:T(8,128)(2,1)}, bf16[256,1536]{1,0:T(8,128)(2,1)},...) custom-call(s32[2]{0:T(128)} %pad_add_fusion.refs_0_, ...), custom_call_target="tpu_custom_call", output_to_operand_aliasing={{0}: (11, {}), {1}: (12, {}), {2}: (13, {}), {3}: (14, {}),... | custom-call | flops 8000000000 | bytes 40000000 | tf_op jit(solution)/shard_map/layer_backward/pallas_call | solution.py:493
  227.2 1.9 collective-permute-done.3.refs_1_
  229.1 14.2 %backward_hidden.1 = (bf16[3888,256]{1,0:T(8,128)(2,1)}, bf16[256,3072]{1,0:T(8,128)(2,1)}, bf16[256,3072]{1,0:T(8,128)(2,1)}, f32[256,768]{1,0:T(8,128)}) custom-call(s32[2]{0:T(128)} %pad_add_fusion.refs_0_, bf16[256,768]{1,0:T(8,128)(2,1)} %collective-permute-done.3.refs_1_, ...), custom_call_target="tpu_custom_call", output_to_operand_aliasing={{0}: (9, {}), {1}: (10, {}), {2}: (11, {})} | custom-call | flops 60000002048 | bytes 300000000 | tf_op jit(solution)/shard_map/backward_hidden/pallas_call | solution.py:493
  244.5 3.2 collective-permute-done.10.refs_4_.refs_14_
  247.9 7.0 %weight_grad.4 = (bf16[4,192,768]{2,1,0:T(8,128)(2,1)}, bf16[4,192,768]{2,1,0:T(8,128)(2,1)}) custom-call(s32[2]{0:T(128)} %pad_add_fusion.refs_0_, bf16[3888,256]{1,0:T(8,128)(2,1)} %get-tuple-element.134.refs_1_.refs_11_, bf16[3888,256]{1,0:T(8,128)(2,1)} %get-tuple-element.135.refs_2_.refs_12_, bf16[3888,256]{1,0:T(8,128)(2,1)} %collective-permute-done.9.refs_3_.refs_13_, ...), custom_call_target="tpu_custom_call" | custom-call | flops 73600000000 | bytes 368000000 | tf_op jit(solution)/shard_map/weight_grad/pallas_call | solution.py:754
  255.3 1.4 collective-permute-done.8.refs_6_
  258.0 7.9 %weight_grad.5 = (bf16[4,48,3072]{2,1,0:T(8,128)(2,1)}, bf16[4,48,3072]{2,1,0:T(8,128)(2,1)}) custom-call(s32[2]{0:T(128)} %pad_add_fusion.refs_0_, bf16[2,2304,256]{2,1,0:T(8,128)(2,1)} %get-tuple-element.114.refs_1_, bf16[2,2304,256]{2,1,0:T(8,128)(2,1)} %collective-permute-done.2.refs_12_.refs_2_, bf16[256,3072]{1,0:T(8,128)(2,1)} %get-tuple-element.132.refs_3_, ...), custom_call_target="tpu_custom_call" | custom-call | flops 73600000000 | bytes 368000000 | tf_op jit(solution)/shard_map/weight_grad/pallas_call | solution.py:754
  266.0 1.6 collective-permute-start.18
  267.5 7.8 %weight_grad.6 = (bf16[4,48,3072]{2,1,0:T(8,128)(2,1)}, bf16[4,48,3072]{2,1,0:T(8,128)(2,1)}) custom-call(s32[2]{0:T(128)} %pad_add_fusion.refs_0_, bf16[2,2304,256]{2,1,0:T(8,128)(2,1)} %get-tuple-element.114.refs_1_, bf16[2,2304,256]{2,1,0:T(8,128)(2,1)} %collective-permute-done.2.refs_12_.refs_2_, bf16[256,3072]{1,0:T(8,128)(2,1)} %get-tuple-element.130.refs_3_, ...), custom_call_target="tpu_custom_call" | custom-call | flops 73600000000 | bytes 368000000 | tf_op jit(solution)/shard_map/weight_grad/pallas_call | solution.py:754
  276.2 9.8 %backward_attention.1 = (bf16[256,1536]{1,0:T(8,128)(2,1)}, bf16[256,1536]{1,0:T(8,128)(2,1)}, f32[2,256,768]{2,1,0:T(8,128)}, bf16[256,768]{1,0:T(8,128)(2,1)}) custom-call(s32[2]{0:T(128)} %pad_add_fusion.refs_0_, f32[256,768]{1,0:T(8,128)} %get-tuple-element.119.refs_1_, ...), custom_call_target="tpu_custom_call", output_to_operand_aliasing={{0}: (5, {}), {1}: (6, {}), {2}: (7, {})} | custom-call | flops 92000002048 | bytes 460000000 | tf_op jit(solution)/shard_map/backward_attention/pallas_call | solution.py:493
  286.6 2.0 halve.8.refs_15_
  289.8 8.7 %weight_grad.7 = (bf16[4,48,3200]{2,1,0:T(8,128)(2,1)}, bf16[4,48,3200]{2,1,0:T(8,128)(2,1)}) custom-call(s32[2]{0:T(128)} %pad_add_fusion.refs_0_, bf16[2,2304,256]{2,1,0:T(8,128)(2,1)} %get-tuple-element.114.refs_1_, bf16[2,2304,256]{2,1,0:T(8,128)(2,1)} %collective-permute-done.2.refs_12_.refs_2_, bf16[256,1536]{1,0:T(8,128)(2,1)} %get-tuple-element.139.refs_3_, ...), custom_call_target="tpu_custom_call" | custom-call | flops 73600000000 | bytes 368000000 | tf_op jit(solution)/shard_map/weight_grad/pallas_call | solution.py:754
  298.5 1.3 collective-permute-start.16
  299.9 2.0 halve.9.refs_2_
  302.7 8.4 %collective-permute-done.17.refs_1_ = bf16[4,48,3072]{2,1,0:T(8,128)(2,1)} collective-permute-done((bf16[4,48,3072]{2,1,0:T(8,128)(2,1)}, bf16[4,48,3072]{2,1,0:T(8,128)(2,1)}, u32[]{:S(2)}, u32[]{:S(2)}) %collective-permute-start.17) | collective-permute-done | bytes 1179680 | tf_op jit(solution)/shard_map/ppermute | solution.py:768
  311.2 2.0 halve.10.refs_3_
  313.2 1.6 collective-permute-start.19
  314.8 1.9 halve.11.refs_3_
  316.7 2.5 collective-permute-start.24
  319.2 14.5 %collective-permute-done.19.refs_2_ = bf16[2,48,3072]{2,1,0:T(8,128)(2,1)} collective-permute-done((bf16[2,48,3072]{2,1,0:T(8,128)(2,1)}, bf16[2,48,3072]{2,1,0:T(8,128)(2,1)}, u32[]{:S(2)}, u32[]{:S(2)}) %collective-permute-start.19) | collective-permute-done | bytes 589856 | tf_op jit(solution)/shard_map/ppermute | solution.py:768
  333.6 1.9 halve.12.refs_2_
  335.6 1.5 collective-permute-start.26
  337.5 2.1 halve.13.refs_4_
  339.6 2.1 collective-permute-start.21
  341.7 2.1 finish.5.refs_3_
  343.8 5.5 %collective-permute-done.23.refs_2_ = bf16[2,48,3072]{2,1,0:T(8,128)(2,1)} collective-permute-done((bf16[2,48,3072]{2,1,0:T(8,128)(2,1)}, bf16[2,48,3072]{2,1,0:T(8,128)(2,1)}, u32[]{:S(2)}, u32[]{:S(2)}) %collective-permute-start.23) | collective-permute-done | bytes 589856 | tf_op jit(solution)/shard_map/ppermute | solution.py:768
  349.3 1.9 halve.15.refs_4_
  351.3 2.5 collective-permute-start.25
  353.7 2.1 finish.6.refs_5_
  355.9 6.8 %collective-permute-done.21.refs_2_ = bf16[2,48,3200]{2,1,0:T(8,128)(2,1)} collective-permute-done((bf16[2,48,3200]{2,1,0:T(8,128)(2,1)}, bf16[2,48,3200]{2,1,0:T(8,128)(2,1)}, u32[]{:S(2)}, u32[]{:S(2)}) %collective-permute-start.21) | collective-permute-done | bytes 614432 | tf_op jit(solution)/shard_map/ppermute | solution.py:768
  362.6 2.0 halve.14.refs_4_
  365.1 9.4 %collective-permute-done.25.refs_3_ = bf16[1,48,3072]{2,1,0:T(8,128)(2,1)} collective-permute-done((bf16[1,48,3072]{2,1,0:T(8,128)(2,1)}, bf16[1,48,3072]{2,1,0:T(8,128)(2,1)}, u32[]{:S(2)}, u32[]{:S(2)}) %collective-permute-start.25) | collective-permute-done | bytes 294944 | tf_op jit(solution)/shard_map/ppermute | solution.py:768
  374.5 2.1 finish.7
  376.6 3.6 collective-permute-done.22.refs_3_
  380.3 2.2 finish.4
  382.5 1.3 slice_bitcast_fusion
  (55 shorter events, 15.6 us)
Async XLA Ops:
  7.2 3.3 copy-start.2
  7.2 3.4 copy-start.1
  7.2 107.2 %all-gather.2.cloned.1.call-start = ((), (), s32[]{:S(2)}) async-start(), calls=%async_computation | async-start | bytes 20262912 | tf_op jit(solution)/shard_map/all_gather | solution.py:1021
  10.7 1.0 copy-start
  130.7 18.8 %collective-permute-start.1 = (bf16[256,768]{1,0:T(8,128)(2,1)}, bf16[256,768]{1,0:T(8,128)(2,1)}, u32[]{:S(2)}, u32[]{:S(2)}) collective-permute-start(bf16[256,768]{1,0:T(8,128)(2,1)} %get-tuple-element.89), channel_id=1, source_target_pairs={{0,16},{1,17},{2,18},{3,19},{4,20},{5,21},{6,22},{7,23},{8,24},{9,... | collective-permute-start | bytes 1179656 | tf_op jit(solution)/shard_map/ppermute | solution.py:1030
  147.4 10.7 %collective-permute-start = (bf16[256,768]{1,0:T(8,128)(2,1)}, bf16[256,768]{1,0:T(8,128)(2,1)}, u32[]{:S(2)}, u32[]{:S(2)}) collective-permute-start(bf16[256,768]{1,0:T(8,128)(2,1)} %get-tuple-element.88), channel_id=1, source_target_pairs={{0,16},{1,17},{2,18},{3,19},{4,20},{5,21},{6,22},{7,23},{8,24},{9,... | collective-permute-start | bytes 1179656 | tf_op jit(solution)/shard_map/ppermute | solution.py:1030
  159.6 16.6 %collective-permute-start.2 = (bf16[2,2304,256]{2,1,0:T(8,128)(2,1)}, bf16[2,2304,256]{2,1,0:T(8,128)(2,1)}, u32[]{:S(2)}, u32[]{:S(2)}) collective-permute-start(bf16[2,2304,256]{2,1,0:T(8,128)(2,1)} %get-tuple-element.114.refs_1_), channel_id=1, source_target_pairs={{0,1},{1,0},{2,3},{3,2},{4,5},{5,4},{6,7},{7,6},{8,9},{9,8},{10,11... | collective-permute-start | bytes 7077896 | tf_op jit(solution)/shard_map/ppermute | solution.py:768
  168.3 38.5 %collective-permute-start.4 = (bf16[256,768]{1,0:T(8,128)(2,1)}, bf16[256,768]{1,0:T(8,128)(2,1)}, u32[]{:S(2)}, u32[]{:S(2)}) collective-permute-start(bf16[256,768]{1,0:T(8,128)(2,1)} %get-tuple-element.122), channel_id=1, source_target_pairs={{16,0},{17,1},{18,2},{19,3},{20,4},{21,5},{22,6},{23,7},{24,8},{25... | collective-permute-start | bytes 1179656 | tf_op jit(solution)/shard_map/ppermute | solution.py:1030
  185.5 43.6 %collective-permute-start.3 = (bf16[256,768]{1,0:T(8,128)(2,1)}, bf16[256,768]{1,0:T(8,128)(2,1)}, u32[]{:S(2)}, u32[]{:S(2)}) collective-permute-start(bf16[256,768]{1,0:T(8,128)(2,1)} %get-tuple-element.115), channel_id=1, source_target_pairs={{16,0},{17,1},{18,2},{19,3},{20,4},{21,5},{22,6},{23,7},{24,8},{25... | collective-permute-start | bytes 1179656 | tf_op jit(solution)/shard_map/ppermute | solution.py:1030
  227.2 17.3 %collective-permute-start.9 = (bf16[3888,256]{1,0:T(8,128)(2,1)}, bf16[3888,256]{1,0:T(8,128)(2,1)}, u32[]{:S(2)}, u32[]{:S(2)}) collective-permute-start(bf16[3888,256]{1,0:T(8,128)(2,1)} %get-tuple-element.134.refs_1_.refs_11_), channel_id=1, source_target_pairs={{0,1},{1,0},{2,3},{3,2},{4,5},{5,4},{6,7},{7,6},{8,9},{9,8},{10,11... | collective-permute-start | bytes 5971976 | tf_op jit(solution)/shard_map/ppermute | solution.py:768
  243.3 4.4 %collective-permute-start.10 = (bf16[3888,256]{1,0:T(8,128)(2,1)}, bf16[3888,256]{1,0:T(8,128)(2,1)}, u32[]{:S(2)}, u32[]{:S(2)}) collective-permute-start(bf16[3888,256]{1,0:T(8,128)(2,1)} %get-tuple-element.135.refs_2_.refs_12_), channel_id=1, source_target_pairs={{0,1},{1,0},{2,3},{3,2},{4,5},{5,4},{6,7},{7,6},{8,9},{9,8},{10,11... | collective-permute-start | bytes 5971976 | tf_op jit(solution)/shard_map/ppermute | solution.py:768
  243.4 11.5 %collective-permute-start.7 = (bf16[256,3072]{1,0:T(8,128)(2,1)}, bf16[256,3072]{1,0:T(8,128)(2,1)}, u32[]{:S(2)}, u32[]{:S(2)}) collective-permute-start(bf16[256,3072]{1,0:T(8,128)(2,1)} %get-tuple-element.132.refs_3_), channel_id=1, source_target_pairs={{0,1},{1,0},{2,3},{3,2},{4,5},{5,4},{6,7},{7,6},{8,9},{9,8},{10,11... | collective-permute-start | bytes 4718600 | tf_op jit(solution)/shard_map/ppermute | solution.py:768
  243.9 22.0 %collective-permute-start.5 = (bf16[256,3072]{1,0:T(8,128)(2,1)}, bf16[256,3072]{1,0:T(8,128)(2,1)}, u32[]{:S(2)}, u32[]{:S(2)}) collective-permute-start(bf16[256,3072]{1,0:T(8,128)(2,1)} %get-tuple-element.130.refs_3_), channel_id=1, source_target_pairs={{0,1},{1,0},{2,3},{3,2},{4,5},{5,4},{6,7},{7,6},{8,9},{9,8},{10,11... | collective-permute-start | bytes 4718600 | tf_op jit(solution)/shard_map/ppermute | solution.py:768
  244.0 32.2 %collective-permute-start.11 = (bf16[256,1536]{1,0:T(8,128)(2,1)}, bf16[256,1536]{1,0:T(8,128)(2,1)}, u32[]{:S(2)}, u32[]{:S(2)}) collective-permute-start(bf16[256,1536]{1,0:T(8,128)(2,1)} %get-tuple-element.139.refs_3_), channel_id=1, source_target_pairs={{0,1},{1,0},{2,3},{3,2},{4,5},{5,4},{6,7},{7,6},{8,9},{9,8},{10,11... | collective-permute-start | bytes 2359304 | tf_op jit(solution)/shard_map/ppermute | solution.py:768
  244.4 31.8 %collective-permute-start.12 = (bf16[256,1536]{1,0:T(8,128)(2,1)}, bf16[256,1536]{1,0:T(8,128)(2,1)}, u32[]{:S(2)}, u32[]{:S(2)}) collective-permute-start(bf16[256,1536]{1,0:T(8,128)(2,1)} %get-tuple-element.140.refs_7_), channel_id=1, source_target_pairs={{0,1},{1,0},{2,3},{3,2},{4,5},{5,4},{6,7},{7,6},{8,9},{9,8},{10,11... | collective-permute-start | bytes 2359304 | tf_op jit(solution)/shard_map/ppermute | solution.py:768
  247.8 9.0 %collective-permute-start.8 = (bf16[256,3072]{1,0:T(8,128)(2,1)}, bf16[256,3072]{1,0:T(8,128)(2,1)}, u32[]{:S(2)}, u32[]{:S(2)}) collective-permute-start(bf16[256,3072]{1,0:T(8,128)(2,1)} %get-tuple-element.133.refs_4_), channel_id=1, source_target_pairs={{0,1},{1,0},{2,3},{3,2},{4,5},{5,4},{6,7},{7,6},{8,9},{9,8},{10,11... | collective-permute-start | bytes 4718600 | tf_op jit(solution)/shard_map/ppermute | solution.py:768
  254.9 12.6 %collective-permute-start.6 = (bf16[256,3072]{1,0:T(8,128)(2,1)}, bf16[256,3072]{1,0:T(8,128)(2,1)}, u32[]{:S(2)}, u32[]{:S(2)}) collective-permute-start(bf16[256,3072]{1,0:T(8,128)(2,1)} %get-tuple-element.131.refs_4_), channel_id=1, source_target_pairs={{0,1},{1,0},{2,3},{3,2},{4,5},{5,4},{6,7},{7,6},{8,9},{9,8},{10,11... | collective-permute-start | bytes 4718600 | tf_op jit(solution)/shard_map/ppermute | solution.py:768
  256.8 29.9 %collective-permute-start.15 = (bf16[4,192,768]{2,1,0:T(8,128)(2,1)}, bf16[4,192,768]{2,1,0:T(8,128)(2,1)}, u32[]{:S(2)}, u32[]{:S(2)}) collective-permute-start(bf16[4,192,768]{2,1,0:T(8,128)(2,1)} %get-tuple-element.136.refs_7_), channel_id=1, source_target_pairs={{0,2},{1,3},{2,0},{3,1},{4,6},{5,7},{6,4},{7,5},{8,10},{9,11},{10,... | collective-permute-start | bytes 3538952 | tf_op jit(solution)/shard_map/ppermute | solution.py:768
  266.0 33.9 %collective-permute-start.18 = (bf16[4,48,3072]{2,1,0:T(8,128)(2,1)}, bf16[4,48,3072]{2,1,0:T(8,128)(2,1)}, u32[]{:S(2)}, u32[]{:S(2)}) collective-permute-start(bf16[4,48,3072]{2,1,0:T(8,128)(2,1)} %get-tuple-element.137.refs_7_), channel_id=1, source_target_pairs={{0,4},{1,5},{2,6},{3,7},{4,0},{5,1},{6,2},{7,3},{8,12},{9,13},{10,... | collective-permute-start | bytes 3538952 | tf_op jit(solution)/shard_map/ppermute | solution.py:768
  275.4 35.8 %collective-permute-start.17 = (bf16[4,48,3072]{2,1,0:T(8,128)(2,1)}, bf16[4,48,3072]{2,1,0:T(8,128)(2,1)}, u32[]{:S(2)}, u32[]{:S(2)}) collective-permute-start(bf16[4,48,3072]{2,1,0:T(8,128)(2,1)} %get-tuple-element.138.refs_8_), channel_id=1, source_target_pairs={{0,2},{1,3},{2,0},{3,1},{4,6},{5,7},{6,4},{7,5},{8,10},{9,11},{10,... | collective-permute-start | bytes 3538952 | tf_op jit(solution)/shard_map/ppermute | solution.py:768
  286.0 3.5 collective-permute-start.13
  286.1 3.7 collective-permute-start.14
  288.7 26.1 %collective-permute-start.20 = (bf16[2,192,768]{2,1,0:T(8,128)(2,1)}, bf16[2,192,768]{2,1,0:T(8,128)(2,1)}, u32[]{:S(2)}, u32[]{:S(2)}) collective-permute-start(bf16[2,192,768]{2,1,0:T(8,128)(2,1)} %halve.8.refs_15_), channel_id=1, source_target_pairs={{0,4},{1,5},{2,6},{3,7},{4,0},{5,1},{6,2},{7,3},{8,12},{9,13},{10,... | collective-permute-start | bytes 1769480 | tf_op jit(solution)/shard_map/ppermute | solution.py:768
  298.5 39.0 %collective-permute-start.16 = (bf16[4,48,3200]{2,1,0:T(8,128)(2,1)}, bf16[4,48,3200]{2,1,0:T(8,128)(2,1)}, u32[]{:S(2)}, u32[]{:S(2)}) collective-permute-start(bf16[4,48,3200]{2,1,0:T(8,128)(2,1)} %get-tuple-element.146.refs_2_), channel_id=1, source_target_pairs={{0,2},{1,3},{2,0},{3,1},{4,6},{5,7},{6,4},{7,5},{8,10},{9,11},{10,... | collective-permute-start | bytes 3686408 | tf_op jit(solution)/shard_map/ppermute | solution.py:768
  301.9 47.4 %collective-permute-start.23 = (bf16[2,48,3072]{2,1,0:T(8,128)(2,1)}, bf16[2,48,3072]{2,1,0:T(8,128)(2,1)}, u32[]{:S(2)}, u32[]{:S(2)}) collective-permute-start(bf16[2,48,3072]{2,1,0:T(8,128)(2,1)} %halve.9.refs_2_), channel_id=1, source_target_pairs={{0,2},{1,3},{2,0},{3,1},{4,6},{5,7},{6,4},{7,5},{8,10},{9,11},{10,... | collective-permute-start | bytes 1769480 | tf_op jit(solution)/shard_map/ppermute | solution.py:768
  313.2 20.4 %collective-permute-start.19 = (bf16[2,48,3072]{2,1,0:T(8,128)(2,1)}, bf16[2,48,3072]{2,1,0:T(8,128)(2,1)}, u32[]{:S(2)}, u32[]{:S(2)}) collective-permute-start(bf16[2,48,3072]{2,1,0:T(8,128)(2,1)} %halve.10.refs_3_), channel_id=1, source_target_pairs={{0,4},{1,5},{2,6},{3,7},{4,0},{5,1},{6,2},{7,3},{8,12},{9,13},{10,... | collective-permute-start | bytes 1769480 | tf_op jit(solution)/shard_map/ppermute | solution.py:768
  316.7 25.0 %collective-permute-start.24 = (bf16[1,192,768]{2,1,0:T(8,128)(2,1)}, bf16[1,192,768]{2,1,0:T(8,128)(2,1)}, u32[]{:S(2)}, u32[]{:S(2)}) collective-permute-start(bf16[1,192,768]{2,1,0:T(8,128)(2,1)} %halve.11.refs_3_), channel_id=1, source_target_pairs={{0,8},{1,9},{2,10},{3,11},{4,12},{5,13},{6,14},{7,15},{8,0},{9,1},... | collective-permute-start | bytes 884744 | tf_op jit(solution)/shard_map/ppermute | solution.py:768
  335.6 18.1 %collective-permute-start.26 = (bf16[1,48,3072]{2,1,0:T(8,128)(2,1)}, bf16[1,48,3072]{2,1,0:T(8,128)(2,1)}, u32[]{:S(2)}, u32[]{:S(2)}) collective-permute-start(bf16[1,48,3072]{2,1,0:T(8,128)(2,1)} %halve.12.refs_2_), channel_id=1, source_target_pairs={{0,8},{1,9},{2,10},{3,11},{4,12},{5,13},{6,14},{7,15},{8,0},{9,1},... | collective-permute-start | bytes 884744 | tf_op jit(solution)/shard_map/ppermute | solution.py:768
  339.6 23.1 %collective-permute-start.21 = (bf16[2,48,3200]{2,1,0:T(8,128)(2,1)}, bf16[2,48,3200]{2,1,0:T(8,128)(2,1)}, u32[]{:S(2)}, u32[]{:S(2)}) collective-permute-start(bf16[2,48,3200]{2,1,0:T(8,128)(2,1)} %halve.13.refs_4_), channel_id=1, source_target_pairs={{0,4},{1,5},{2,6},{3,7},{4,0},{5,1},{6,2},{7,3},{8,12},{9,13},{10,... | collective-permute-start | bytes 1843208 | tf_op jit(solution)/shard_map/ppermute | solution.py:768
  351.3 23.3 %collective-permute-start.25 = (bf16[1,48,3072]{2,1,0:T(8,128)(2,1)}, bf16[1,48,3072]{2,1,0:T(8,128)(2,1)}, u32[]{:S(2)}, u32[]{:S(2)}) collective-permute-start(bf16[1,48,3072]{2,1,0:T(8,128)(2,1)} %halve.15.refs_4_), channel_id=1, source_target_pairs={{0,8},{1,9},{2,10},{3,11},{4,12},{5,13},{6,14},{7,15},{8,0},{9,1},... | collective-permute-start | bytes 884744 | tf_op jit(solution)/shard_map/ppermute | solution.py:768
  364.6 15.7 %collective-permute-start.22 = (bf16[1,48,3200]{2,1,0:T(8,128)(2,1)}, bf16[1,48,3200]{2,1,0:T(8,128)(2,1)}, u32[]{:S(2)}, u32[]{:S(2)}) collective-permute-start(bf16[1,48,3200]{2,1,0:T(8,128)(2,1)} %halve.14.refs_4_), channel_id=1, source_target_pairs={{0,8},{1,9},{2,10},{3,11},{4,12},{5,13},{6,14},{7,15},{8,0},{9,1},... | collective-permute-start | bytes 921608 | tf_op jit(solution)/shard_map/ppermute | solution.py:768
Sparse Core Ops, SparseCore 0:
  11.8 102.5 all-gather.1

commit v4 on v3

--- a/solution.py
+++ b/solution.py
@@ -80,10 +80,10 @@
 
 
 def forward_window(
-    ids, lengths, given, wide, down, norms,
+    ids, lengths, given, wide, down,
     left_out, qkv_out, probs_out, n1_out, h1_out, n2_out, inv_out, layer_out, hop_out,
     w_qkv, w_out, w_gu, w_down, x, qkv, probs, context, n1, h1, n2, inv, result, norm, left,
-    w_sem, o_sem, i_sem, *, micro, direct,
+    w_sem, o_sem, i_sem, *, micro, direct, fused=False,
 ):
     window = ids[1]
     copies = {}
@@ -91,7 +91,7 @@
     for k in range(3):
         cols = pl.ds(D * k, D)
         copies["qkv", k] = begin(wide.at[:, cols], w_qkv.at[:, cols], w_sem.at[k])
-    copies["norm"] = begin(norms, norm, i_sem.at[1])
+    copies["norm"] = begin(wide.at[:, pl.ds(COL_NORM, 128)], norm, i_sem.at[1])
 
     def fetch_down(j, base):
         owners = down.at[pl.ds(4 * j, 4)]
@@ -111,6 +111,8 @@
     flushed = []
 
     def flush(source, target):
+        if target is None:
+            return
         flushed.append(begin(source, target, o_sem.at[len(flushed)]))
 
     row_place = lax.broadcasted_iota(jnp.int32, (SEQ, SEQ), 0)
@@ -163,8 +165,9 @@
     flush_turned(1, context[...])
     copies["out"].wait()
     copies["norm"].wait()
+    params = norm[...].astype(F32).T
     summed = rows_in.astype(F32) + matmul(context[...], w_out[...])
-    hidden, normed, inverse_one = norm_forward(summed, norm[0:1, :], norm[2:3, :])
+    hidden, normed, inverse_one = norm_forward(summed, params[0:1], params[2:3])
     n1[...] = normed
     flush(n1, n1_out)
     low_hidden = hidden.astype(BF)
@@ -180,7 +183,7 @@
         for q in range(4):
             copies["down", j, q].wait()
         hidden = hidden + matmul(gated, w_down[j].reshape(CHUNK, D))
-    final, normed, inverse_two = norm_forward(hidden, norm[1:2, :], norm[3:4, :])
+    final, normed, inverse_two = norm_forward(hidden, params[1:2], params[3:4])
     result[...] = final.astype(BF)
     flush(result, hop_out)
     flush(result, layer_out)
@@ -188,35 +191,50 @@
     flush(n2, n2_out)
     inv[...] = jnp.where(first, inverse_one, inverse_two)
     flush(inv, inv_out)
+    if fused:
+        return flushed
     for copy in flushed:
         copy.wait()
 
 
+class InPlace:
+    def wait(self):
+        return None
+
+
 def backward_hidden(
-    ids, given, wide, down, norms, n1_in, h1_in, n2_in, inv_in, hidden_out, gate_out, up_out,
+    ids, given, wide, down, n1_in, h1_in, n2_in, inv_in, hidden_out, gate_out, up_out,
     w_gu, w_down, upstream, n1, h1, n2, inv, norm, gated, down_grad, gu_grad, norm_grad,
-    low_norm, w_sem, o_sem, i_sem, *, micro, direct, ahead,
+    low_norm, w_sem, o_sem, i_sem, *, micro, direct, ahead, arriving=None,
 ):
-    arriving = begin(own_window(given, micro), upstream, i_sem.at[0])
-    normed_two = begin(n2_in.at[micro], n2, i_sem.at[1])
-    inverses = begin(inv_in.at[micro], inv, i_sem.at[2])
-    gains = begin(norms, norm, i_sem.at[3])
-    hidden = begin(h1_in.at[micro], h1, i_sem.at[4])
+    resident = arriving is not None
+
+    def load(source, target, semaphore):
+        return InPlace() if resident else begin(source, target, semaphore)
+
+    if not resident:
+        arriving = begin(own_window(given, micro), upstream, i_sem.at[0])
+        normed_two = begin(n2_in.at[micro], n2, i_sem.at[1])
+        inverses = begin(inv_in.at[micro], inv, i_sem.at[2])
+        gains = begin(wide.at[:, pl.ds(COL_NORM, 128)], norm, i_sem.at[3])
+        hidden = begin(h1_in.at[micro], h1, i_sem.at[4])
+    else:
+        normed_two = inverses = gains = hidden = InPlace()
     copies = {}
 
     def fetch_down(j, base):
         owners = down.at[pl.ds(4 * j, 4)]
         for q in range(4):
             source = owners.at[:, :, pl.ds(COL_DOWN + D * q, D)] if direct else owners.at[:, q]
-            copies["down", j, q] = begin(
+            copies["down", j, q] = load(
                 source, w_down.at[j, :, q], w_sem.at[base + 4 * j + q]
             )
 
     def fetch_chunk(j):
         gate = wide.at[:, pl.ds(COL_GU + j * CHUNK, CHUNK)]
         rise = wide.at[:, pl.ds(COL_GU + FF + j * CHUNK, CHUNK)]
-        copies["gate", j] = begin(gate, w_gu.at[j], w_sem.at[j])
-        copies["up", j] = begin(rise, w_gu.at[CHUNKS + j], w_sem.at[CHUNKS + j])
+        copies["gate", j] = load(gate, w_gu.at[j], w_sem.at[j])
+        copies["up", j] = load(rise, w_gu.at[CHUNKS + j], w_sem.at[CHUNKS + j])
         fetch_down(j, 2 * CHUNKS)
 
     fetch_chunk(0)
@@ -229,9 +247,10 @@
     normed_two.wait()
     inverses.wait()
     gains.wait()
+    params = norm[...].astype(F32).T
     up = upstream[...].astype(F32)
     normed = n2[...]
-    grad_two = norm_backward(up, normed, inv[:, HEAD : HEAD + 1], norm[1:2, :])
+    grad_two = norm_backward(up, normed, inv[:, HEAD : HEAD + 1], params[1:2])
     norm_grad[...] = jnp.zeros_like(norm_grad)
     norm_grad[1:2, :] = jnp.sum(up * normed, axis=0, keepdims=True)
     norm_grad[3:4, :] = jnp.sum(up, axis=0, keepdims=True)
@@ -247,7 +266,9 @@
         if j + 1 < CHUNKS:
             fetch_chunk(j + 1)
         else:
-            first_norm = begin(n1_in.at[micro], n1, i_sem.at[5])
+            first_norm = InPlace()
+            if not resident:
+                first_norm = begin(n1_in.at[micro], n1, i_sem.at[5])
             ahead()
         gate = matmul(low_hidden, w_gu[j])
         rise = matmul(low_hidden, w_gu[CHUNKS + j])
@@ -270,7 +291,7 @@
         total = total + matmul(gate_grad, w_gu[j], NT) + matmul(rise_grad, w_gu[CHUNKS + j], NT)
     first_norm.wait()
     normed = n1[...]
-    grad_one = norm_backward(total, normed, inv[:, 0:1], norm[0:1, :])
+    grad_one = norm_backward(total, normed, inv[:, 0:1], params[0:1])
     norm_grad[0:1, :] = jnp.sum(total * normed, axis=0, keepdims=True)
     norm_grad[2:3, :] = jnp.sum(total, axis=0, keepdims=True)
     low_norm[...] = norm_grad[...].astype(BF)
@@ -353,7 +374,7 @@
 
 
 def backward_window(
-    ids, given, wide, down, norms, qkv_in, probs_in, n1_in, h1_in, n2_in, inv_in,
+    ids, given, wide, down, qkv_in, probs_in, n1_in, h1_in, n2_in, inv_in,
     hidden_out, gate_out, up_out, qk_out, vc_out, grad_out, hop_out,
     w_gu, w_down, upstream, n1, h1, n2, inv, norm, gated, down_grad, gu_grad, norm_grad, low_norm,
     w_qkv, w_out, qkv, probs, attn_grad, context_grad, qkv_grad, grad, result,
@@ -370,7 +391,7 @@
         )
 
     grad_one, flushed = backward_hidden(
-        ids, given, wide, down, norms, n1_in, h1_in, n2_in, inv_in, hidden_out, gate_out, up_out,
+        ids, given, wide, down, n1_in, h1_in, n2_in, inv_in, hidden_out, gate_out, up_out,
         w_gu, w_down, upstream, n1, h1, n2, inv, norm, gated, down_grad, gu_grad, norm_grad,
         low_norm, w_sem, o_sem, i_sem, micro=micro, direct=direct, ahead=ahead,
     )
@@ -383,14 +404,44 @@
         copy.wait()
 
 
+def both_ways(
+    ids, lengths, given, cotangent, wide, down,
+    left_out, layer_out, hidden_out, gate_out, up_out, qk_out, vc_out, grad_out, hop_out,
+    w_gu, w_down, upstream, n1, h1, n2, inv, norm, gated, down_grad, gu_grad, norm_grad, low_norm,
+    w_qkv, w_out, qkv, probs, attn_grad, context_grad, qkv_grad, grad, result,
+    x, context, final, left, w_sem, o_sem, i_sem, f_sem, *, micro, direct,
+):
+    arriving = begin(own_window(cotangent, micro), upstream, i_sem.at[2])
+    flushed = forward_window(
+        ids, lengths, given, wide, down,
+        left_out, None, None, None, None, None, None, layer_out, None,
+        w_qkv, w_out, w_gu, w_down, x, qkv, probs, context, n1, h1, n2, inv, final, norm, left,
+        w_sem, f_sem, i_sem, micro=micro, direct=direct, fused=True,
+    )
+    grad_one, stores = backward_hidden(
+        ids, None, wide, down, None, None, None, None, hidden_out, gate_out, up_out,
+        w_gu, w_down, upstream, n1, h1, n2, inv, norm, gated, down_grad, gu_grad, norm_grad,
+        low_norm, w_sem, o_sem, i_sem, micro=micro, direct=direct, ahead=lambda: None,
+        arriving=arriving,
+    )
+    flushed += stores
+    flushed += backward_attention(
+        grad_one, [InPlace()] * 6, qk_out, vc_out, grad_out, hop_out,
+        w_qkv, w_out, qkv, probs, attn_grad, context_grad, qkv_grad, grad, result,
+        o_sem.at[pl.ds(HIDDEN_STORES, 5)], micro=micro,
+    )
+    for copy in flushed:
+        copy.wait()
+
+
 def backward_first_half(
-    ids, given, wide, down, norms, n1_in, h1_in, n2_in, inv_in,
+    ids, given, wide, down, n1_in, h1_in, n2_in, inv_in,
     hidden_out, gate_out, up_out, half_out,
     w_gu, w_down, upstream, n1, h1, n2, inv, norm, gated, down_grad, gu_grad, norm_grad, low_norm,
     half, w_sem, o_sem, i_sem, *, micro, direct,
 ):
     grad_one, flushed = backward_hidden(
-        ids, given, wide, down, norms, n1_in, h1_in, n2_in, inv_in, hidden_out, gate_out, up_out,
+        ids, given, wide, down, n1_in, h1_in, n2_in, inv_in, hidden_out, gate_out, up_out,
         w_gu, w_down, upstream, n1, h1, n2, inv, norm, gated, down_grad, gu_grad, norm_grad,
         low_norm, w_sem, o_sem, i_sem, micro=micro, direct=direct, ahead=lambda: None,
     )
@@ -444,7 +495,7 @@
     pltpu.VMEM((SEQ, D), BF),
     pltpu.VMEM((SEQ, D), F32),
     pltpu.VMEM((SEQ, 128), F32),
-    pltpu.VMEM((8, D), F32),
+    pltpu.VMEM((D, 128), BF),
     pltpu.VMEM((FF, SEQ), BF),
     pltpu.VMEM((D, SEQ), BF),
     pltpu.VMEM((SEQ, 2 * FF), BF),
@@ -505,7 +556,7 @@
     )(*operands)
 
 
-def forward_call(owner, micro, direct, ids, lengths, given, wide, down, norms, before):
+def forward_call(owner, micro, direct, ids, lengths, given, wide, down, before):
     scratch = (
         ATTENTION_WEIGHTS
         + HIDDEN_WEIGHTS
@@ -519,7 +570,7 @@
             pltpu.VMEM((SEQ, D), F32),
             pltpu.VMEM((SEQ, 128), F32),
             pltpu.VMEM((SEQ, D), BF),
-            pltpu.VMEM((8, D), F32),
+            pltpu.VMEM((D, 128), BF),
             pltpu.VMEM((3 * D, SEQ), BF),
             DMA((4 + 6 * CHUNKS,)),
             DMA((12,)),
@@ -531,7 +582,7 @@
         "layer_forward",
         owner,
         micro,
-        (ids, lengths, given, wide, down, norms),
+        (ids, lengths, given, wide, down),
         FORWARD_KEPT,
         BF,
         before,
@@ -541,34 +592,61 @@
     )
 
 
-def backward_call(owner, micro, direct, ids, given, wide, down, norms, stash, before, gates):
+def both_ways_call(owner, micro, direct, ids, lengths, given, cotangent, wide, down, before):
+    return call_window(
+        functools.partial(both_ways, micro=micro, direct=direct),
+        "layer_both_ways",
+        owner,
+        micro,
+        (ids, lengths, given, cotangent, wide, down),
+        (FORWARD_KEPT[0], FORWARD_KEPT[-1]) + HIDDEN_KEPT + ATTENTION_KEPT,
+        BF,
+        before,
+        HIDDEN_SCRATCH
+        + ATTENTION_SCRATCH
+        + (
+            pltpu.VMEM((SEQ, D), BF),
+            pltpu.VMEM((SEQ, D), BF),
+            pltpu.VMEM((SEQ, D), BF),
+            pltpu.VMEM((3 * D, SEQ), BF),
+            DMA((4 + 6 * CHUNKS,)),
+            DMA((HIDDEN_STORES + 5,)),
+            DMA((3,)),
+            DMA((12,)),
+        ),
+        130_000_000_000,
+        2,
+    )
+
+
+def backward_call(owner, micro, direct, ids, given, wide, down, stash, before, gates):
     return call_window(
         functools.partial(backward_window, micro=micro, direct=direct),
         "layer_backward",
         owner,
         micro,
-        (ids, given, wide, down, norms) + tuple(stash),
+        (ids, given, wide, down) + tuple(stash),
         HIDDEN_KEPT + ATTENTION_KEPT,
         BF,
         before,
         HIDDEN_SCRATCH
         + ATTENTION_SCRATCH
         + (DMA((4 + 6 * CHUNKS,)), DMA((HIDDEN_STORES + 5,)), DMA((8,))),
-        8_000_000_000,
+        80_000_000_000,
         1,
         gates,
     )
 
 
 def first_half_call(
-    owner, micro, direct, ids, given, wide, down, norms, stash, before, gates
+    owner, micro, direct, ids, given, wide, down, stash, before, gates
 ):
     return call_window(
         functools.partial(backward_first_half, micro=micro, direct=direct),
         "backward_hidden",
         owner,
         micro,
-        (ids, given, wide, down, norms) + tuple(stash),
+        (ids, given, wide, down) + tuple(stash),
         HIDDEN_KEPT,
         F32,
         before,
@@ -600,6 +678,52 @@
         1,
         gates,
     )
+
+
+def pack_direct(w_qkv, w_out, w_gate_up, w_down, norm_gain, norm_bias):
+    columns = [(0, 3 * D), (COL_OUT, D), (COL_GU, FF), (COL_GU + FF, FF)]
+    columns += [(COL_DOWN + D * q, D) for q in range(4)]
+
+    def body(qkv, out, gate_up, down, gain, bias, packed, held, low, square, i_sem, o_sem):
+        sources = [qkv, out, gate_up.at[:, pl.ds(0, FF)], gate_up.at[:, pl.ds(FF, FF)]]
+        sources += [down.at[pl.ds(ROWS * q, ROWS)] for q in range(4)]
+        loads = [
+            begin(source, held.at[:, pl.ds(start, size)], i_sem.at[k])
+            for k, (source, (start, size)) in enumerate(zip(sources, columns))
+        ]
+        square[...] = jnp.zeros_like(square)
+        square[pl.ds(0, 2), pl.ds(0, ROWS)] = gain[...]
+        square[pl.ds(2, 2), pl.ds(0, ROWS)] = bias[...]
+        low[:, pl.ds(COL_NORM, 128)] = square[...].T[:ROWS].astype(BF)
+        stores = []
+        for k, (load, (start, size)) in enumerate(zip(loads, columns)):
+            cols = pl.ds(start, size)
+            load.wait()
+            low[:, cols] = held[:, cols].astype(BF)
+            if k + 1 < len(loads):
+                stores.append(begin(low.at[:, cols], packed.at[:, cols], o_sem.at[k]))
+        cols = pl.ds(columns[-1][0], D + 128)
+        stores.append(begin(low.at[:, cols], packed.at[:, cols], o_sem.at[len(loads) - 1]))
+        for store in stores:
+            store.wait()
+
+    small = pl.BlockSpec(memory_space=pltpu.VMEM)
+    return pl.pallas_call(
+        body,
+        out_shape=jax.ShapeDtypeStruct((ROWS, WIDE), BF),
+        in_specs=[ANY] * 4 + [small] * 2,
+        out_specs=ANY,
+        scratch_shapes=[
+            pltpu.VMEM((ROWS, COL_NORM), F32),
+            pltpu.VMEM((ROWS, WIDE), BF),
+            pltpu.VMEM((128, 128), F32),
+            DMA((8,)),
+            DMA((8,)),
+        ],
+        compiler_params=pltpu.CompilerParams(vmem_limit_bytes=VMEM_LIMIT),
+        cost_estimate=cost_of(2),
+        name="pack",
+    )(w_qkv, w_out, w_gate_up, w_down, norm_gain, norm_bias)
 
 
 def pack(w_qkv, w_out, w_gate_up, w_down, norm_gain, norm_bias):
@@ -850,11 +974,12 @@
                 [total[:, 4 * D :], jnp.zeros((128 - rows, 128), F32)], axis=0
             ).T
             made[:, pl.ds(0, 4 * D)] = total[:, : 4 * D]
-            made[pl.ds(0, 8), pl.ds(4 * D, 128)] = norms[:8]
+            outs[2][...] = norms[0:2, :rows]
+            outs[3][...] = norms[2:4, :rows]
         else:
             made[...] = total
         stores = []
-        for k, (out, (shape, start, column)) in enumerate(zip(outs, pieces)):
+        for k, (out, (shape, start, column)) in enumerate(zip(outs, pieces[:2])):
             count, size = min(shape[0], rows), min(shape[1], width)
             source = made.at[pl.ds(0, count), pl.ds(start, size)]
             stores.append(begin(source, out.at[:, pl.ds(column, size)], o_sem.at[k]))
@@ -865,7 +990,9 @@
         body,
         out_shape=[jax.ShapeDtypeStruct(shape, F32) for shape, _, _ in pieces],
         in_specs=[ANY] * len(operands),
-        out_specs=[ANY] * len(pieces),
+        out_specs=([ANY] * 2 + [pl.BlockSpec(memory_space=pltpu.VMEM)] * 2)[: len(pieces)]
+        if len(pieces) > 1
+        else [ANY],
         input_output_aliases={} if carried is None else {len(operands) - 1: 0},
         scratch_shapes=[
             pltpu.VMEM((len(parts), rows, width), BF),
@@ -937,7 +1064,7 @@
                 "down": [((4 * ROWS, D), 0, 0)],
                 "gate": [(wide, 0, 0)],
                 "rise": [(wide, 0, FF)],
-                "attn": [((ROWS, 3 * D), 0, 0), ((ROWS, D), 3 * D, 0), ((8, 128), 4 * D, 0)],
+                "attn": [((ROWS, 3 * D), 0, 0), ((ROWS, D), 3 * D, 0)] + [((2, ROWS), 0, 0)] * 2,
             }
             carried = done["gate"][0] if "gate" in done and name in ("gate", "rise") else None
             made = finish(parts[name], last, pieces[name], carried)
@@ -962,14 +1089,13 @@
         else:
             rows = 4 * ROWS if name == "down" else ROWS
             local(name, hidden_pairs[name], rows, LINKS[name], turned=name == "down")
-    norm = done["attn"][2][:4, :ROWS]
     shares = (
         done["attn"][0],
         done["attn"][1],
         done["gate"][0],
         done["down"][0],
-        norm[:2],
-        norm[2:],
+        done["attn"][2],
+        done["attn"][3],
     )
     return shares, input_grads
 
@@ -1015,55 +1141,55 @@
     direct = rows == ROWS
     section = lax.axis_index("section")
     ids = jnp.stack([section, lax.axis_index("dp")]).astype(jnp.int32)
-    packed = pack(
-        *(w[0].astype(BF) for w in (w_qkv, w_out, w_gate_up, w_down, norm_gain, norm_bias))
-    )
+    sharded = [w[0] for w in (w_qkv, w_out, w_gate_up, w_down, norm_gain, norm_bias)]
+    packed = pack_direct(*sharded) if direct else pack(*(w.astype(BF) for w in sharded))
     wide = lax.all_gather(packed, "dp", axis=0, tiled=True)
     if direct:
         down = wide.reshape(D // rows, rows, WIDE)
     else:
         down = wide[:, COL_DOWN:COL_NORM].reshape(D // rows, rows, 4, D)
         down = down.transpose(0, 2, 1, 3).reshape(FF // (4 * ROWS), 4, ROWS, D)
-    norms = wide[:, COL_NORM : COL_NORM + 8].astype(F32).T
 
     def hop(rows_sent, pair):
         return lax.ppermute(rows_sent, "section", [pair])
 
     def forward(owner, micro, given, before):
         return forward_call(
-            owner, micro, direct, ids, lengths, given, wide, down, norms, before
+            owner, micro, direct, ids, lengths, given, wide, down, before
         )
 
     *kept, sent = forward(0, 0, tokens, [None] * len(FORWARD_KEPT))
     arrived_first = hop(sent, (0, 1))
     *kept, sent = forward(0, 1, tokens, kept)
     arrived_second = hop(sent, (0, 1))
-    *kept, sent = forward(1, 0, arrived_first, kept)
-    *kept, sent = forward(1, 1, arrived_second, kept)
     left, qkv, probs, n1, h1, n2, inv, layer_out = kept
     stash = (qkv, probs, n1, h1, n2, inv)
 
-    def backward(owner, micro, given, before, gates=()):
-        return backward_call(
-            owner, micro, direct, ids, given, wide, down, norms, stash, before, gates
+    def both_passes(micro, given, before):
+        return both_ways_call(
+            1, micro, direct, ids, lengths, given, cotangent, wide, down, before
         )
 
     def both(array):
         return [(array, None), (exchange(array, BIT_CORE), None)]
 
+    left, layer_out, *first, input_grads, sent = both_passes(
+        0, arrived_first, [left, layer_out] + [None] * 6
+    )
+    arrived_first = hop(sent, (1, 0))
+    left, layer_out, *second, input_grads, sent = both_passes(
+        1, arrived_second, [left, layer_out] + [None] * 5 + [input_grads]
+    )
+    arrived_second = hop(sent, (1, 0))
     left_other = exchange(left, BIT_CORE) if direct else left
-    *first, input_grads, sent = backward(1, 0, cotangent, [None] * 6)
-    arrived_first = hop(sent, (1, 0))
-    gates = (left_other,) if direct else ()
-    *second, input_grads, sent = backward(
-        1, 1, cotangent, [None] * 5 + [input_grads], gates
-    )
-    arrived_second = hop(sent, (1, 0))
-    *first, input_grads, sent = backward(0, 0, arrived_first, first + [input_grads])
+    *first, input_grads, sent = backward_call(
+        0, 0, direct, ids, arrived_first, wide, down, stash, first + [input_grads], ()
+    )
     if direct:
         first = [both(array) for array in first]
+    gates = (left_other,) if direct else ()
     *hidden, half = first_half_call(
-        0, 1, direct, ids, arrived_second, wide, down, norms, (n1, h1, n2, inv), second[:3], ()
+        0, 1, direct, ids, arrived_second, wide, down, (n1, h1, n2, inv), second[:3], gates
     )
 
     def second_half(gates):

time: 399 us -> 380 us (0.952)
  waiting for transfers between devices: 185 us -> 174 us
  Pallas kernels: 150 us -> 157 us
  starting transfers between devices: 33 us -> 26.7 us
  other arithmetic: 4.58 us -> 0.59 us
    ppermute x4, waiting for transfers between devices: 29.1 us -> 18.4 us  [hop(): return lax.ppermute(rows_sent, 'section', [pair])]
    ppermute x4, starting transfers between devices: 13.4 us -> 6.69 us  [hop(): return lax.ppermute(rows_sent, 'section', [pair])]
    pallas_call x9 -> x7, Pallas kernels: 94.3 us -> 96.9 us  [call_window(): pl.pallas_call(kernel, out_shape=shapes, in_specs=[SMEM] * small + [ANY]...]
  transfers between devices with their start and end apart: 28 -> 28, of which waited for: 14 -> 13; matrix products, arithmetic and copies ran while one was open for 0% -> 0% of each run, Pallas kernels for 34% -> 37%
where the time goes in v4:
time: 380 us; the launch traced here: 373 us
  waiting for transfers between devices  174 us (46%)
  Pallas kernels  157 us (41%)
  starting transfers between devices  26.7 us (7%)
  between operations  14.8 us (4%)
    all_gather x1, waiting for transfers between devices, shards(): wide = lax.all_gather(packed, 'dp', axis=0, tiled=True)  102 us
    pallas_call x7, Pallas kernels, call_window(): pl.pallas_call(kernel, out_shape=shapes, in_specs=[SMEM] * small + [ANY]...  96.9 us
    ppermute x23, waiting for transfers between devices, exchange(): return lax.ppermute(values, 'dp', [(i, i ^ bit) for i in range(count)])  53.5 us
    pallas_call x4, Pallas kernels, weight_grad(): pl.pallas_call(body, out_shape=[shape, shape], in_specs=[SMEM] + [ANY] *...  31.6 us
    ppermute x23, starting transfers between devices, exchange(): return lax.ppermute(values, 'dp', [(i, i ^ bit) for i in range(count)])  19.9 us
    ppermute x4, waiting for transfers between devices, hop(): return lax.ppermute(rows_sent, 'section', [pair])  18.4 us
    pallas_call x8, Pallas kernels, halve(): pl.pallas_call(body, out_shape=jax.ShapeDtypeStruct((half,) + block, BF),...  16 us
    pallas_call x4, Pallas kernels, finish(): pl.pallas_call(body, out_shape=[jax.ShapeDtypeStruct(shape, F32) for shap...  9.15 us
  transfers between devices with their start and end apart: 28, of which 13 were waited for; matrix products, arithmetic and copies ran while one was open for 0% of the time, Pallas kernels for 37%

profile of v4, /device:TPU:0, one launch (start us, length us, event | category | flops | bytes accessed | tf_op | source)
XLA Modules:
  0.0 372.9 jit_solution(6157788968769278543)
XLA Ops:
  7.2 3.1 pack.1
  11.0 102.1 %all-gather.2.cloned.1.call-done.refs_3_.refs_4_.refs_2_ = bf16[768,12416]{1,0:T(8,128)(2,1)} async-done(((bf16[48,12416]{1,0:T(8,128)(2,1)}), bf16[768,12416]{1,0:T(8,128)(2,1)}) %all-gather.2.cloned.1.call-update) | async-done | bytes 19070992 | tf_op jit(solution)/shard_map/all_gather | solution.py:1146
  113.1 14.5 %layer_forward.2 = (bf16[2,2304,256]{2,1,0:T(8,128)(2,1)}, bf16[2,256,2304]{2,1,0:T(8,128)(2,1)}, bf16[2,12,256,256]{3,2,1,0:T(8,128)(2,1)}, f32[2,256,768]{2,1,...) custom-call(s32[2]{0:T(128)} %pad_add_fusion.refs_0_, ...), custom_call_target="tpu_custom_call" | custom-call | flops 5000000000 | bytes 25000000 | tf_op jit(solution)/shard_map/layer_forward/pallas_call | solution.py:544
  127.6 2.1 collective-permute-start.1
  129.7 14.7 %layer_forward.3 = (bf16[2,2304,256]{2,1,0:T(8,128)(2,1)}, bf16[2,256,2304]{2,1,0:T(8,128)(2,1)}, bf16[2,12,256,256]{3,2,1,0:T(8,128)(2,1)}, f32[2,256,768]{2,1,...) custom-call(s32[2]{0:T(128)} %pad_add_fusion.refs_0_, ...), custom_call_target="tpu_custom_call", output_to_operand_aliasing={{0}: (5, {}), {1}: (6, {}), {2}: (7, {}), {3}: (8, {}), {4}... | custom-call | flops 5000000000 | bytes 25000000 | tf_op jit(solution)/shard_map/layer_forward/pallas_call | solution.py:544
  144.4 2.0 collective-permute-start
  146.4 10.2 %layer_both_ways.2 = (bf16[2,2304,256]{2,1,0:T(8,128)(2,1)}, bf16[2,256,768]{2,1,0:T(8,128)(2,1)}, bf16[3888,256]{1,0:T(8,128)(2,1)}, bf16[256,3072]{1,0:T(8,128...) custom-call(s32[2]{0:T(128)} %pad_add_fusion.refs_0_, ...), custom_call_target="tpu_custom_call", output_to_operand_aliasing={{0}: (6, {}), {1}: (7, {})} | custom-call | flops 130000003072 | bytes 650000000 | tf_op jit(solution)/shard_map/layer_both_ways/pallas_call | solution.py:544
  156.7 1.3 collective-permute-start.4
  158.0 13.0 %layer_both_ways.3 = (bf16[2,2304,256]{2,1,0:T(8,128)(2,1)}, bf16[2,256,768]{2,1,0:T(8,128)(2,1)}, bf16[3888,256]{1,0:T(8,128)(2,1)}, bf16[256,3072]{1,0:T(8,128...) custom-call(s32[2]{0:T(128)} %pad_add_fusion.refs_0_, ...), custom_call_target="tpu_custom_call", output_to_operand_aliasing={{0}: (6, {}), {1}: (7, {}), {7}: (8, {})} | custom-call | flops 130000003072 | bytes 650000000 | tf_op jit(solution)/shard_map/layer_both_ways/pallas_call | solution.py:544
  171.3 1.3 collective-permute-start.2
  172.6 7.5 %collective-permute-done.4.refs_1_ = bf16[256,768]{1,0:T(8,128)(2,1)} collective-permute-done((bf16[256,768]{1,0:T(8,128)(2,1)}, bf16[256,768]{1,0:T(8,128)(2,1)}, u32[]{:S(2)}, u32[]{:S(2)}) %collective-permute-start.4) | collective-permute-done | bytes 393248 | tf_op jit(solution)/shard_map/ppermute | solution.py:1154
  180.1 20.4 %layer_backward.1 = (bf16[3888,256]{1,0:T(8,128)(2,1)}, bf16[256,3072]{1,0:T(8,128)(2,1)}, bf16[256,3072]{1,0:T(8,128)(2,1)}, bf16[256,1536]{1,0:T(8,128)(2,1)},...) custom-call(s32[2]{0:T(128)} %pad_add_fusion.refs_0_, ...), custom_call_target="tpu_custom_call", output_to_operand_aliasing={{0}: (10, {}), {1}: (11, {}), {2}: (12, {}), {3}: (13, {}),... | custom-call | flops 80000000000 | bytes 400000000 | tf_op jit(solution)/shard_map/layer_backward/pallas_call | solution.py:544
  200.6 10.9 %collective-permute-done.2.refs_1_ = bf16[256,768]{1,0:T(8,128)(2,1)} collective-permute-done((bf16[256,768]{1,0:T(8,128)(2,1)}, bf16[256,768]{1,0:T(8,128)(2,1)}, u32[]{:S(2)}, u32[]{:S(2)}) %collective-permute-start.2) | collective-permute-done | bytes 393248 | tf_op jit(solution)/shard_map/ppermute | solution.py:1154
  211.5 14.3 %backward_hidden.1 = (bf16[3888,256]{1,0:T(8,128)(2,1)}, bf16[256,3072]{1,0:T(8,128)(2,1)}, bf16[256,3072]{1,0:T(8,128)(2,1)}, f32[256,768]{1,0:T(8,128)}) custom-call(s32[2]{0:T(128)} %pad_add_fusion.refs_0_, bf16[256,768]{1,0:T(8,128)(2,1)} %collective-permute-done.2.refs_1_, ...), custom_call_target="tpu_custom_call", output_to_operand_aliasing={{0}: (8, {}), {1}: (9, {}), {2}: (10, {})} | custom-call | flops 60000002048 | bytes 300000000 | tf_op jit(solution)/shard_map/backward_hidden/pallas_call | solution.py:544
  227.0 3.2 collective-permute-done.10.refs_4_.refs_14_
  230.4 7.0 %weight_grad.4 = (bf16[4,192,768]{2,1,0:T(8,128)(2,1)}, bf16[4,192,768]{2,1,0:T(8,128)(2,1)}) custom-call(s32[2]{0:T(128)} %pad_add_fusion.refs_0_, bf16[3888,256]{1,0:T(8,128)(2,1)} %get-tuple-element.111.refs_1_.refs_11_, bf16[3888,256]{1,0:T(8,128)(2,1)} %get-tuple-element.112.refs_2_.refs_12_, bf16[3888,256]{1,0:T(8,128)(2,1)} %collective-permute-done.9.refs_3_.refs_13_, ...), custom_call_target="tpu_custom_call" | custom-call | flops 73600000000 | bytes 368000000 | tf_op jit(solution)/shard_map/weight_grad/pallas_call | solution.py:878
  237.8 1.4 collective-permute-done.8.refs_6_
  239.2 1.3 collective-permute-start.15
  240.5 7.9 %weight_grad.5 = (bf16[4,48,3072]{2,1,0:T(8,128)(2,1)}, bf16[4,48,3072]{2,1,0:T(8,128)(2,1)}) custom-call(s32[2]{0:T(128)} %pad_add_fusion.refs_0_, bf16[2,2304,256]{2,1,0:T(8,128)(2,1)} %get-tuple-element.93.refs_1_, bf16[2,2304,256]{2,1,0:T(8,128)(2,1)} %collective-permute-done.3.refs_11_.refs_2_, bf16[256,3072]{1,0:T(8,128)(2,1)} %get-tuple-element.109.refs_3_, ...), custom_call_target="tpu_custom_call" | custom-call | flops 73600000000 | bytes 368000000 | tf_op jit(solution)/shard_map/weight_grad/pallas_call | solution.py:878
  248.4 1.6 collective-permute-start.18
  249.9 7.9 %weight_grad.6 = (bf16[4,48,3072]{2,1,0:T(8,128)(2,1)}, bf16[4,48,3072]{2,1,0:T(8,128)(2,1)}) custom-call(s32[2]{0:T(128)} %pad_add_fusion.refs_0_, bf16[2,2304,256]{2,1,0:T(8,128)(2,1)} %get-tuple-element.93.refs_1_, bf16[2,2304,256]{2,1,0:T(8,128)(2,1)} %collective-permute-done.3.refs_11_.refs_2_, bf16[256,3072]{1,0:T(8,128)(2,1)} %get-tuple-element.107.refs_3_, ...), custom_call_target="tpu_custom_call" | custom-call | flops 73600000000 | bytes 368000000 | tf_op jit(solution)/shard_map/weight_grad/pallas_call | solution.py:878
  258.7 9.8 %backward_attention.1 = (bf16[256,1536]{1,0:T(8,128)(2,1)}, bf16[256,1536]{1,0:T(8,128)(2,1)}, f32[2,256,768]{2,1,0:T(8,128)}, bf16[256,768]{1,0:T(8,128)(2,1)}) custom-call(s32[2]{0:T(128)} %pad_add_fusion.refs_0_, f32[256,768]{1,0:T(8,128)} %get-tuple-element.94.refs_1_, ...), custom_call_target="tpu_custom_call", output_to_operand_aliasing={{0}: (5, {}), {1}: (6, {}), {2}: (7, {})} | custom-call | flops 92000002048 | bytes 460000000 | tf_op jit(solution)/shard_map/backward_attention/pallas_call | solution.py:544
  269.1 2.0 halve.8.refs_15_
  271.1 0.8 collective-permute-start.20
  272.3 8.9 %weight_grad.7 = (bf16[4,48,3200]{2,1,0:T(8,128)(2,1)}, bf16[4,48,3200]{2,1,0:T(8,128)(2,1)}) custom-call(s32[2]{0:T(128)} %pad_add_fusion.refs_0_, bf16[2,2304,256]{2,1,0:T(8,128)(2,1)} %get-tuple-element.93.refs_1_, bf16[2,2304,256]{2,1,0:T(8,128)(2,1)} %collective-permute-done.3.refs_11_.refs_2_, bf16[256,1536]{1,0:T(8,128)(2,1)} %get-tuple-element.116.refs_3_, ...), custom_call_target="tpu_custom_call" | custom-call | flops 73600000000 | bytes 368000000 | tf_op jit(solution)/shard_map/weight_grad/pallas_call | solution.py:878
  281.2 1.3 collective-permute-start.16
  282.5 2.0 halve.9.refs_2_
  285.4 8.2 %collective-permute-done.17.refs_1_ = bf16[4,48,3072]{2,1,0:T(8,128)(2,1)} collective-permute-done((bf16[4,48,3072]{2,1,0:T(8,128)(2,1)}, bf16[4,48,3072]{2,1,0:T(8,128)(2,1)}, u32[]{:S(2)}, u32[]{:S(2)}) %collective-permute-start.17) | collective-permute-done | bytes 1179680 | tf_op jit(solution)/shard_map/ppermute | solution.py:892
  293.6 2.1 halve.10.refs_3_
  295.7 1.6 collective-permute-start.19
  297.2 1.9 halve.11.refs_3_
  299.2 2.5 collective-permute-start.24
  301.6 14.5 %collective-permute-done.19.refs_2_ = bf16[2,48,3072]{2,1,0:T(8,128)(2,1)} collective-permute-done((bf16[2,48,3072]{2,1,0:T(8,128)(2,1)}, bf16[2,48,3072]{2,1,0:T(8,128)(2,1)}, u32[]{:S(2)}, u32[]{:S(2)}) %collective-permute-start.19) | collective-permute-done | bytes 589856 | tf_op jit(solution)/shard_map/ppermute | solution.py:892
  316.1 1.9 halve.12.refs_2_
  318.1 1.5 collective-permute-start.26
  320.0 2.1 halve.13.refs_4_
  322.0 2.1 collective-permute-start.21
  324.2 2.1 finish.5.refs_3_
  326.3 5.5 %collective-permute-done.23.refs_2_ = bf16[2,48,3072]{2,1,0:T(8,128)(2,1)} collective-permute-done((bf16[2,48,3072]{2,1,0:T(8,128)(2,1)}, bf16[2,48,3072]{2,1,0:T(8,128)(2,1)}, u32[]{:S(2)}, u32[]{:S(2)}) %collective-permute-start.23) | collective-permute-done | bytes 589856 | tf_op jit(solution)/shard_map/ppermute | solution.py:892
  331.8 1.9 halve.15.refs_4_
  333.7 2.5 collective-permute-start.25
  336.2 2.1 finish.6.refs_5_
  338.4 6.7 %collective-permute-done.21.refs_2_ = bf16[2,48,3200]{2,1,0:T(8,128)(2,1)} collective-permute-done((bf16[2,48,3200]{2,1,0:T(8,128)(2,1)}, bf16[2,48,3200]{2,1,0:T(8,128)(2,1)}, u32[]{:S(2)}, u32[]{:S(2)}) %collective-permute-start.21) | collective-permute-done | bytes 614432 | tf_op jit(solution)/shard_map/ppermute | solution.py:892
  345.1 2.0 halve.14.refs_4_
  347.6 9.4 %collective-permute-done.25.refs_3_ = bf16[1,48,3072]{2,1,0:T(8,128)(2,1)} collective-permute-done((bf16[1,48,3072]{2,1,0:T(8,128)(2,1)}, bf16[1,48,3072]{2,1,0:T(8,128)(2,1)}, u32[]{:S(2)}, u32[]{:S(2)}) %collective-permute-start.25) | collective-permute-done | bytes 294944 | tf_op jit(solution)/shard_map/ppermute | solution.py:892
  357.0 2.1 finish.7
  359.2 3.6 collective-permute-done.22.refs_3_
  362.8 2.8 finish.4
  (34 shorter events, 6.4 us)
Async XLA Ops:
  7.2 105.9 %all-gather.2.cloned.1.call-start = ((), (), s32[]{:S(2)}) async-start(), calls=%async_computation | async-start | bytes 20262912 | tf_op jit(solution)/shard_map/all_gather | solution.py:1146
  127.6 18.8 %collective-permute-start.1 = (bf16[256,768]{1,0:T(8,128)(2,1)}, bf16[256,768]{1,0:T(8,128)(2,1)}, u32[]{:S(2)}, u32[]{:S(2)}) collective-permute-start(bf16[256,768]{1,0:T(8,128)(2,1)} %get-tuple-element.78), channel_id=1, source_target_pairs={{0,16},{1,17},{2,18},{3,19},{4,20},{5,21},{6,22},{7,23},{8,24},{9,... | collective-permute-start | bytes 1179656 | tf_op jit(solution)/shard_map/ppermute | solution.py:1154
  144.4 13.6 %collective-permute-start = (bf16[256,768]{1,0:T(8,128)(2,1)}, bf16[256,768]{1,0:T(8,128)(2,1)}, u32[]{:S(2)}, u32[]{:S(2)}) collective-permute-start(bf16[256,768]{1,0:T(8,128)(2,1)} %get-tuple-element.77), channel_id=1, source_target_pairs={{0,16},{1,17},{2,18},{3,19},{4,20},{5,21},{6,22},{7,23},{8,24},{9,... | collective-permute-start | bytes 1179656 | tf_op jit(solution)/shard_map/ppermute | solution.py:1154
  156.7 23.4 %collective-permute-start.4 = (bf16[256,768]{1,0:T(8,128)(2,1)}, bf16[256,768]{1,0:T(8,128)(2,1)}, u32[]{:S(2)}, u32[]{:S(2)}) collective-permute-start(bf16[256,768]{1,0:T(8,128)(2,1)} %get-tuple-element.99), channel_id=1, source_target_pairs={{16,0},{17,1},{18,2},{19,3},{20,4},{21,5},{22,6},{23,7},{24,8},{25... | collective-permute-start | bytes 1179656 | tf_op jit(solution)/shard_map/ppermute | solution.py:1154
  171.0 40.5 %collective-permute-start.3 = (bf16[2,2304,256]{2,1,0:T(8,128)(2,1)}, bf16[2,2304,256]{2,1,0:T(8,128)(2,1)}, u32[]{:S(2)}, u32[]{:S(2)}) collective-permute-start(bf16[2,2304,256]{2,1,0:T(8,128)(2,1)} %get-tuple-element.93.refs_1_), channel_id=1, source_target_pairs={{0,1},{1,0},{2,3},{3,2},{4,5},{5,4},{6,7},{7,6},{8,9},{9,8},{10,11... | collective-permute-start | bytes 7077896 | tf_op jit(solution)/shard_map/ppermute | solution.py:892
  171.3 40.2 %collective-permute-start.2 = (bf16[256,768]{1,0:T(8,128)(2,1)}, bf16[256,768]{1,0:T(8,128)(2,1)}, u32[]{:S(2)}, u32[]{:S(2)}) collective-permute-start(bf16[256,768]{1,0:T(8,128)(2,1)} %get-tuple-element.85), channel_id=1, source_target_pairs={{16,0},{17,1},{18,2},{19,3},{20,4},{21,5},{22,6},{23,7},{24,8},{25... | collective-permute-start | bytes 1179656 | tf_op jit(solution)/shard_map/ppermute | solution.py:1154
  200.5 26.4 %collective-permute-start.9 = (bf16[3888,256]{1,0:T(8,128)(2,1)}, bf16[3888,256]{1,0:T(8,128)(2,1)}, u32[]{:S(2)}, u32[]{:S(2)}) collective-permute-start(bf16[3888,256]{1,0:T(8,128)(2,1)} %get-tuple-element.111.refs_1_.refs_11_), channel_id=1, source_target_pairs={{0,1},{1,0},{2,3},{3,2},{4,5},{5,4},{6,7},{7,6},{8,9},{9,8},{10,11... | collective-permute-start | bytes 5971976 | tf_op jit(solution)/shard_map/ppermute | solution.py:892
  225.8 4.4 %collective-permute-start.10 = (bf16[3888,256]{1,0:T(8,128)(2,1)}, bf16[3888,256]{1,0:T(8,128)(2,1)}, u32[]{:S(2)}, u32[]{:S(2)}) collective-permute-start(bf16[3888,256]{1,0:T(8,128)(2,1)} %get-tuple-element.112.refs_2_.refs_12_), channel_id=1, source_target_pairs={{0,1},{1,0},{2,3},{3,2},{4,5},{5,4},{6,7},{7,6},{8,9},{9,8},{10,11... | collective-permute-start | bytes 5971976 | tf_op jit(solution)/shard_map/ppermute | solution.py:892
  225.9 11.5 %collective-permute-start.7 = (bf16[256,3072]{1,0:T(8,128)(2,1)}, bf16[256,3072]{1,0:T(8,128)(2,1)}, u32[]{:S(2)}, u32[]{:S(2)}) collective-permute-start(bf16[256,3072]{1,0:T(8,128)(2,1)} %get-tuple-element.109.refs_3_), channel_id=1, source_target_pairs={{0,1},{1,0},{2,3},{3,2},{4,5},{5,4},{6,7},{7,6},{8,9},{9,8},{10,11... | collective-permute-start | bytes 4718600 | tf_op jit(solution)/shard_map/ppermute | solution.py:892
  226.4 22.0 %collective-permute-start.5 = (bf16[256,3072]{1,0:T(8,128)(2,1)}, bf16[256,3072]{1,0:T(8,128)(2,1)}, u32[]{:S(2)}, u32[]{:S(2)}) collective-permute-start(bf16[256,3072]{1,0:T(8,128)(2,1)} %get-tuple-element.107.refs_3_), channel_id=1, source_target_pairs={{0,1},{1,0},{2,3},{3,2},{4,5},{5,4},{6,7},{7,6},{8,9},{9,8},{10,11... | collective-permute-start | bytes 4718600 | tf_op jit(solution)/shard_map/ppermute | solution.py:892
  226.5 32.2 %collective-permute-start.11 = (bf16[256,1536]{1,0:T(8,128)(2,1)}, bf16[256,1536]{1,0:T(8,128)(2,1)}, u32[]{:S(2)}, u32[]{:S(2)}) collective-permute-start(bf16[256,1536]{1,0:T(8,128)(2,1)} %get-tuple-element.116.refs_3_), channel_id=1, source_target_pairs={{0,1},{1,0},{2,3},{3,2},{4,5},{5,4},{6,7},{7,6},{8,9},{9,8},{10,11... | collective-permute-start | bytes 2359304 | tf_op jit(solution)/shard_map/ppermute | solution.py:892
  226.9 31.8 %collective-permute-start.12 = (bf16[256,1536]{1,0:T(8,128)(2,1)}, bf16[256,1536]{1,0:T(8,128)(2,1)}, u32[]{:S(2)}, u32[]{:S(2)}) collective-permute-start(bf16[256,1536]{1,0:T(8,128)(2,1)} %get-tuple-element.117.refs_7_), channel_id=1, source_target_pairs={{0,1},{1,0},{2,3},{3,2},{4,5},{5,4},{6,7},{7,6},{8,9},{9,8},{10,11... | collective-permute-start | bytes 2359304 | tf_op jit(solution)/shard_map/ppermute | solution.py:892
  230.2 9.0 %collective-permute-start.8 = (bf16[256,3072]{1,0:T(8,128)(2,1)}, bf16[256,3072]{1,0:T(8,128)(2,1)}, u32[]{:S(2)}, u32[]{:S(2)}) collective-permute-start(bf16[256,3072]{1,0:T(8,128)(2,1)} %get-tuple-element.110.refs_4_), channel_id=1, source_target_pairs={{0,1},{1,0},{2,3},{3,2},{4,5},{5,4},{6,7},{7,6},{8,9},{9,8},{10,11... | collective-permute-start | bytes 4718600 | tf_op jit(solution)/shard_map/ppermute | solution.py:892
  237.4 12.5 %collective-permute-start.6 = (bf16[256,3072]{1,0:T(8,128)(2,1)}, bf16[256,3072]{1,0:T(8,128)(2,1)}, u32[]{:S(2)}, u32[]{:S(2)}) collective-permute-start(bf16[256,3072]{1,0:T(8,128)(2,1)} %get-tuple-element.108.refs_4_), channel_id=1, source_target_pairs={{0,1},{1,0},{2,3},{3,2},{4,5},{5,4},{6,7},{7,6},{8,9},{9,8},{10,11... | collective-permute-start | bytes 4718600 | tf_op jit(solution)/shard_map/ppermute | solution.py:892
  239.2 29.8 %collective-permute-start.15 = (bf16[4,192,768]{2,1,0:T(8,128)(2,1)}, bf16[4,192,768]{2,1,0:T(8,128)(2,1)}, u32[]{:S(2)}, u32[]{:S(2)}) collective-permute-start(bf16[4,192,768]{2,1,0:T(8,128)(2,1)} %get-tuple-element.113.refs_7_), channel_id=1, source_target_pairs={{0,2},{1,3},{2,0},{3,1},{4,6},{5,7},{6,4},{7,5},{8,10},{9,11},{10,... | collective-permute-start | bytes 3538952 | tf_op jit(solution)/shard_map/ppermute | solution.py:892
  248.4 34.2 %collective-permute-start.18 = (bf16[4,48,3072]{2,1,0:T(8,128)(2,1)}, bf16[4,48,3072]{2,1,0:T(8,128)(2,1)}, u32[]{:S(2)}, u32[]{:S(2)}) collective-permute-start(bf16[4,48,3072]{2,1,0:T(8,128)(2,1)} %get-tuple-element.114.refs_7_), channel_id=1, source_target_pairs={{0,4},{1,5},{2,6},{3,7},{4,0},{5,1},{6,2},{7,3},{8,12},{9,13},{10,... | collective-permute-start | bytes 3538952 | tf_op jit(solution)/shard_map/ppermute | solution.py:892
  257.8 35.8 %collective-permute-start.17 = (bf16[4,48,3072]{2,1,0:T(8,128)(2,1)}, bf16[4,48,3072]{2,1,0:T(8,128)(2,1)}, u32[]{:S(2)}, u32[]{:S(2)}) collective-permute-start(bf16[4,48,3072]{2,1,0:T(8,128)(2,1)} %get-tuple-element.115.refs_8_), channel_id=1, source_target_pairs={{0,2},{1,3},{2,0},{3,1},{4,6},{5,7},{6,4},{7,5},{8,10},{9,11},{10,... | collective-permute-start | bytes 3538952 | tf_op jit(solution)/shard_map/ppermute | solution.py:892
  268.5 3.5 collective-permute-start.13
  268.6 3.7 %collective-permute-start.14 = (bf16[256,1536]{1,0:T(8,128)(2,1)}, bf16[256,1536]{1,0:T(8,128)(2,1)}, u32[]{:S(2)}, u32[]{:S(2)}) collective-permute-start(bf16[256,1536]{1,0:T(8,128)(2,1)} %get-tuple-element.120.refs_8_), channel_id=1, source_target_pairs={{0,1},{1,0},{2,3},{3,2},{4,5},{5,4},{6,7},{7,6},{8,9},{9,8},{10,11... | collective-permute-start | bytes 2359304 | tf_op jit(solution)/shard_map/ppermute | solution.py:892
  271.1 26.1 %collective-permute-start.20 = (bf16[2,192,768]{2,1,0:T(8,128)(2,1)}, bf16[2,192,768]{2,1,0:T(8,128)(2,1)}, u32[]{:S(2)}, u32[]{:S(2)}) collective-permute-start(bf16[2,192,768]{2,1,0:T(8,128)(2,1)} %halve.8.refs_15_), channel_id=1, source_target_pairs={{0,4},{1,5},{2,6},{3,7},{4,0},{5,1},{6,2},{7,3},{8,12},{9,13},{10,... | collective-permute-start | bytes 1769480 | tf_op jit(solution)/shard_map/ppermute | solution.py:892
  281.2 38.8 %collective-permute-start.16 = (bf16[4,48,3200]{2,1,0:T(8,128)(2,1)}, bf16[4,48,3200]{2,1,0:T(8,128)(2,1)}, u32[]{:S(2)}, u32[]{:S(2)}) collective-permute-start(bf16[4,48,3200]{2,1,0:T(8,128)(2,1)} %get-tuple-element.123.refs_2_), channel_id=1, source_target_pairs={{0,2},{1,3},{2,0},{3,1},{4,6},{5,7},{6,4},{7,5},{8,10},{9,11},{10,... | collective-permute-start | bytes 3686408 | tf_op jit(solution)/shard_map/ppermute | solution.py:892
  284.6 47.2 %collective-permute-start.23 = (bf16[2,48,3072]{2,1,0:T(8,128)(2,1)}, bf16[2,48,3072]{2,1,0:T(8,128)(2,1)}, u32[]{:S(2)}, u32[]{:S(2)}) collective-permute-start(bf16[2,48,3072]{2,1,0:T(8,128)(2,1)} %halve.9.refs_2_), channel_id=1, source_target_pairs={{0,2},{1,3},{2,0},{3,1},{4,6},{5,7},{6,4},{7,5},{8,10},{9,11},{10,... | collective-permute-start | bytes 1769480 | tf_op jit(solution)/shard_map/ppermute | solution.py:892
  295.7 20.4 %collective-permute-start.19 = (bf16[2,48,3072]{2,1,0:T(8,128)(2,1)}, bf16[2,48,3072]{2,1,0:T(8,128)(2,1)}, u32[]{:S(2)}, u32[]{:S(2)}) collective-permute-start(bf16[2,48,3072]{2,1,0:T(8,128)(2,1)} %halve.10.refs_3_), channel_id=1, source_target_pairs={{0,4},{1,5},{2,6},{3,7},{4,0},{5,1},{6,2},{7,3},{8,12},{9,13},{10,... | collective-permute-start | bytes 1769480 | tf_op jit(solution)/shard_map/ppermute | solution.py:892
  299.2 25.0 %collective-permute-start.24 = (bf16[1,192,768]{2,1,0:T(8,128)(2,1)}, bf16[1,192,768]{2,1,0:T(8,128)(2,1)}, u32[]{:S(2)}, u32[]{:S(2)}) collective-permute-start(bf16[1,192,768]{2,1,0:T(8,128)(2,1)} %halve.11.refs_3_), channel_id=1, source_target_pairs={{0,8},{1,9},{2,10},{3,11},{4,12},{5,13},{6,14},{7,15},{8,0},{9,1},... | collective-permute-start | bytes 884744 | tf_op jit(solution)/shard_map/ppermute | solution.py:892
  318.1 18.1 %collective-permute-start.26 = (bf16[1,48,3072]{2,1,0:T(8,128)(2,1)}, bf16[1,48,3072]{2,1,0:T(8,128)(2,1)}, u32[]{:S(2)}, u32[]{:S(2)}) collective-permute-start(bf16[1,48,3072]{2,1,0:T(8,128)(2,1)} %halve.12.refs_2_), channel_id=1, source_target_pairs={{0,8},{1,9},{2,10},{3,11},{4,12},{5,13},{6,14},{7,15},{8,0},{9,1},... | collective-permute-start | bytes 884744 | tf_op jit(solution)/shard_map/ppermute | solution.py:892
  322.0 23.1 %collective-permute-start.21 = (bf16[2,48,3200]{2,1,0:T(8,128)(2,1)}, bf16[2,48,3200]{2,1,0:T(8,128)(2,1)}, u32[]{:S(2)}, u32[]{:S(2)}) collective-permute-start(bf16[2,48,3200]{2,1,0:T(8,128)(2,1)} %halve.13.refs_4_), channel_id=1, source_target_pairs={{0,4},{1,5},{2,6},{3,7},{4,0},{5,1},{6,2},{7,3},{8,12},{9,13},{10,... | collective-permute-start | bytes 1843208 | tf_op jit(solution)/shard_map/ppermute | solution.py:892
  333.7 23.3 %collective-permute-start.25 = (bf16[1,48,3072]{2,1,0:T(8,128)(2,1)}, bf16[1,48,3072]{2,1,0:T(8,128)(2,1)}, u32[]{:S(2)}, u32[]{:S(2)}) collective-permute-start(bf16[1,48,3072]{2,1,0:T(8,128)(2,1)} %halve.15.refs_4_), channel_id=1, source_target_pairs={{0,8},{1,9},{2,10},{3,11},{4,12},{5,13},{6,14},{7,15},{8,0},{9,1},... | collective-permute-start | bytes 884744 | tf_op jit(solution)/shard_map/ppermute | solution.py:892
  347.1 15.7 %collective-permute-start.22 = (bf16[1,48,3200]{2,1,0:T(8,128)(2,1)}, bf16[1,48,3200]{2,1,0:T(8,128)(2,1)}, u32[]{:S(2)}, u32[]{:S(2)}) collective-permute-start(bf16[1,48,3200]{2,1,0:T(8,128)(2,1)} %halve.14.refs_4_), channel_id=1, source_target_pairs={{0,8},{1,9},{2,10},{3,11},{4,12},{5,13},{6,14},{7,15},{8,0},{9,1},... | collective-permute-start | bytes 921608 | tf_op jit(solution)/shard_map/ppermute | solution.py:892
Sparse Core Ops, SparseCore 0:
  10.5 102.5 all-gather.1

commit v5 on v4

--- a/solution.py
+++ b/solution.py
@@ -83,7 +83,7 @@
     ids, lengths, given, wide, down,
     left_out, qkv_out, probs_out, n1_out, h1_out, n2_out, inv_out, layer_out, hop_out,
     w_qkv, w_out, w_gu, w_down, x, qkv, probs, context, n1, h1, n2, inv, result, norm, left,
-    w_sem, o_sem, i_sem, *, micro, direct, fused=False,
+    w_sem, o_sem, i_sem, *, micro, direct, fused=False, ready=None,
 ):
     window = ids[1]
     copies = {}
@@ -179,7 +179,11 @@
         copies["up", j].wait()
         gate = matmul(low_hidden, w_gu[j])
         rise = matmul(low_hidden, w_gu[CHUNKS + j])
-        gated = (gate * (0.5 * (1.0 + lax.erf(gate * ROOT_HALF))) * rise).astype(BF)
+        cdf = 0.5 * (1.0 + lax.erf(gate * ROOT_HALF))
+        bent = gate * cdf
+        gated = (bent * rise).astype(BF)
+        if ready is not None:
+            ready(j, gate, rise, cdf, bent, gated)
         for q in range(4):
             copies["down", j, q].wait()
         hidden = hidden + matmul(gated, w_down[j].reshape(CHUNK, D))
@@ -195,6 +199,37 @@
         return flushed
     for copy in flushed:
         copy.wait()
+
+
+def forward_ready(
+    ids, lengths, given, wide, down,
+    left_out, qkv_out, probs_out, n1_out, h1_out, n2_out, inv_out, layer_out,
+    hidden_out, slope_out, bent_out, hop_out, *scratch, micro, direct,
+):
+    gated_turned, slopes, bents, r_sem = scratch[-4:]
+    stores = []
+
+    def ready(j, gate, rise, cdf, bent, gated):
+        cols = pl.ds(j * CHUNK, CHUNK)
+        density = jnp.exp(-0.5 * gate * gate) * INV_SQRT_2PI
+        slopes[:, cols] = rise * (cdf + gate * density)
+        bents[:, cols] = bent
+        gated_turned[cols] = gated.T
+        made = (
+            (gated_turned.at[cols], hidden_out.at[cols]),
+            (slopes.at[:, cols], slope_out.at[:, cols]),
+            (bents.at[:, cols], bent_out.at[:, cols]),
+        )
+        for source, target in made:
+            stores.append(begin(source, target, r_sem.at[len(stores)]))
+
+    forward_window(
+        ids, lengths, given, wide, down,
+        left_out, qkv_out, probs_out, n1_out, h1_out, n2_out, inv_out, layer_out, hop_out,
+        *scratch[:-4], micro=micro, direct=direct, ready=ready,
+    )
+    for store in stores:
+        store.wait()
 
 
 class InPlace:
@@ -435,18 +470,87 @@
 
 
 def backward_first_half(
-    ids, given, wide, down, n1_in, h1_in, n2_in, inv_in,
+    ids, given, wide, down, n1_in, n2_in, inv_in, slope_in, bent_in,
     hidden_out, gate_out, up_out, half_out,
-    w_gu, w_down, upstream, n1, h1, n2, inv, norm, gated, down_grad, gu_grad, norm_grad, low_norm,
-    half, w_sem, o_sem, i_sem, *, micro, direct,
+    w_gu, w_down, upstream, n1, n2, inv, norm, slopes, bents, down_grad, gu_grad, norm_grad,
+    low_norm, half, w_sem, o_sem, i_sem, *, micro, direct,
 ):
-    grad_one, flushed = backward_hidden(
-        ids, given, wide, down, n1_in, h1_in, n2_in, inv_in, hidden_out, gate_out, up_out,
-        w_gu, w_down, upstream, n1, h1, n2, inv, norm, gated, down_grad, gu_grad, norm_grad,
-        low_norm, w_sem, o_sem, i_sem, micro=micro, direct=direct, ahead=lambda: None,
-    )
+    arriving = begin(own_window(given, micro), upstream, i_sem.at[0])
+    small = [
+        begin(n2_in.at[micro], n2, i_sem.at[1]),
+        begin(inv_in.at[micro], inv, i_sem.at[2]),
+        begin(wide.at[:, pl.ds(COL_NORM, 128)], norm, i_sem.at[3]),
+    ]
+    copies = {}
+
+    def fetch_chunk(j):
+        owners = down.at[pl.ds(4 * j, 4)]
+        parts = []
+        for q in range(4):
+            source = owners.at[:, :, pl.ds(COL_DOWN + D * q, D)] if direct else owners.at[:, q]
+            parts.append(begin(source, w_down.at[j, :, q], w_sem.at[2 * CHUNKS + 4 * j + q]))
+        cols = pl.ds(j * CHUNK, CHUNK)
+        parts.append(begin(slope_in.at[:, cols], slopes.at[:, cols], i_sem.at[5 + j]))
+        parts.append(begin(bent_in.at[:, cols], bents.at[:, cols], i_sem.at[5 + CHUNKS + j]))
+        copies["first", j] = parts
+        gate = wide.at[:, pl.ds(COL_GU + j * CHUNK, CHUNK)]
+        rise = wide.at[:, pl.ds(COL_GU + FF + j * CHUNK, CHUNK)]
+        copies["second", j] = [
+            begin(gate, w_gu.at[j], w_sem.at[j]),
+            begin(rise, w_gu.at[CHUNKS + j], w_sem.at[CHUNKS + j]),
+        ]
+
+    fetch_chunk(0)
+    fetch_chunk(1)
+    flushed = []
+
+    def flush(source, target):
+        flushed.append(begin(source, target, o_sem.at[len(flushed)]))
+
+    arriving.wait()
+    for copy in small:
+        copy.wait()
+    params = norm[...].astype(F32).T
+    up = upstream[...].astype(F32)
+    normed = n2[...]
+    grad_two = norm_backward(up, normed, inv[:, HEAD : HEAD + 1], params[1:2])
+    norm_grad[...] = jnp.zeros_like(norm_grad)
+    norm_grad[1:2, :] = jnp.sum(up * normed, axis=0, keepdims=True)
+    norm_grad[3:4, :] = jnp.sum(up, axis=0, keepdims=True)
+    low_grad = grad_two.astype(BF)
+    down_grad[...] = low_grad.T
+    flush(down_grad, hidden_out.at[pl.ds(FF, D)])
+    total = grad_two
+    for j in range(CHUNKS):
+        for copy in copies["first", j]:
+            copy.wait()
+        if j + 2 < CHUNKS:
+            fetch_chunk(j + 2)
+        if j + 1 == CHUNKS:
+            first_norm = begin(n1_in.at[micro], n1, i_sem.at[4])
+        gated_grad = matmul(low_grad, w_down[j].reshape(CHUNK, D), NT)
+        cols = pl.ds(j * CHUNK, CHUNK)
+        late_cols = pl.ds(FF + j * CHUNK, CHUNK)
+        gate_grad = (gated_grad * slopes[:, cols]).astype(BF)
+        rise_grad = (gated_grad * bents[:, cols]).astype(BF)
+        gu_grad[:, cols] = gate_grad
+        gu_grad[:, late_cols] = rise_grad
+        flush(gu_grad.at[:, cols], gate_out.at[:, cols])
+        flush(gu_grad.at[:, late_cols], up_out.at[:, cols])
+        for copy in copies["second", j]:
+            copy.wait()
+        total = total + matmul(gate_grad, w_gu[j], NT) + matmul(rise_grad, w_gu[CHUNKS + j], NT)
+    first_norm.wait()
+    normed = n1[...]
+    grad_one = norm_backward(total, normed, inv[:, 0:1], params[0:1])
+    norm_grad[0:1, :] = jnp.sum(total * normed, axis=0, keepdims=True)
+    norm_grad[2:3, :] = jnp.sum(total, axis=0, keepdims=True)
+    low_norm[...] = norm_grad[...].astype(BF)
+    for k in range(3):
+        source = low_norm.at[:, pl.ds(SEQ * k, SEQ)]
+        flush(source, hidden_out.at[pl.ds(FF + D + 16 * k, 16)])
     half[...] = grad_one
-    flushed.append(begin(half, half_out, o_sem.at[HIDDEN_STORES]))
+    flush(half, half_out)
     for copy in flushed:
         copy.wait()
 
@@ -482,6 +586,7 @@
     (True, SEQ, D, BF),
 )
 HIDDEN_KEPT = ((False, FF + D + 48, SEQ, BF), (False, SEQ, FF, BF), (False, SEQ, FF, BF))
+READY_KEPT = (HIDDEN_KEPT[0], (False, SEQ, FF, F32), (False, SEQ, FF, F32))
 ATTENTION_KEPT = ((False, SEQ, 2 * D, BF), (False, SEQ, 2 * D, BF), (True, SEQ, D, F32))
 HIDDEN_STORES = 3 * CHUNKS + 4
 HIDDEN_WEIGHTS = (
@@ -556,7 +661,7 @@
     )(*operands)
 
 
-def forward_call(owner, micro, direct, ids, lengths, given, wide, down, before):
+def forward_call(owner, micro, direct, ids, lengths, given, wide, down, before, ready=False):
     scratch = (
         ATTENTION_WEIGHTS
         + HIDDEN_WEIGHTS
@@ -577,13 +682,22 @@
             DMA((2,)),
         )
     )
+    body, kept = forward_window, FORWARD_KEPT
+    if ready:
+        body, kept = forward_ready, FORWARD_KEPT + READY_KEPT
+        scratch += (
+            pltpu.VMEM((FF, SEQ), BF),
+            pltpu.VMEM((SEQ, FF), F32),
+            pltpu.VMEM((SEQ, FF), F32),
+            DMA((3 * CHUNKS,)),
+        )
     return call_window(
-        functools.partial(forward_window, micro=micro, direct=direct),
+        functools.partial(body, micro=micro, direct=direct),
         "layer_forward",
         owner,
         micro,
         (ids, lengths, given, wide, down),
-        FORWARD_KEPT,
+        kept,
         BF,
         before,
         scratch,
@@ -650,12 +764,23 @@
         HIDDEN_KEPT,
         F32,
         before,
-        HIDDEN_SCRATCH
+        HIDDEN_WEIGHTS
         + (
+            pltpu.VMEM((SEQ, D), BF),
+            pltpu.VMEM((SEQ, D), F32),
+            pltpu.VMEM((SEQ, D), F32),
+            pltpu.VMEM((SEQ, 128), F32),
+            pltpu.VMEM((D, 128), BF),
+            pltpu.VMEM((SEQ, FF), F32),
+            pltpu.VMEM((SEQ, FF), F32),
+            pltpu.VMEM((D, SEQ), BF),
+            pltpu.VMEM((SEQ, 2 * FF), BF),
+            pltpu.VMEM((16, D), F32),
+            pltpu.VMEM((16, D), BF),
             pltpu.VMEM((SEQ, D), F32),
             DMA((6 * CHUNKS,)),
-            DMA((HIDDEN_STORES + 1,)),
-            DMA((6,)),
+            DMA((2 * CHUNKS + 5,)),
+            DMA((5 + 2 * CHUNKS,)),
         ),
         60_000_000_000,
         1,
@@ -1153,14 +1278,14 @@
     def hop(rows_sent, pair):
         return lax.ppermute(rows_sent, "section", [pair])
 
-    def forward(owner, micro, given, before):
+    def forward(owner, micro, given, before, ready=False):
         return forward_call(
-            owner, micro, direct, ids, lengths, given, wide, down, before
+            owner, micro, direct, ids, lengths, given, wide, down, before, ready
         )
 
     *kept, sent = forward(0, 0, tokens, [None] * len(FORWARD_KEPT))
     arrived_first = hop(sent, (0, 1))
-    *kept, sent = forward(0, 1, tokens, kept)
+    *kept, hidden_second, slopes, bents, sent = forward(0, 1, tokens, kept + [None] * 3, True)
     arrived_second = hop(sent, (0, 1))
     left, qkv, probs, n1, h1, n2, inv, layer_out = kept
     stash = (qkv, probs, n1, h1, n2, inv)
@@ -1178,7 +1303,7 @@
     )
     arrived_first = hop(sent, (1, 0))
     left, layer_out, *second, input_grads, sent = both_passes(
-        1, arrived_second, [left, layer_out] + [None] * 5 + [input_grads]
+        1, arrived_second, [left, layer_out, hidden_second] + [None] * 4 + [input_grads]
     )
     arrived_second = hop(sent, (1, 0))
     left_other = exchange(left, BIT_CORE) if direct else left
@@ -1189,7 +1314,7 @@
         first = [both(array) for array in first]
     gates = (left_other,) if direct else ()
     *hidden, half = first_half_call(
-        0, 1, direct, ids, arrived_second, wide, down, (n1, h1, n2, inv), second[:3], gates
+        0, 1, direct, ids, arrived_second, wide, down, (n1, n2, inv, slopes, bents), second[:3], gates
     )
 
     def second_half(gates):

time: 380 us -> 377 us (level)
  transfers between devices with their start and end apart: 28 -> 28, of which waited for: 13 -> 13; matrix products, arithmetic and copies ran while one was open for 0% -> 0% of each run, Pallas kernels for 37% -> 36%
where the time goes in v5:
time: 377 us; the launch traced here: 370 us
  waiting for transfers between devices  173 us (46%)
  Pallas kernels  155 us (41%)
  starting transfers between devices  26.7 us (7%)
  between operations  14.5 us (4%)
    all_gather x1, waiting for transfers between devices, shards(): wide = lax.all_gather(packed, 'dp', axis=0, tiled=True)  102 us
    pallas_call x7, Pallas kernels, call_window(): pl.pallas_call(kernel, out_shape=shapes, in_specs=[SMEM] * small + [ANY]...  95.4 us
    ppermute x23, waiting for transfers between devices, exchange(): return lax.ppermute(values, 'dp', [(i, i ^ bit) for i in range(count)])  53.7 us
    pallas_call x4, Pallas kernels, weight_grad(): pl.pallas_call(body, out_shape=[shape, shape], in_specs=[SMEM] + [ANY] *...  31.4 us
    ppermute x23, starting transfers between devices, exchange(): return lax.ppermute(values, 'dp', [(i, i ^ bit) for i in range(count)])  20 us
    ppermute x4, waiting for transfers between devices, hop(): return lax.ppermute(rows_sent, 'section', [pair])  17.3 us
    pallas_call x8, Pallas kernels, halve(): pl.pallas_call(body, out_shape=jax.ShapeDtypeStruct((half,) + block, BF),...  16 us
    pallas_call x4, Pallas kernels, finish(): pl.pallas_call(body, out_shape=[jax.ShapeDtypeStruct(shape, F32) for shap...  9.15 us
  transfers between devices with their start and end apart: 28, of which 13 were waited for; matrix products, arithmetic and copies ran while one was open for 0% of the time, Pallas kernels for 36%

profile of v5, /device:TPU:0, one launch (start us, length us, event | category | flops | bytes accessed | tf_op | source)
XLA Modules:
  0.0 369.9 jit_solution(6010646518263352417)
XLA Ops:
  7.2 3.1 pack.1
  11.0 102.1 %all-gather.2.cloned.1.call-done.refs_3_.refs_4_.refs_2_ = bf16[768,12416]{1,0:T(8,128)(2,1)} async-done(((bf16[48,12416]{1,0:T(8,128)(2,1)}), bf16[768,12416]{1,0:T(8,128)(2,1)}) %all-gather.2.cloned.1.call-update) | async-done | bytes 19070992 | tf_op jit(solution)/shard_map/all_gather | solution.py:1271
  113.1 14.5 %layer_forward.2 = (bf16[2,2304,256]{2,1,0:T(8,128)(2,1)}, bf16[2,256,2304]{2,1,0:T(8,128)(2,1)}, bf16[2,12,256,256]{3,2,1,0:T(8,128)(2,1)}, f32[2,256,768]{2,1,...) custom-call(s32[2]{0:T(128)} %pad_add_fusion.refs_0_, ...), custom_call_target="tpu_custom_call" | custom-call | flops 5000000000 | bytes 25000000 | tf_op jit(solution)/shard_map/layer_forward/pallas_call | solution.py:649
  127.6 2.0 collective-permute-start.1
  129.6 15.5 %layer_forward.3 = (bf16[2,2304,256]{2,1,0:T(8,128)(2,1)}, bf16[2,256,2304]{2,1,0:T(8,128)(2,1)}, bf16[2,12,256,256]{3,2,1,0:T(8,128)(2,1)}, f32[2,256,768]{2,1,...) custom-call(s32[2]{0:T(128)} %pad_add_fusion.refs_0_, ...), custom_call_target="tpu_custom_call", output_to_operand_aliasing={{0}: (5, {}), {1}: (6, {}), {2}: (7, {}), {3}: (8, {}), {4}... | custom-call | flops 5000000000 | bytes 25000000 | tf_op jit(solution)/shard_map/layer_forward/pallas_call | solution.py:649
  145.1 2.1 collective-permute-start
  147.2 10.0 %layer_both_ways.2 = (bf16[2,2304,256]{2,1,0:T(8,128)(2,1)}, bf16[2,256,768]{2,1,0:T(8,128)(2,1)}, bf16[3888,256]{1,0:T(8,128)(2,1)}, bf16[256,3072]{1,0:T(8,128...) custom-call(s32[2]{0:T(128)} %pad_add_fusion.refs_0_, ...), custom_call_target="tpu_custom_call", output_to_operand_aliasing={{0}: (6, {}), {1}: (7, {})} | custom-call | flops 130000003072 | bytes 650000000 | tf_op jit(solution)/shard_map/layer_both_ways/pallas_call | solution.py:649
  157.2 1.3 collective-permute-start.4
  158.5 13.0 %layer_both_ways.3 = (bf16[2,2304,256]{2,1,0:T(8,128)(2,1)}, bf16[2,256,768]{2,1,0:T(8,128)(2,1)}, bf16[3888,256]{1,0:T(8,128)(2,1)}, bf16[256,3072]{1,0:T(8,128...) custom-call(s32[2]{0:T(128)} %pad_add_fusion.refs_0_, ...), custom_call_target="tpu_custom_call", output_to_operand_aliasing={{0}: (6, {}), {1}: (7, {}), {2}: (8, {}), {7}: (9, {})} | custom-call | flops 130000003072 | bytes 650000000 | tf_op jit(solution)/shard_map/layer_both_ways/pallas_call | solution.py:649
  171.5 1.3 collective-permute-start.2
  173.2 6.9 %collective-permute-done.4.refs_1_ = bf16[256,768]{1,0:T(8,128)(2,1)} collective-permute-done((bf16[256,768]{1,0:T(8,128)(2,1)}, bf16[256,768]{1,0:T(8,128)(2,1)}, u32[]{:S(2)}, u32[]{:S(2)}) %collective-permute-start.4) | collective-permute-done | bytes 393248 | tf_op jit(solution)/shard_map/ppermute | solution.py:1279
  180.1 20.7 %layer_backward.1 = (bf16[3888,256]{1,0:T(8,128)(2,1)}, bf16[256,3072]{1,0:T(8,128)(2,1)}, bf16[256,3072]{1,0:T(8,128)(2,1)}, bf16[256,1536]{1,0:T(8,128)(2,1)},...) custom-call(s32[2]{0:T(128)} %pad_add_fusion.refs_0_, ...), custom_call_target="tpu_custom_call", output_to_operand_aliasing={{0}: (10, {}), {1}: (11, {}), {2}: (12, {}), {3}: (13, {}),... | custom-call | flops 80000000000 | bytes 400000000 | tf_op jit(solution)/shard_map/layer_backward/pallas_call | solution.py:649
  200.8 10.3 %collective-permute-done.2.refs_1_ = bf16[256,768]{1,0:T(8,128)(2,1)} collective-permute-done((bf16[256,768]{1,0:T(8,128)(2,1)}, bf16[256,768]{1,0:T(8,128)(2,1)}, u32[]{:S(2)}, u32[]{:S(2)}) %collective-permute-start.2) | collective-permute-done | bytes 393248 | tf_op jit(solution)/shard_map/ppermute | solution.py:1279
  211.2 12.0 %backward_hidden.1 = (bf16[3888,256]{1,0:T(8,128)(2,1)}, bf16[256,3072]{1,0:T(8,128)(2,1)}, bf16[256,3072]{1,0:T(8,128)(2,1)}, f32[256,768]{1,0:T(8,128)}) custom-call(s32[2]{0:T(128)} %pad_add_fusion.refs_0_, bf16[256,768]{1,0:T(8,128)(2,1)} %collective-permute-done.2.refs_1_, ...), custom_call_target="tpu_custom_call", output_to_operand_aliasing={{0}: (9, {}), {1}: (10, {}), {2}: (11, {})} | custom-call | flops 60000002048 | bytes 300000000 | tf_op jit(solution)/shard_map/backward_hidden/pallas_call | solution.py:649
  224.3 3.2 collective-permute-done.10.refs_4_.refs_14_
  227.7 7.0 %weight_grad.4 = (bf16[4,192,768]{2,1,0:T(8,128)(2,1)}, bf16[4,192,768]{2,1,0:T(8,128)(2,1)}) custom-call(s32[2]{0:T(128)} %pad_add_fusion.refs_0_, bf16[3888,256]{1,0:T(8,128)(2,1)} %get-tuple-element.117.refs_1_.refs_11_, bf16[3888,256]{1,0:T(8,128)(2,1)} %get-tuple-element.118.refs_2_.refs_12_, bf16[3888,256]{1,0:T(8,128)(2,1)} %collective-permute-done.9.refs_3_.refs_13_, ...), custom_call_target="tpu_custom_call" | custom-call | flops 73600000000 | bytes 368000000 | tf_op jit(solution)/shard_map/weight_grad/pallas_call | solution.py:1003
  235.1 1.4 collective-permute-done.8.refs_6_
  236.6 1.3 collective-permute-start.15
  237.8 7.9 %weight_grad.5 = (bf16[4,48,3072]{2,1,0:T(8,128)(2,1)}, bf16[4,48,3072]{2,1,0:T(8,128)(2,1)}) custom-call(s32[2]{0:T(128)} %pad_add_fusion.refs_0_, bf16[2,2304,256]{2,1,0:T(8,128)(2,1)} %get-tuple-element.98.refs_1_, bf16[2,2304,256]{2,1,0:T(8,128)(2,1)} %collective-permute-done.3.refs_12_.refs_2_, bf16[256,3072]{1,0:T(8,128)(2,1)} %get-tuple-element.115.refs_3_, ...), custom_call_target="tpu_custom_call" | custom-call | flops 73600000000 | bytes 368000000 | tf_op jit(solution)/shard_map/weight_grad/pallas_call | solution.py:1003
  245.7 1.6 collective-permute-start.18
  247.3 7.9 %weight_grad.6 = (bf16[4,48,3072]{2,1,0:T(8,128)(2,1)}, bf16[4,48,3072]{2,1,0:T(8,128)(2,1)}) custom-call(s32[2]{0:T(128)} %pad_add_fusion.refs_0_, bf16[2,2304,256]{2,1,0:T(8,128)(2,1)} %get-tuple-element.98.refs_1_, bf16[2,2304,256]{2,1,0:T(8,128)(2,1)} %collective-permute-done.3.refs_12_.refs_2_, bf16[256,3072]{1,0:T(8,128)(2,1)} %get-tuple-element.113.refs_3_, ...), custom_call_target="tpu_custom_call" | custom-call | flops 73600000000 | bytes 368000000 | tf_op jit(solution)/shard_map/weight_grad/pallas_call | solution.py:1003
  256.0 9.8 %backward_attention.1 = (bf16[256,1536]{1,0:T(8,128)(2,1)}, bf16[256,1536]{1,0:T(8,128)(2,1)}, f32[2,256,768]{2,1,0:T(8,128)}, bf16[256,768]{1,0:T(8,128)(2,1)}) custom-call(s32[2]{0:T(128)} %pad_add_fusion.refs_0_, f32[256,768]{1,0:T(8,128)} %get-tuple-element.99.refs_1_, ...), custom_call_target="tpu_custom_call", output_to_operand_aliasing={{0}: (5, {}), {1}: (6, {}), {2}: (7, {})} | custom-call | flops 92000002048 | bytes 460000000 | tf_op jit(solution)/shard_map/backward_attention/pallas_call | solution.py:649
  266.4 2.0 halve.8.refs_15_
  268.4 0.9 collective-permute-start.20
  269.6 8.7 %weight_grad.7 = (bf16[4,48,3200]{2,1,0:T(8,128)(2,1)}, bf16[4,48,3200]{2,1,0:T(8,128)(2,1)}) custom-call(s32[2]{0:T(128)} %pad_add_fusion.refs_0_, bf16[2,2304,256]{2,1,0:T(8,128)(2,1)} %get-tuple-element.98.refs_1_, bf16[2,2304,256]{2,1,0:T(8,128)(2,1)} %collective-permute-done.3.refs_12_.refs_2_, bf16[256,1536]{1,0:T(8,128)(2,1)} %get-tuple-element.122.refs_3_, ...), custom_call_target="tpu_custom_call" | custom-call | flops 73600000000 | bytes 368000000 | tf_op jit(solution)/shard_map/weight_grad/pallas_call | solution.py:1003
  278.3 1.3 collective-permute-start.16
  279.6 2.0 halve.9.refs_2_
  282.5 8.5 %collective-permute-done.17.refs_1_ = bf16[4,48,3072]{2,1,0:T(8,128)(2,1)} collective-permute-done((bf16[4,48,3072]{2,1,0:T(8,128)(2,1)}, bf16[4,48,3072]{2,1,0:T(8,128)(2,1)}, u32[]{:S(2)}, u32[]{:S(2)}) %collective-permute-start.17) | collective-permute-done | bytes 1179680 | tf_op jit(solution)/shard_map/ppermute | solution.py:1017
  291.0 2.1 halve.10.refs_3_
  293.0 1.6 collective-permute-start.19
  294.6 1.9 halve.11.refs_3_
  296.5 2.5 collective-permute-start.24
  299.0 14.5 %collective-permute-done.19.refs_2_ = bf16[2,48,3072]{2,1,0:T(8,128)(2,1)} collective-permute-done((bf16[2,48,3072]{2,1,0:T(8,128)(2,1)}, bf16[2,48,3072]{2,1,0:T(8,128)(2,1)}, u32[]{:S(2)}, u32[]{:S(2)}) %collective-permute-start.19) | collective-permute-done | bytes 589856 | tf_op jit(solution)/shard_map/ppermute | solution.py:1017
  313.5 1.9 halve.12.refs_2_
  315.4 1.5 collective-permute-start.26
  317.3 2.1 halve.13.refs_4_
  319.4 2.1 collective-permute-start.21
  321.5 2.1 finish.5.refs_3_
  323.7 5.5 %collective-permute-done.23.refs_2_ = bf16[2,48,3072]{2,1,0:T(8,128)(2,1)} collective-permute-done((bf16[2,48,3072]{2,1,0:T(8,128)(2,1)}, bf16[2,48,3072]{2,1,0:T(8,128)(2,1)}, u32[]{:S(2)}, u32[]{:S(2)}) %collective-permute-start.23) | collective-permute-done | bytes 589856 | tf_op jit(solution)/shard_map/ppermute | solution.py:1017
  329.1 1.9 halve.15.refs_4_
  331.1 2.5 collective-permute-start.25
  333.6 2.1 finish.6.refs_5_
  335.7 6.8 %collective-permute-done.21.refs_2_ = bf16[2,48,3200]{2,1,0:T(8,128)(2,1)} collective-permute-done((bf16[2,48,3200]{2,1,0:T(8,128)(2,1)}, bf16[2,48,3200]{2,1,0:T(8,128)(2,1)}, u32[]{:S(2)}, u32[]{:S(2)}) %collective-permute-start.21) | collective-permute-done | bytes 614432 | tf_op jit(solution)/shard_map/ppermute | solution.py:1017
  342.5 2.0 halve.14.refs_4_
  345.0 9.4 %collective-permute-done.25.refs_3_ = bf16[1,48,3072]{2,1,0:T(8,128)(2,1)} collective-permute-done((bf16[1,48,3072]{2,1,0:T(8,128)(2,1)}, bf16[1,48,3072]{2,1,0:T(8,128)(2,1)}, u32[]{:S(2)}, u32[]{:S(2)}) %collective-permute-start.25) | collective-permute-done | bytes 294944 | tf_op jit(solution)/shard_map/ppermute | solution.py:1017
  354.4 2.1 finish.7
  356.5 3.6 collective-permute-done.22.refs_3_
  360.1 2.8 finish.4
  (34 shorter events, 6.3 us)
Async XLA Ops:
  7.2 105.9 %all-gather.2.cloned.1.call-start = ((), (), s32[]{:S(2)}) async-start(), calls=%async_computation | async-start | bytes 20262912 | tf_op jit(solution)/shard_map/all_gather | solution.py:1271
  127.6 19.6 %collective-permute-start.1 = (bf16[256,768]{1,0:T(8,128)(2,1)}, bf16[256,768]{1,0:T(8,128)(2,1)}, u32[]{:S(2)}, u32[]{:S(2)}) collective-permute-start(bf16[256,768]{1,0:T(8,128)(2,1)} %get-tuple-element.81), channel_id=1, source_target_pairs={{0,16},{1,17},{2,18},{3,19},{4,20},{5,21},{6,22},{7,23},{8,24},{9,... | collective-permute-start | bytes 1179656 | tf_op jit(solution)/shard_map/ppermute | solution.py:1279
  145.1 13.4 %collective-permute-start = (bf16[256,768]{1,0:T(8,128)(2,1)}, bf16[256,768]{1,0:T(8,128)(2,1)}, u32[]{:S(2)}, u32[]{:S(2)}) collective-permute-start(bf16[256,768]{1,0:T(8,128)(2,1)} %get-tuple-element.80), channel_id=1, source_target_pairs={{0,16},{1,17},{2,18},{3,19},{4,20},{5,21},{6,22},{7,23},{8,24},{9,... | collective-permute-start | bytes 1179656 | tf_op jit(solution)/shard_map/ppermute | solution.py:1279
  157.2 22.9 %collective-permute-start.4 = (bf16[256,768]{1,0:T(8,128)(2,1)}, bf16[256,768]{1,0:T(8,128)(2,1)}, u32[]{:S(2)}, u32[]{:S(2)}) collective-permute-start(bf16[256,768]{1,0:T(8,128)(2,1)} %get-tuple-element.104), channel_id=1, source_target_pairs={{16,0},{17,1},{18,2},{19,3},{20,4},{21,5},{22,6},{23,7},{24,8},{25... | collective-permute-start | bytes 1179656 | tf_op jit(solution)/shard_map/ppermute | solution.py:1279
  171.5 39.6 %collective-permute-start.2 = (bf16[256,768]{1,0:T(8,128)(2,1)}, bf16[256,768]{1,0:T(8,128)(2,1)}, u32[]{:S(2)}, u32[]{:S(2)}) collective-permute-start(bf16[256,768]{1,0:T(8,128)(2,1)} %get-tuple-element.89), channel_id=1, source_target_pairs={{16,0},{17,1},{18,2},{19,3},{20,4},{21,5},{22,6},{23,7},{24,8},{25... | collective-permute-start | bytes 1179656 | tf_op jit(solution)/shard_map/ppermute | solution.py:1279
  172.8 38.3 %collective-permute-start.3 = (bf16[2,2304,256]{2,1,0:T(8,128)(2,1)}, bf16[2,2304,256]{2,1,0:T(8,128)(2,1)}, u32[]{:S(2)}, u32[]{:S(2)}) collective-permute-start(bf16[2,2304,256]{2,1,0:T(8,128)(2,1)} %get-tuple-element.98.refs_1_), channel_id=1, source_target_pairs={{0,1},{1,0},{2,3},{3,2},{4,5},{5,4},{6,7},{7,6},{8,9},{9,8},{10,11... | collective-permute-start | bytes 7077896 | tf_op jit(solution)/shard_map/ppermute | solution.py:1017
  200.8 23.5 %collective-permute-start.9 = (bf16[3888,256]{1,0:T(8,128)(2,1)}, bf16[3888,256]{1,0:T(8,128)(2,1)}, u32[]{:S(2)}, u32[]{:S(2)}) collective-permute-start(bf16[3888,256]{1,0:T(8,128)(2,1)} %get-tuple-element.117.refs_1_.refs_11_), channel_id=1, source_target_pairs={{0,1},{1,0},{2,3},{3,2},{4,5},{5,4},{6,7},{7,6},{8,9},{9,8},{10,11... | collective-permute-start | bytes 5971976 | tf_op jit(solution)/shard_map/ppermute | solution.py:1017
  223.1 4.4 %collective-permute-start.10 = (bf16[3888,256]{1,0:T(8,128)(2,1)}, bf16[3888,256]{1,0:T(8,128)(2,1)}, u32[]{:S(2)}, u32[]{:S(2)}) collective-permute-start(bf16[3888,256]{1,0:T(8,128)(2,1)} %get-tuple-element.118.refs_2_.refs_12_), channel_id=1, source_target_pairs={{0,1},{1,0},{2,3},{3,2},{4,5},{5,4},{6,7},{7,6},{8,9},{9,8},{10,11... | collective-permute-start | bytes 5971976 | tf_op jit(solution)/shard_map/ppermute | solution.py:1017
  223.2 22.5 %collective-permute-start.5 = (bf16[256,3072]{1,0:T(8,128)(2,1)}, bf16[256,3072]{1,0:T(8,128)(2,1)}, u32[]{:S(2)}, u32[]{:S(2)}) collective-permute-start(bf16[256,3072]{1,0:T(8,128)(2,1)} %get-tuple-element.113.refs_3_), channel_id=1, source_target_pairs={{0,1},{1,0},{2,3},{3,2},{4,5},{5,4},{6,7},{7,6},{8,9},{9,8},{10,11... | collective-permute-start | bytes 4718600 | tf_op jit(solution)/shard_map/ppermute | solution.py:1017
  223.7 11.0 %collective-permute-start.7 = (bf16[256,3072]{1,0:T(8,128)(2,1)}, bf16[256,3072]{1,0:T(8,128)(2,1)}, u32[]{:S(2)}, u32[]{:S(2)}) collective-permute-start(bf16[256,3072]{1,0:T(8,128)(2,1)} %get-tuple-element.115.refs_3_), channel_id=1, source_target_pairs={{0,1},{1,0},{2,3},{3,2},{4,5},{5,4},{6,7},{7,6},{8,9},{9,8},{10,11... | collective-permute-start | bytes 4718600 | tf_op jit(solution)/shard_map/ppermute | solution.py:1017
  223.8 32.2 %collective-permute-start.11 = (bf16[256,1536]{1,0:T(8,128)(2,1)}, bf16[256,1536]{1,0:T(8,128)(2,1)}, u32[]{:S(2)}, u32[]{:S(2)}) collective-permute-start(bf16[256,1536]{1,0:T(8,128)(2,1)} %get-tuple-element.122.refs_3_), channel_id=1, source_target_pairs={{0,1},{1,0},{2,3},{3,2},{4,5},{5,4},{6,7},{7,6},{8,9},{9,8},{10,11... | collective-permute-start | bytes 2359304 | tf_op jit(solution)/shard_map/ppermute | solution.py:1017
  224.2 31.8 %collective-permute-start.12 = (bf16[256,1536]{1,0:T(8,128)(2,1)}, bf16[256,1536]{1,0:T(8,128)(2,1)}, u32[]{:S(2)}, u32[]{:S(2)}) collective-permute-start(bf16[256,1536]{1,0:T(8,128)(2,1)} %get-tuple-element.123.refs_7_), channel_id=1, source_target_pairs={{0,1},{1,0},{2,3},{3,2},{4,5},{5,4},{6,7},{7,6},{8,9},{9,8},{10,11... | collective-permute-start | bytes 2359304 | tf_op jit(solution)/shard_map/ppermute | solution.py:1017
  227.6 9.0 %collective-permute-start.8 = (bf16[256,3072]{1,0:T(8,128)(2,1)}, bf16[256,3072]{1,0:T(8,128)(2,1)}, u32[]{:S(2)}, u32[]{:S(2)}) collective-permute-start(bf16[256,3072]{1,0:T(8,128)(2,1)} %get-tuple-element.116.refs_4_), channel_id=1, source_target_pairs={{0,1},{1,0},{2,3},{3,2},{4,5},{5,4},{6,7},{7,6},{8,9},{9,8},{10,11... | collective-permute-start | bytes 4718600 | tf_op jit(solution)/shard_map/ppermute | solution.py:1017
  234.7 12.6 %collective-permute-start.6 = (bf16[256,3072]{1,0:T(8,128)(2,1)}, bf16[256,3072]{1,0:T(8,128)(2,1)}, u32[]{:S(2)}, u32[]{:S(2)}) collective-permute-start(bf16[256,3072]{1,0:T(8,128)(2,1)} %get-tuple-element.114.refs_4_), channel_id=1, source_target_pairs={{0,1},{1,0},{2,3},{3,2},{4,5},{5,4},{6,7},{7,6},{8,9},{9,8},{10,11... | collective-permute-start | bytes 4718600 | tf_op jit(solution)/shard_map/ppermute | solution.py:1017
  236.6 29.8 %collective-permute-start.15 = (bf16[4,192,768]{2,1,0:T(8,128)(2,1)}, bf16[4,192,768]{2,1,0:T(8,128)(2,1)}, u32[]{:S(2)}, u32[]{:S(2)}) collective-permute-start(bf16[4,192,768]{2,1,0:T(8,128)(2,1)} %get-tuple-element.119.refs_7_), channel_id=1, source_target_pairs={{0,2},{1,3},{2,0},{3,1},{4,6},{5,7},{6,4},{7,5},{8,10},{9,11},{10,... | collective-permute-start | bytes 3538952 | tf_op jit(solution)/shard_map/ppermute | solution.py:1017
  245.7 33.9 %collective-permute-start.18 = (bf16[4,48,3072]{2,1,0:T(8,128)(2,1)}, bf16[4,48,3072]{2,1,0:T(8,128)(2,1)}, u32[]{:S(2)}, u32[]{:S(2)}) collective-permute-start(bf16[4,48,3072]{2,1,0:T(8,128)(2,1)} %get-tuple-element.120.refs_7_), channel_id=1, source_target_pairs={{0,4},{1,5},{2,6},{3,7},{4,0},{5,1},{6,2},{7,3},{8,12},{9,13},{10,... | collective-permute-start | bytes 3538952 | tf_op jit(solution)/shard_map/ppermute | solution.py:1017
  255.2 35.8 %collective-permute-start.17 = (bf16[4,48,3072]{2,1,0:T(8,128)(2,1)}, bf16[4,48,3072]{2,1,0:T(8,128)(2,1)}, u32[]{:S(2)}, u32[]{:S(2)}) collective-permute-start(bf16[4,48,3072]{2,1,0:T(8,128)(2,1)} %get-tuple-element.121.refs_8_), channel_id=1, source_target_pairs={{0,2},{1,3},{2,0},{3,1},{4,6},{5,7},{6,4},{7,5},{8,10},{9,11},{10,... | collective-permute-start | bytes 3538952 | tf_op jit(solution)/shard_map/ppermute | solution.py:1017
  265.8 3.5 collective-permute-start.13
  265.9 3.7 %collective-permute-start.14 = (bf16[256,1536]{1,0:T(8,128)(2,1)}, bf16[256,1536]{1,0:T(8,128)(2,1)}, u32[]{:S(2)}, u32[]{:S(2)}) collective-permute-start(bf16[256,1536]{1,0:T(8,128)(2,1)} %get-tuple-element.126.refs_8_), channel_id=1, source_target_pairs={{0,1},{1,0},{2,3},{3,2},{4,5},{5,4},{6,7},{7,6},{8,9},{9,8},{10,11... | collective-permute-start | bytes 2359304 | tf_op jit(solution)/shard_map/ppermute | solution.py:1017
  268.4 26.2 %collective-permute-start.20 = (bf16[2,192,768]{2,1,0:T(8,128)(2,1)}, bf16[2,192,768]{2,1,0:T(8,128)(2,1)}, u32[]{:S(2)}, u32[]{:S(2)}) collective-permute-start(bf16[2,192,768]{2,1,0:T(8,128)(2,1)} %halve.8.refs_15_), channel_id=1, source_target_pairs={{0,4},{1,5},{2,6},{3,7},{4,0},{5,1},{6,2},{7,3},{8,12},{9,13},{10,... | collective-permute-start | bytes 1769480 | tf_op jit(solution)/shard_map/ppermute | solution.py:1017
  278.3 39.0 %collective-permute-start.16 = (bf16[4,48,3200]{2,1,0:T(8,128)(2,1)}, bf16[4,48,3200]{2,1,0:T(8,128)(2,1)}, u32[]{:S(2)}, u32[]{:S(2)}) collective-permute-start(bf16[4,48,3200]{2,1,0:T(8,128)(2,1)} %get-tuple-element.129.refs_2_), channel_id=1, source_target_pairs={{0,2},{1,3},{2,0},{3,1},{4,6},{5,7},{6,4},{7,5},{8,10},{9,11},{10,... | collective-permute-start | bytes 3686408 | tf_op jit(solution)/shard_map/ppermute | solution.py:1017
  281.6 47.5 %collective-permute-start.23 = (bf16[2,48,3072]{2,1,0:T(8,128)(2,1)}, bf16[2,48,3072]{2,1,0:T(8,128)(2,1)}, u32[]{:S(2)}, u32[]{:S(2)}) collective-permute-start(bf16[2,48,3072]{2,1,0:T(8,128)(2,1)} %halve.9.refs_2_), channel_id=1, source_target_pairs={{0,2},{1,3},{2,0},{3,1},{4,6},{5,7},{6,4},{7,5},{8,10},{9,11},{10,... | collective-permute-start | bytes 1769480 | tf_op jit(solution)/shard_map/ppermute | solution.py:1017
  293.0 20.4 %collective-permute-start.19 = (bf16[2,48,3072]{2,1,0:T(8,128)(2,1)}, bf16[2,48,3072]{2,1,0:T(8,128)(2,1)}, u32[]{:S(2)}, u32[]{:S(2)}) collective-permute-start(bf16[2,48,3072]{2,1,0:T(8,128)(2,1)} %halve.10.refs_3_), channel_id=1, source_target_pairs={{0,4},{1,5},{2,6},{3,7},{4,0},{5,1},{6,2},{7,3},{8,12},{9,13},{10,... | collective-permute-start | bytes 1769480 | tf_op jit(solution)/shard_map/ppermute | solution.py:1017
  296.5 25.0 %collective-permute-start.24 = (bf16[1,192,768]{2,1,0:T(8,128)(2,1)}, bf16[1,192,768]{2,1,0:T(8,128)(2,1)}, u32[]{:S(2)}, u32[]{:S(2)}) collective-permute-start(bf16[1,192,768]{2,1,0:T(8,128)(2,1)} %halve.11.refs_3_), channel_id=1, source_target_pairs={{0,8},{1,9},{2,10},{3,11},{4,12},{5,13},{6,14},{7,15},{8,0},{9,1},... | collective-permute-start | bytes 884744 | tf_op jit(solution)/shard_map/ppermute | solution.py:1017
  315.4 18.1 %collective-permute-start.26 = (bf16[1,48,3072]{2,1,0:T(8,128)(2,1)}, bf16[1,48,3072]{2,1,0:T(8,128)(2,1)}, u32[]{:S(2)}, u32[]{:S(2)}) collective-permute-start(bf16[1,48,3072]{2,1,0:T(8,128)(2,1)} %halve.12.refs_2_), channel_id=1, source_target_pairs={{0,8},{1,9},{2,10},{3,11},{4,12},{5,13},{6,14},{7,15},{8,0},{9,1},... | collective-permute-start | bytes 884744 | tf_op jit(solution)/shard_map/ppermute | solution.py:1017
  319.4 23.1 %collective-permute-start.21 = (bf16[2,48,3200]{2,1,0:T(8,128)(2,1)}, bf16[2,48,3200]{2,1,0:T(8,128)(2,1)}, u32[]{:S(2)}, u32[]{:S(2)}) collective-permute-start(bf16[2,48,3200]{2,1,0:T(8,128)(2,1)} %halve.13.refs_4_), channel_id=1, source_target_pairs={{0,4},{1,5},{2,6},{3,7},{4,0},{5,1},{6,2},{7,3},{8,12},{9,13},{10,... | collective-permute-start | bytes 1843208 | tf_op jit(solution)/shard_map/ppermute | solution.py:1017
  331.1 23.3 %collective-permute-start.25 = (bf16[1,48,3072]{2,1,0:T(8,128)(2,1)}, bf16[1,48,3072]{2,1,0:T(8,128)(2,1)}, u32[]{:S(2)}, u32[]{:S(2)}) collective-permute-start(bf16[1,48,3072]{2,1,0:T(8,128)(2,1)} %halve.15.refs_4_), channel_id=1, source_target_pairs={{0,8},{1,9},{2,10},{3,11},{4,12},{5,13},{6,14},{7,15},{8,0},{9,1},... | collective-permute-start | bytes 884744 | tf_op jit(solution)/shard_map/ppermute | solution.py:1017
  344.4 15.7 %collective-permute-start.22 = (bf16[1,48,3200]{2,1,0:T(8,128)(2,1)}, bf16[1,48,3200]{2,1,0:T(8,128)(2,1)}, u32[]{:S(2)}, u32[]{:S(2)}) collective-permute-start(bf16[1,48,3200]{2,1,0:T(8,128)(2,1)} %halve.14.refs_4_), channel_id=1, source_target_pairs={{0,8},{1,9},{2,10},{3,11},{4,12},{5,13},{6,14},{7,15},{8,0},{9,1},... | collective-permute-start | bytes 921608 | tf_op jit(solution)/shard_map/ppermute | solution.py:1017
Sparse Core Ops, SparseCore 0:
  10.5 102.5 all-gather.1
